TPU v7x, 32 devices: a whole 2x2x4 slice. The times are simulated.
32 devices in a mesh: dp: 8 (over z, y), tp: 4 (over x, core).
Axes of the slice: x: 2, y: 2, z: 4, core: 2. Of those that a mesh axis runs over, the one named last changes fastest.
Arguments:
- attn_partial: bfloat16 [4, 512, 7168], P('tp', 'dp'), may hold values from -3 to 3
- hidden_in: bfloat16 [512, 7168], P('dp', 'tp'), may hold values from -6 to 6
- norm_gain: float32 [7168], replicated, may hold values from 0.5 to 1.5
- expert_ids: int32 [512, 8], P('dp'), may hold values from 0 to 255, all different within a row; in each aligned block of 64 rows (0 to 63, 64 to 127, ...) at most 4 rows name the same one
- route_prob: bfloat16 [512, 8], P('dp'), may hold values from 0.049804688 to 0.3984375
- w_gate: bfloat16 [8, 7168, 1024], P('dp', None, 'tp'), may hold values from -0.0625 to 0.0625
- w_up: bfloat16 [8, 7168, 1024], P('dp', None, 'tp'), may hold values from -0.0625 to 0.0625
- w_down: bfloat16 [8, 1024, 7168], P('dp', 'tp'), may hold values from -0.1875 to 0.1875
Outputs:
- layer_out: bfloat16 [512, 7168], P('dp', 'tp')
- amax_input: float32 [8], P('dp')
- amax_hidden: float32 [8], P('dp')
Inputs may be any that keep to these rules, and one draw needn't show every extreme that they name: `expert_ids`: each token names 8 different experts; within each aligned block of 64 tokens no expert is named by more than 4 tokens.
All inputs are finite; a program needn't handle non-finite values.
Results may differ from a plain program's by a relative error of at most 0.0075.
Values may be sent and summed in bfloat16 or wider, within the bound.
No kernel may reach another device: no remote copies, remote signals or barrier semaphores. Data moves between devices by JAX's collectives and lax.ppermute only.
A program may use at most 64 MiB of HBM per device.

v0:
```python
import jax
import jax.numpy as jnp
from jax import lax
from jax.sharding import PartitionSpec as P

EXPERT_SLOTS = 4


eps = 1e-06


def route_tables(expert_ids, route_prob, experts, capacity):
    matches = expert_ids[:, :, None] == jnp.arange(experts, dtype=jnp.int32)[None, None, :]
    onehot = jnp.sum(matches.astype(jnp.int32), axis=1)
    weight = jnp.sum(
        jnp.where(matches, route_prob[:, :, None].astype(jnp.float32), jnp.float32(0.0)), axis=1
    )
    before = jnp.cumsum(onehot, axis=0) - onehot
    placing = (onehot.T[:, None, :] == 1) & (
        before.T[:, None, :] == jnp.arange(capacity, dtype=jnp.int32)[None, :, None]
    )
    return (onehot, weight, placing)


def on_device(attn_partial, hidden_in, norm_gain, expert_ids, route_prob, w_gate, w_up, w_down):
    experts = lax.axis_size("dp")
    tp_index = lax.axis_index("tp")
    partial_value = attn_partial[0].astype(jnp.float32)
    token_count = partial_value.shape[0]
    columns = hidden_in.shape[1]
    start_col = tp_index * columns
    own_cols = lax.dynamic_slice_in_dim(partial_value, start_col, columns, 1) + hidden_in.astype(
        jnp.float32
    )
    summand = lax.dynamic_update_slice_in_dim(partial_value, own_cols, start_col, 1)
    residual = lax.psum(summand, "tp")
    mean_sq = jnp.mean(residual * residual, axis=1, keepdims=True)
    normed = (residual * lax.rsqrt(mean_sq + eps) * norm_gain).astype(jnp.bfloat16)
    residual_cols = lax.dynamic_slice_in_dim(residual, start_col, columns, 1)
    onehot, weight, placing = route_tables(expert_ids, route_prob, experts, EXPERT_SLOTS)
    selection_mask = placing.reshape(experts * EXPERT_SLOTS, token_count).astype(jnp.bfloat16)
    outgoing = jnp.dot(selection_mask, normed, preferred_element_type=jnp.float32).astype(
        jnp.bfloat16
    )
    piece_width = outgoing.shape[1]
    incoming = lax.all_to_all(
        outgoing.reshape(experts, EXPERT_SLOTS, piece_width),
        "dp",
        split_axis=0,
        concat_axis=0,
        tiled=True,
    )
    expert_slot_rows = incoming.reshape(experts * EXPERT_SLOTS, piece_width)
    gate_val = jnp.dot(expert_slot_rows, w_gate[0], preferred_element_type=jnp.float32)
    up_val = jnp.dot(expert_slot_rows, w_up[0], preferred_element_type=jnp.float32)
    hidden_act = (jax.nn.silu(gate_val) * up_val).astype(jnp.bfloat16)
    partial_out = jnp.dot(hidden_act, w_down[0], preferred_element_type=jnp.float32)
    combine_matrix = (placing.astype(jnp.float32) * weight.T[:, None, :]).reshape(
        experts * EXPERT_SLOTS, token_count
    )
    expert_cols = lax.psum_scatter(
        partial_out.astype(jnp.bfloat16), "tp", scatter_dimension=1, tiled=True
    ).astype(jnp.float32)
    returned = lax.all_to_all(
        expert_cols.reshape(experts, EXPERT_SLOTS, columns).astype(jnp.bfloat16),
        "dp",
        split_axis=0,
        concat_axis=0,
        tiled=True,
    ).astype(jnp.float32)
    moe_out = jnp.dot(
        combine_matrix.T,
        returned.reshape(experts * EXPERT_SLOTS, columns),
        precision=lax.Precision.HIGHEST,
        preferred_element_type=jnp.float32,
    )
    layer_out = (residual_cols + moe_out).astype(jnp.bfloat16)
    hidden_peak = jnp.max(jnp.abs(hidden_act.astype(jnp.float32)))
    input_peak = jnp.max(jnp.abs(expert_slot_rows.astype(jnp.float32)))
    input_peak, hidden_peak = lax.pmax((input_peak, hidden_peak), "tp")
    amax_input = input_peak.reshape(1)
    amax_hidden = hidden_peak.reshape(1)
    return (layer_out, amax_input, amax_hidden)


def solution(mesh):
    placed = (
        P("tp", "dp", None),
        P("dp", "tp"),
        P(),
        P("dp", None),
        P("dp", None),
        P("dp", None, "tp"),
        P("dp", None, "tp"),
        P("dp", "tp", None),
    )
    return jax.shard_map(
        on_device,
        mesh=mesh,
        in_specs=placed,
        out_specs=(P("dp", "tp"), P("dp"), P("dp")),
        check_vma=False,
    )
```

profile of v0, /device:TPU:0, one launch (start us, length us, event | category | flops | bytes accessed | tf_op | source)
XLA Modules:
  0.0 132.3 jit_solution(10730123870915161944)
XLA Ops:
  7.2 0.0 all-reduce.3.cloned.1.call-start
  7.2 0.0 copy-start.4
  7.2 2.8 %fusion.27 = (f32[1,64,7168]{2,1,0:T(8,128)}, f32[64,7168]{1,0:T(8,128)S(1)}) fusion(bf16[1,64,7168]{2,1,0:T(8,128)(2,1)} %param.8), kind=kLoop, calls=%fused_computation.38 | loop fusion | flops 458752 | bytes 4587520 | tf_op jit(solution)/shard_map/convert_element_type | solution.py:28
  10.1 0.0 copy-start.6
  10.1 0.0 copy-done.4
  10.1 1.1 fusion.15
  11.1 0.0 copy-start
  11.1 0.0 copy-start.5
  11.2 1.2 copy-done
  12.4 0.0 all-reduce.3.cloned.1.call-update
  12.4 0.0 reduce-scatter.2.cloned.1.call-start
  12.4 0.0 copy-done.6
  12.5 0.1 copy.26
  12.5 0.1 reduce_window_sum.11
  12.6 0.1 copy.28
  12.7 0.1 eq.58
  12.8 49.6 %all-reduce.3.cloned.1.call-done = f32[64,7168]{1,0:T(8,128)} async-done(((f32[64,7168]{1,0:T(8,128)}), f32[64,7168]{1,0:T(8,128)}) %all-reduce.3.cloned.1.call-update) | async-done | bytes 1835024 | tf_op jit(solution)/shard_map/psum | solution.py:36
  62.4 0.0 copy-start.1
  62.4 1.9 %multiply_reduce_fusion = f32[64]{0:T(128)S(1)} fusion(f32[64,7168]{1,0:T(8,128)} %all-reduce.3.cloned.1.call-done), kind=kLoop, calls=%fused_computation.11 | loop fusion | flops 917440 | bytes 1835264 | tf_op jit(solution)/shard_map/reduce_sum | solution.py:37
  64.3 0.0 copy-done.5
  64.3 0.1 copy-done.1
  64.4 0.4 convolution_convert_fusion.1
  64.8 0.2 reshape.44
  65.0 18.3 %all_to_all.10 = bf16[8,4,7168]{2,1,0:T(4,128)(2,1)S(1)} all-to-all(bf16[8,4,7168]{2,1,0:T(4,128)(2,1)S(1)} %reshape.44), channel_id=1, replica_groups=mesh['dp'=8,'tp'=4] {'dp'}, dimensions={0} | all-to-all | bytes 917504 | tf_op jit(solution)/shard_map/all_to_all | solution.py:46
  83.3 0.1 reshape.45
  83.4 0.0 copy-start.2
  83.4 2.9 %fusion.3 = f32[32,256]{1,0:T(8,128)S(1)} fusion(bf16[32,7168]{1,0:T(8,128)(2,1)S(1)} %reshape.45, bf16[1,7168,256]{2,1,0:T(8,128)(2,1)} %param.13), kind=kOutput, calls=%fused_computation.5 | convolution fusion | flops 117440512 | bytes 4161536 | tf_op jit(solution)/shard_map/dot_general | solution.py:54
  86.3 0.2 copy-done.2
  86.5 0.0 copy-start.3
  86.5 1.3 %abs_reduce_fusion.1 = (f32[]{:T(128)}, bf16[32,256]{1,0:T(8,128)(2,1)S(1)}) fusion(bf16[32,7168]{1,0:T(8,128)(2,1)S(1)} %reshape.45, bf16[1,7168,256]{2,1,0:T(8,128)(2,1)S(1)} %copy-done.2, f32[32,256]{1,0:T(8,128)S(1)} %fusion.3), kind=kOutput, calls=%fused_computation.20 | convolution fusion | flops 117514240 | bytes 4177924 | tf_op jit(solution)/shard_map/dot_general | solution.py:55
  87.9 0.7 copy-done.3
  88.6 0.0 copy-start.7
  88.6 1.5 %convolution_convert_fusion = bf16[32,7168]{1,0:T(8,128)(2,1)} fusion(bf16[32,256]{1,0:T(8,128)(2,1)S(1)} %get-tuple-element.8, bf16[1,256,7168]{2,1,0:T(8,128)(2,1)S(1)} %copy-done.3), kind=kOutput, calls=%fused_computation | convolution fusion | flops 117669888 | bytes 4145152 | tf_op jit(solution)/shard_map/dot_general | solution.py:57
  90.1 0.0 reduce-scatter.2.cloned.1.call-update
  90.1 0.0 copy-done.7
  90.1 19.5 %reduce-scatter.2.cloned.1.call-done = bf16[32,1792]{1,0:T(8,128)(2,1)} async-done(((bf16[32,7168]{1,0:T(8,128)(2,1)}), bf16[32,1792]{1,0:T(8,128)(2,1)}) %reduce-scatter.2.cloned.1.call-update) | async-done | bytes 114704 | tf_op jit(solution)/shard_map/reduce_scatter | solution.py:61
  109.7 1.6 %convert_element_type.55 = bf16[8,4,1792]{2,1,0:T(4,128)(2,1)} reshape(bf16[32,1792]{1,0:T(8,128)(2,1)} %reduce-scatter.2.cloned.1.call-done) | data formatting | bytes 229376 | tf_op jit(solution)/shard_map/convert_element_type | solution.py:65
  111.2 5.5 %all-to-all-start.1 = ((bf16[8,4,1792]{2,1,0:T(4,128)(2,1)}), bf16[8,4,1792]{2,1,0:T(4,128)(2,1)S(1)}, u32[]{:S(2)}, u32[]{:S(2)}) async-start(bf16[8,4,1792]{2,1,0:T(4,128)(2,1)} %convert_element_type.55), calls=%async_computation.2 | async-start | bytes 229376 | tf_op jit(solution)/shard_map/all_to_all | solution.py:64
  116.7 1.1 abs_reduce_fusion
  117.8 6.6 %all-reduce = (f32[1]{0:T(128)}, f32[1]{0:T(128)}) all-reduce(f32[1]{0:T(128)} %bitcast.11, f32[1]{0:T(128)} %bitcast.12), channel_id=1, replica_groups=mesh['dp'=8,'tp'=4] {'tp'}, use_global_device_ids=true, to_apply=%region_7.8 | all-reduce | flops 2 | bytes 16 | tf_op jit(solution)/shard_map/pmax | solution.py:80
  124.4 0.0 all-to-all-done.1
  124.4 1.1 fusion.6
  (9 shorter events, 0.1 us)
Async XLA Ops:
  7.2 55.2 %all-reduce.3.cloned.1.call-start = ((), (), s32[]{:S(2)}) async-start(), calls=%async_computation.3 | async-start | bytes 3670016 | tf_op jit(solution)/shard_map/psum | solution.py:36
  7.2 2.8 %copy-start.4 = (bf16[64,1792]{1,0:T(8,128)(2,1)S(1)}, bf16[64,1792]{1,0:T(8,128)(2,1)}, u32[]{:S(2)}) copy-start(bf16[64,1792]{1,0:T(8,128)(2,1)} %param.9) | copy-start | bytes 688132
  10.1 2.4 %copy-start.6 = (s32[64,8]{0,1:T(8,128)S(1)}, s32[64,8]{0,1:T(8,128)}, u32[]{:S(2)}) copy-start(s32[64,8]{0,1:T(8,128)} %param.11) | copy-start | bytes 6148
  11.1 1.2 copy-start
  11.1 53.1 %copy-start.5 = (f32[7168]{0:T(1024)S(1)}, f32[7168]{0:T(1024)}, u32[]{:S(2)}) copy-start(f32[7168]{0:T(1024)} %param.10) | copy-start | bytes 86020
  12.4 97.3 %reduce-scatter.2.cloned.1.call-start = ((), (), s32[]{:S(2)}) async-start(), calls=%async_computation.4 | async-start | bytes 573440 | tf_op jit(solution)/shard_map/reduce_scatter | solution.py:61
  62.4 2.1 %copy-start.1 = (f32[64,7168]{1,0:T(8,128)S(1)}, f32[64,7168]{1,0:T(8,128)}, u32[]{:S(2)}) copy-start(f32[64,7168]{1,0:T(8,128)} %all-reduce.3.cloned.1.call-done) | copy-start | bytes 5505028
  83.4 3.1 %copy-start.2 = (bf16[1,7168,256]{2,1,0:T(8,128)(2,1)S(1)}, bf16[1,7168,256]{2,1,0:T(8,128)(2,1)}, u32[]{:S(2)}) copy-start(bf16[1,7168,256]{2,1,0:T(8,128)(2,1)} %param.14) | copy-start | bytes 11010052
  86.5 2.0 %copy-start.3 = (bf16[1,256,7168]{2,1,0:T(8,128)(2,1)S(1)}, bf16[1,256,7168]{2,1,0:T(8,128)(2,1)}, u32[]{:S(2)}) copy-start(bf16[1,256,7168]{2,1,0:T(8,128)(2,1)} %param.15) | copy-start | bytes 11010052
  88.6 1.5 %copy-start.7 = (bf16[64,8]{0,1:T(8,128)(2,1)S(1)}, bf16[64,8]{0,1:T(8,128)(2,1)}, u32[]{:S(2)}) copy-start(bf16[64,8]{0,1:T(8,128)(2,1)} %param.12) | copy-start | bytes 3076
  111.2 13.2 %all-to-all-start.1 = ((bf16[8,4,1792]{2,1,0:T(4,128)(2,1)}), bf16[8,4,1792]{2,1,0:T(4,128)(2,1)S(1)}, u32[]{:S(2)}, u32[]{:S(2)}) async-start(bf16[8,4,1792]{2,1,0:T(4,128)(2,1)} %convert_element_type.55), calls=%async_computation.2 | async-start | bytes 229376 | tf_op jit(solution)/shard_map/all_to_all | solution.py:64
Sparse Core Ops, SparseCore 0:
  12.5 49.8 all-reduce.2
  90.2 19.3 reduce-scatter.1
where the time goes:
time: 133 us; the launch traced here: 132 us
  waiting for transfers between devices  69.1 us (52%)
  blocking collectives  24.9 us (19%)
  between operations  14.2 us (11%)
  matrix products  7.23 us (5%)
  other arithmetic  6.96 us (5%)
  starting transfers between devices  5.58 us (4%)
  local copies, waits for them, and re-layouts  4.39 us (3%)
    psum x1, waiting for transfers between devices, on_device(): residual = lax.psum(summand, 'tp')  49.6 us
    reduce_scatter x1, waiting for transfers between devices, on_device(): lax.psum_scatter(partial_out.astype(jnp.bfloat16), 'tp', scatter_dimensio...  19.5 us
    all_to_all x1, blocking collectives, on_device(): lax.all_to_all(outgoing.reshape(experts, EXPERT_SLOTS, piece_width), 'dp'...  18.3 us
    pmax x1, blocking collectives, on_device(): input_peak, hidden_peak = lax.pmax((input_peak, hidden_peak), 'tp')  6.59 us
    all_to_all x1, starting transfers between devices, on_device(): lax.all_to_all(expert_cols.reshape(experts, EXPERT_SLOTS, columns).astype...  5.5 us
    dot_general x1, matrix products, on_device(): jnp.dot(expert_slot_rows, w_gate[0], preferred_element_type=jnp.float32)  2.92 us
    convert_element_type x1, other arithmetic, on_device(): partial_value = attn_partial[0].astype(jnp.float32)  2.83 us
  transfers between devices with their start and end apart: 3, of which 2 were waited for; matrix products, arithmetic and copies ran while one was open for 1% of the time, Pallas kernels for 0%

commit v1 on v0

v1 whole, which is shorter than its diff:
```python
import jax
import jax.numpy as jnp
from jax import lax
from jax.sharding import Mesh
from jax.sharding import PartitionSpec as P

EXPERT_SLOTS = 4
LANES = 128
eps = 1e-06
BF = jnp.bfloat16
F32 = jnp.float32


def route_tables(expert_ids, route_prob, experts, capacity):
    matches = expert_ids[:, :, None] == jnp.arange(experts, dtype=jnp.int32)[None, None, :]
    onehot = jnp.sum(matches.astype(jnp.int32), axis=1)
    weight = jnp.sum(jnp.where(matches, route_prob[:, :, None].astype(F32), F32(0.0)), axis=1)
    before = jnp.cumsum(onehot, axis=0) - onehot
    placing = (onehot.T[:, None, :] == 1) & (
        before.T[:, None, :] == jnp.arange(capacity, dtype=jnp.int32)[None, :, None]
    )
    return weight, placing


def shift(x, axis, by):
    n = lax.axis_size(axis)
    return lax.ppermute(x, axis, [(i, (i + by) % n) for i in range(n)])


def on_device(attn_partial, hidden_in, norm_gain, expert_ids, route_prob, w_gate, w_up, w_down):
    experts, his, los = lax.axis_size("dp"), lax.axis_size("hi"), lax.axis_size("lo")
    h, l = lax.axis_index("hi"), lax.axis_index("lo")
    tokens, cols = hidden_in.shape
    slots = experts * EXPERT_SLOTS
    partial = attn_partial[0]

    def piece(x, hh, ll):
        return lax.dynamic_slice_in_dim(x, (hh * los + ll) * cols, cols, 1)

    def half(x, ll):
        return jnp.concatenate([piece(x, hh, ll) for hh in range(his)], axis=1)

    pair = half(partial, l).astype(F32)
    for k in range(1, los):
        pair = pair + shift(half(partial, (l + k) % los), "lo", k).astype(F32)
    residual = lax.dynamic_slice_in_dim(pair, h * cols, cols, 1) + hidden_in.astype(F32)
    for k in range(1, his):
        out = lax.dynamic_slice_in_dim(pair, (h + k) % his * cols, cols, 1).astype(BF)
        residual = residual + shift(out, "hi", k).astype(F32)

    weight, placing = route_tables(expert_ids, route_prob, experts, EXPERT_SLOTS)
    selection = placing.reshape(slots, tokens).astype(BF)
    chosen = jnp.dot(selection, residual.astype(BF), preferred_element_type=F32).astype(BF)
    outgoing = jnp.broadcast_to(
        chosen.reshape(experts, 1, EXPERT_SLOTS, cols), (experts, his, EXPERT_SLOTS, cols)
    ).reshape(experts * his, EXPERT_SLOTS, cols)
    incoming = lax.all_to_all(outgoing, ("dp", "hi"), 0, 0, tiled=True)
    incoming = incoming.reshape(experts, his, EXPERT_SLOTS, cols)
    own = jnp.concatenate([incoming[:, hh].reshape(slots, cols) for hh in range(his)], axis=1)
    held = [own] + [shift(own, "lo", k) for k in range(1, los)]
    by_lo = []
    for ll in range(los):
        value = held[0]
        for k in range(1, los):
            value = jnp.where((l - ll) % los == k, held[k], value)
        by_lo.append(value)
    rows = jnp.concatenate(
        [by_lo[ll][:, hh * cols : (hh + 1) * cols] for hh in range(his) for ll in range(los)], axis=1
    ).astype(F32)
    mean_sq = jnp.mean(rows * rows, axis=1, keepdims=True)
    slot_rows = (rows * lax.rsqrt(mean_sq + eps) * norm_gain).astype(BF)
    gate_val = jnp.dot(slot_rows, w_gate[0], preferred_element_type=F32)
    up_val = jnp.dot(slot_rows, w_up[0], preferred_element_type=F32)
    hidden_act = (jax.nn.silu(gate_val) * up_val).astype(BF)
    partial_out = jnp.dot(hidden_act, w_down[0], preferred_element_type=F32)
    input_peak = jnp.max(jnp.abs(slot_rows.astype(F32)))
    hidden_peak = jnp.max(jnp.abs(hidden_act.astype(F32)))

    def tagged(x, peak):
        return jnp.concatenate([x.astype(BF), jnp.full((x.shape[0], LANES), peak, BF)], axis=1)

    total = half(partial_out, l)
    for k in range(1, los):
        got = shift(tagged(half(partial_out, (l + k) % los), hidden_peak), "lo", k)
        total = total + got[:, : his * cols].astype(F32)
        hidden_peak = jnp.maximum(hidden_peak, got[0, his * cols].astype(F32))
    back = jnp.stack(
        [
            tagged(total[:, hh * cols : (hh + 1) * cols], hidden_peak).reshape(
                experts, EXPERT_SLOTS, cols + LANES
            )
            for hh in range(his)
        ],
        axis=1,
    ).reshape(experts * his, EXPERT_SLOTS, cols + LANES)
    returned = lax.all_to_all(back, ("dp", "hi"), 0, 0, tiled=True)
    peaks = lax.dynamic_slice_in_dim(
        returned[:, 0, cols].reshape(experts, his), lax.axis_index("dp"), 1, 0
    )
    combine = (placing.astype(F32) * weight.T[:, None, :]).astype(BF)
    combine = jnp.broadcast_to(
        combine[:, None], (experts, his, EXPERT_SLOTS, tokens)
    ).reshape(slots * his, tokens)
    moe_out = jnp.dot(
        combine.T,
        returned[:, :, :cols].reshape(slots * his, cols),
        preferred_element_type=F32,
    )
    layer_out = (residual + moe_out).astype(BF)
    return layer_out, input_peak.reshape(1), jnp.max(peaks.astype(F32)).reshape(1)


def solution(mesh):
    tp = mesh.shape["tp"]
    lo = 2 if tp % 2 == 0 else 1
    split = Mesh(mesh.devices.reshape(mesh.shape["dp"], tp // lo, lo), ("dp", "hi", "lo"))
    tps = ("hi", "lo")
    placed = (
        P(tps, "dp", None),
        P("dp", tps),
        P(),
        P("dp", None),
        P("dp", None),
        P("dp", None, tps),
        P("dp", None, tps),
        P("dp", tps, None),
    )
    return jax.shard_map(
        on_device,
        mesh=split,
        in_specs=placed,
        out_specs=(P("dp", tps), P("dp"), P("dp")),
        check_vma=False,
    )
```

time: 133 us -> 61 us (0.46)
  waiting for transfers between devices: 69.1 us -> 18.4 us
  between operations: 14.2 us -> 4.07 us
  blocking collectives: 24.9 us -> 15.6 us
  other arithmetic: 6.96 us -> 5.15 us
  starting transfers between devices: 5.58 us -> 7.27 us
    psum x1 -> x0, waiting for transfers between devices: 49.6 us -> none  [on_device(): residual = lax.psum(summand, 'tp')]
    reduce_scatter x1 -> x0, waiting for transfers between devices: 19.5 us -> none  [on_device(): lax.psum_scatter(partial_out.astype(jnp.bfloat16), 'tp', scatter_dimensio...]
    all_to_all x1, waiting for transfers between devices: 0.01 us -> 9.26 us  [on_device(): returned = lax.all_to_all(back, ('dp', 'hi'), 0, 0, tiled=True)]
    ppermute x0 -> x4, waiting for transfers between devices: none -> 9.16 us  [shift(): return lax.ppermute(x, axis, [(i, (i + by) % n) for i in range(n)])]
    pmax x1 -> x0, blocking collectives: 6.59 us -> none  [on_device(): input_peak, hidden_peak = lax.pmax((input_peak, hidden_peak), 'tp')]
    ppermute x0 -> x4, starting transfers between devices: none -> 3.74 us  [shift(): return lax.ppermute(x, axis, [(i, (i + by) % n) for i in range(n)])]
    convert_element_type x2, other arithmetic: 2.83 us -> 0.02 us  [the longest x1 0.01 us: on_device(): combine = (placing.astype(F32) * weight.T[:, None, :]).astype(BF)]
    all_to_all x1, blocking collectives: 18.3 us -> 15.6 us  [on_device(): incoming = lax.all_to_all(outgoing, ('dp', 'hi'), 0, 0, tiled=True)]
  transfers between devices with their start and end apart: 3 -> 5, of which waited for: 2 -> 5; matrix products, arithmetic and copies ran while one was open for 1% -> 3% of each run, Pallas kernels for 0% -> 0%
where the time goes in v1:
time: 61 us; the launch traced here: 60.6 us
  waiting for transfers between devices  18.4 us (30%)
  blocking collectives  15.6 us (26%)
  starting transfers between devices  7.27 us (12%)
  matrix products  6.29 us (10%)
  other arithmetic  5.15 us (8%)
  between operations  4.07 us (7%)
  local copies, waits for them, and re-layouts  3.79 us (6%)
    all_to_all x1, blocking collectives, on_device(): incoming = lax.all_to_all(outgoing, ('dp', 'hi'), 0, 0, tiled=True)  15.6 us
    all_to_all x1, waiting for transfers between devices, on_device(): returned = lax.all_to_all(back, ('dp', 'hi'), 0, 0, tiled=True)  9.26 us
    ppermute x4, waiting for transfers between devices, shift(): return lax.ppermute(x, axis, [(i, (i + by) % n) for i in range(n)])  9.16 us
    ppermute x4, starting transfers between devices, shift(): return lax.ppermute(x, axis, [(i, (i + by) % n) for i in range(n)])  3.74 us
    all_to_all x1, starting transfers between devices, on_device(): returned = lax.all_to_all(back, ('dp', 'hi'), 0, 0, tiled=True)  3.53 us
    dot_general x1, matrix products, on_device(): gate_val = jnp.dot(slot_rows, w_gate[0], preferred_element_type=F32)  2.97 us
    dynamic_slice x2, local copies, waits for them, and re-layouts, piece(): return lax.dynamic_slice_in_dim(x, (hh * los + ll) * cols, cols, 1)  1.43 us
    dot_general x1, matrix products, on_device(): up_val = jnp.dot(slot_rows, w_up[0], preferred_element_type=F32)  1.4 us
  transfers between devices with their start and end apart: 5, of which 5 were waited for; matrix products, arithmetic and copies ran while one was open for 3% of the time, Pallas kernels for 0%

profile of v1, /device:TPU:0, one launch (start us, length us, event | category | flops | bytes accessed | tf_op | source)
XLA Modules:
  0.0 60.6 jit_solution(9338435463716641384)
XLA Ops:
  0.6 0.0 copy-start.1
  0.7 1.4 %dynamic-slice_bitcast_fusion.3 = (bf16[64,1792]{1,0:T(8,128)(2,1)S(1)}, bf16[64,1792]{1,0:T(8,128)(2,1)S(1)}, bf16[64,1792]{1,0:T(8,128)(2,1)S(1)}, bf16[64,1792]{1,0:T(8,128)(2,1)S(1)}) fusion(bf16[1,64,7168]{2,1,0:T(8,128)(2,1)} %param.8, s32[]{:T(128)S(6)} %select_n.64, s32[]{:T(128)S(6)} %select_n.65, s32[]{:T(128)S(6)} %select_n.68, s32[]{:T(128)S(6)} %select_n.67), kind=kLoop, calls=%fused_computation.35 | loop fusion | bytes 1835024 | tf_op jit(solution)/shard_map/dynamic_slice | solution.py:38
  2.1 0.0 copy-start.5
  2.1 0.6 collective-permute-start
  2.7 0.7 %convert_reduce_fusion = s32[64,8]{0,1:T(8,128)S(1)} fusion(s32[64,8]{0,1:T(8,128)} %param.11), kind=kLoop, calls=%fused_computation.42 | loop fusion | flops 11776 | bytes 4096 | tf_op jit(solution)/shard_map/reduce_sum | solution.py:16
  3.4 0.1 copy.22
  3.5 0.1 reduce_window_sum.11
  3.6 0.6 collective-permute-done
  4.1 0.1 convert_add_fusion
  4.2 0.0 copy-start.2
  4.3 2.9 %collective-permute-start.1 = (bf16[64,1792]{1,0:T(8,128)(2,1)S(1)}, bf16[64,1792]{1,0:T(8,128)(2,1)S(1)}, u32[]{:S(2)}, u32[]{:S(2)}) collective-permute-start(bf16[64,1792]{1,0:T(8,128)(2,1)S(1)} %dynamic-slice_convert_fusion), channel_id=1, source_target_pairs={{0,2},{2,0},{1,3},{3,1},{4,6},{6,4},{5,7},{7,5},{8,10},{10,8},{9,1... | collective-permute-start | bytes 688136 | tf_op jit(solution)/shard_map/ppermute | solution.py:27
  7.2 0.1 copy.24
  7.3 0.1 eq.75
  7.4 5.7 %collective-permute-done.1 = bf16[64,1792]{1,0:T(8,128)(2,1)S(1)} collective-permute-done((bf16[64,1792]{1,0:T(8,128)(2,1)S(1)}, bf16[64,1792]{1,0:T(8,128)(2,1)S(1)}, u32[]{:S(2)}, u32[]{:S(2)}) %collective-permute-start.1) | collective-permute-done | bytes 229408 | tf_op jit(solution)/shard_map/ppermute | solution.py:27
  13.1 0.0 copy-done.1
  13.1 0.2 convolution_convert_fusion
  13.4 0.1 broadcast_in_dim.22
  13.5 15.6 %all_to_all.10 = bf16[16,4,1792]{2,1,0:T(4,128)(2,1)S(1)} all-to-all(bf16[16,4,1792]{2,1,0:T(4,128)(2,1)S(1)} %bitcast.45), channel_id=1, replica_groups=mesh['dp'=8,'hi'=2,'lo'=2] {'dp','hi'}, dimensions={0} | all-to-all | bytes 458752 | tf_op jit(solution)/shard_map/all_to_all | solution.py:57
  29.1 0.1 fusion.31
  29.3 0.1 collective-permute-start.2
  29.4 0.0 copy-done.5
  29.4 0.0 copy-start.6
  29.4 1.4 %collective-permute-done.2 = bf16[32,3584]{1,0:T(8,128)(2,1)S(1)} collective-permute-done((bf16[32,3584]{1,0:T(8,128)(2,1)S(1)}, bf16[32,3584]{1,0:T(8,128)(2,1)S(1)}, u32[]{:S(2)}, u32[]{:S(2)}) %collective-permute-start.2) | collective-permute-done | bytes 229408 | tf_op jit(solution)/shard_map/ppermute | solution.py:27
  30.9 0.2 fusion.13
  31.1 0.0 copy-done.2
  31.1 0.0 copy-start
  31.2 3.0 %fusion.4 = f32[32,256]{1,0:T(8,128)S(1)} fusion(bf16[1,7168,256]{2,1,0:T(8,128)(2,1)} %param.13, f32[7168]{0:T(1024)S(1)} %copy-done.2, f32[32]{0:T(128)S(1)} %add_rsqrt_fusion, bf16[32,1792]{1,0:T(8,128)(2,1)S(1)} %get-tuple-element.21, bf16[32,1792]{1,0:T(8,128)(2,1)S(1)} %get-tuple-element.14, bf16[32,1792]{1,0:T(8,128)(2,1)S(1)} %get-tuple-element.22, ...), kind=kOutput, calls=%fused_computation.4 | convolution fusion | flops 119963648 | bytes 4190336 | tf_op jit(solution)/shard_map/dot_general | solution.py:72
  34.1 0.0 copy-done.6
  34.1 1.4 %abs_reduce_fusion.1 = (bf16[]{:T(256)}, bf16[32,256]{1,0:T(8,128)(2,1)S(1)}) fusion(bf16[1,7168,256]{2,1,0:T(8,128)(2,1)S(1)} %copy-done.6, f32[7168]{0:T(1024)S(1)} %copy-done.2, f32[32]{0:T(128)S(1)} %add_rsqrt_fusion, bf16[32,1792]{1,0:T(8,128)(2,1)S(1)} %get-tuple-element.21, bf16[32,1792]{1,0:T(8,128)(2,1)S(1)} %get-tuple-element.14, ...), kind=kOutput, calls=%fused_computation.39 | convolution fusion | flops 120037376 | bytes 4206722 | tf_op jit(solution)/shard_map/dot_general | solution.py:73
  35.5 0.0 copy-done
  35.5 0.0 copy-start.4
  35.5 0.0 copy-start.3
  35.6 0.7 %fusion = f32[32,7168]{1,0:T(8,128)S(1)} fusion(bf16[32,256]{1,0:T(8,128)(2,1)S(1)} %get-tuple-element.20, bf16[1,256,7168]{2,1,0:T(8,128)(2,1)S(1)} %copy-done), kind=kOutput, calls=%fused_computation | convolution fusion | flops 117440512 | bytes 4603904 | tf_op jit(solution)/shard_map/dot_general | solution.py:75
  36.3 0.7 %fusion.19 = bf16[32,3712]{1,0:T(8,128)(2,1)S(1)} fusion(bf16[32,1792]{1,0:T(8,128)(2,1)S(1)} %get-tuple-element.4, bf16[32,1792]{1,0:T(8,128)(2,1)S(1)} %get-tuple-element.3, bf16[]{:T(256)} %get-tuple-element.19), kind=kLoop, calls=%fused_computation.28 | loop fusion | flops 831488 | bytes 466946 | tf_op jit(solution)/shard_map/concatenate | solution.py:41
  37.0 0.2 collective-permute-start.3
  37.2 1.5 %collective-permute-done.3 = bf16[32,3712]{1,0:T(8,128)(2,1)} collective-permute-done((bf16[32,3712]{1,0:T(8,128)(2,1)S(1)}, bf16[32,3712]{1,0:T(8,128)(2,1)}, u32[]{:S(2)}, u32[]{:S(2)}) %collective-permute-start.3) | collective-permute-done | bytes 237600 | tf_op jit(solution)/shard_map/ppermute | solution.py:27
  38.7 1.2 %slice.59 = bf16[1,1]{1,0:T(2,128)(2,1)} slice(bf16[32,3712]{1,0:T(8,128)(2,1)} %collective-permute-done.3), slice={[0:1], [3584:3585]} | slice | bytes 4 | tf_op jit(solution)/shard_map/slice | solution.py:86
  41.2 1.0 %fusion.18 = bf16[32,3584]{1,0:T(8,128)(2,1)S(1)} fusion(f32[32,1792]{1,0:T(8,128)S(1)} %get-tuple-element.6, f32[32,1792]{1,0:T(8,128)S(1)} %get-tuple-element.5, bf16[32,3712]{1,0:T(8,128)(2,1)} %collective-permute-done.3), kind=kLoop, calls=%fused_computation.24 | loop fusion | flops 458752 | bytes 917504 | tf_op jit(solution)/shard_map/convert.5
  42.2 0.0 copy-done.4
  42.3 0.8 %pad_maximum_fusion.2 = bf16[8,2,4,1920]{3,2,1,0:T(4,128)(2,1)} fusion(bf16[8,1,4,1920]{3,2,1,0:T(4,128)(2,1)S(1)} %bitcast.47, bf16[8,1,4,1920]{3,2,1,0:T(4,128)(2,1)S(1)} %bitcast.46), kind=kLoop, calls=%fused_computation.27 | loop fusion | flops 122880 | bytes 491520 | tf_op jit(solution)/shard_map/stack | solution.py:87
  43.2 3.5 %all-to-all-start.1 = ((bf16[16,4,1920]{2,1,0:T(4,128)(2,1)}), bf16[16,4,1920]{2,1,0:T(4,128)(2,1)S(1)}, u32[]{:S(2)}, u32[]{:S(2)}) async-start(bf16[16,4,1920]{2,1,0:T(4,128)(2,1)} %bitcast.18), calls=%async_computation.1 | async-start | bytes 491520 | tf_op jit(solution)/shard_map/all_to_all | solution.py:96
  46.7 0.0 copy-done.3
  46.8 0.8 %abs_reduce_fusion = f32[]{:T(128)} fusion(f32[7168]{0:T(1024)S(1)} %copy-done.2, f32[32]{0:T(128)S(1)} %add_rsqrt_fusion, bf16[32,1792]{1,0:T(8,128)(2,1)S(1)} %get-tuple-element.21, bf16[32,1792]{1,0:T(8,128)(2,1)S(1)} %get-tuple-element.14, bf16[32,1792]{1,0:T(8,128)(2,1)S(1)} %get-tuple-element.22, bf16[32,1792]{1,0:T(8,128)(2,1)S(1)} %get-tuple-element.13), kind=kLoop, calls=%fused_computation.16 | loop fusion | flops 3211263 | bytes 487556 | tf_op jit(solution)/shard_map/reduce_max | solution.py:76
  47.5 9.3 %all-to-all-done.1 = bf16[16,4,1920]{2,1,0:T(4,128)(2,1)S(1)} async-done(((bf16[16,4,1920]{2,1,0:T(4,128)(2,1)}), bf16[16,4,1920]{2,1,0:T(4,128)(2,1)S(1)}, u32[]{:S(2)}, u32[]{:S(2)}) %all-to-all-start.1) | async-done | bytes 245792 | tf_op jit(solution)/shard_map/all_to_all | solution.py:96
  56.8 0.1 slice.61
  56.9 0.1 reshape.70
  57.0 0.2 slice_reduce_fusion
  57.2 0.1 reshape_squeeze.11
  57.2 0.6 %fusion.26 = bf16[]{:T(256)} fusion(bf16[8,2]{1,0:T(8,128)(2,1)S(1)} %reshape_squeeze.11, s32[]{:T(128)S(6)} %select_n.79), kind=kLoop, calls=%fused_computation.58 | loop fusion | flops 1 | bytes 10 | tf_op jit(solution)/shard_map/reduce_max | solution.py:110
  58.5 1.0 %fusion.6 = bf16[64,1792]{1,0:T(8,128)(2,1)} fusion(bf16[64,64]{1,0:T(8,128)(2,1)S(1)} %bitcast.49, bf16[64,1792]{1,0:T(8,128)(2,1)S(1)} %reshape.70, bf16[64,1792]{1,0:T(8,128)(2,1)S(1)} %collective-permute-done.1, bf16[64,1792]{1,0:T(8,128)(2,1)S(1)} %copy-done.1, f32[64,3584]{1,0:T(8,128)S(1)} %convert_add_fusion, s32[]{:T(128)S(6)} %select_n.69), kind=kOutput, calls=%fused_computation.7 | convolution fusion | flops 15368192 | bytes 1384452 | tf_op jit(solution)/shard_map/dot_general | solution.py:104
  (26 shorter events, 0.5 us)
Async XLA Ops:
  0.6 12.5 %copy-start.1 = (bf16[64,1792]{1,0:T(8,128)(2,1)S(1)}, bf16[64,1792]{1,0:T(8,128)(2,1)}, u32[]{:S(2)}) copy-start(bf16[64,1792]{1,0:T(8,128)(2,1)} %param.9) | copy-start | bytes 688132
  2.1 27.3 %copy-start.5 = (bf16[64,8]{0,1:T(8,128)(2,1)S(1)}, bf16[64,8]{0,1:T(8,128)(2,1)}, u32[]{:S(2)}) copy-start(bf16[64,8]{0,1:T(8,128)(2,1)} %param.12) | copy-start | bytes 3076
  2.1 2.0 %collective-permute-start = (bf16[64,3584]{1,0:T(8,128)(2,1)S(1)}, bf16[64,3584]{1,0:T(8,128)(2,1)S(1)}, u32[]{:S(2)}, u32[]{:S(2)}) collective-permute-start(bf16[64,3584]{1,0:T(8,128)(2,1)S(1)} %pad_maximum_fusion), channel_id=1, source_target_pairs={{0,1},{1,0},{2,3},{3,2},{4,5},{5,4},{6,7},{7,6},{8,9},{9,8},{10,11... | collective-permute-start | bytes 1376264 | tf_op jit(solution)/shard_map/ppermute | solution.py:27
  4.2 26.9 %copy-start.2 = (f32[7168]{0:T(1024)S(1)}, f32[7168]{0:T(1024)}, u32[]{:S(2)}) copy-start(f32[7168]{0:T(1024)} %param.10) | copy-start | bytes 86020
  4.3 8.8 %collective-permute-start.1 = (bf16[64,1792]{1,0:T(8,128)(2,1)S(1)}, bf16[64,1792]{1,0:T(8,128)(2,1)S(1)}, u32[]{:S(2)}, u32[]{:S(2)}) collective-permute-start(bf16[64,1792]{1,0:T(8,128)(2,1)S(1)} %dynamic-slice_convert_fusion), channel_id=1, source_target_pairs={{0,2},{2,0},{1,3},{3,1},{4,6},{6,4},{5,7},{7,5},{8,10},{10,8},{9,1... | collective-permute-start | bytes 688136 | tf_op jit(solution)/shard_map/ppermute | solution.py:27
  29.3 1.6 %collective-permute-start.2 = (bf16[32,3584]{1,0:T(8,128)(2,1)S(1)}, bf16[32,3584]{1,0:T(8,128)(2,1)S(1)}, u32[]{:S(2)}, u32[]{:S(2)}) collective-permute-start(bf16[32,3584]{1,0:T(8,128)(2,1)S(1)} %constant_dynamic-update-slice_fusion), channel_id=1, source_target_pairs={{0,1},{1,0},{2,3},{3,2},{4,5},{5,4},{6,7},{7,6},{8,9},{9,8},{10,11... | collective-permute-start | bytes 688136 | tf_op jit(solution)/shard_map/ppermute | solution.py:27
  29.4 4.7 %copy-start.6 = (bf16[1,7168,256]{2,1,0:T(8,128)(2,1)S(1)}, bf16[1,7168,256]{2,1,0:T(8,128)(2,1)}, u32[]{:S(2)}) copy-start(bf16[1,7168,256]{2,1,0:T(8,128)(2,1)} %param.14) | copy-start | bytes 11010052
  31.1 4.4 %copy-start = (bf16[1,256,7168]{2,1,0:T(8,128)(2,1)S(1)}, bf16[1,256,7168]{2,1,0:T(8,128)(2,1)}, u32[]{:S(2)}) copy-start(bf16[1,256,7168]{2,1,0:T(8,128)(2,1)} %param.15) | copy-start | bytes 11010052
  35.5 6.7 %copy-start.4 = (pred[1920]{0:T(1024)(128)(4,1)S(1)}, pred[1920]{0:T(1024)(128)(4,1)}, u32[]{:S(2)}) copy-start(pred[1920]{0:T(1024)(128)(4,1)} %constant.66.clone.1) | copy-start | bytes 5764
  35.5 11.2 %copy-start.3 = (s32[64,8]{0,1:T(8,128)S(1)}, s32[64,8]{0,1:T(8,128)}, u32[]{:S(2)}) copy-start(s32[64,8]{0,1:T(8,128)} %param.11) | copy-start | bytes 6148
  37.0 1.7 %collective-permute-start.3 = (bf16[32,3712]{1,0:T(8,128)(2,1)S(1)}, bf16[32,3712]{1,0:T(8,128)(2,1)}, u32[]{:S(2)}, u32[]{:S(2)}) collective-permute-start(bf16[32,3712]{1,0:T(8,128)(2,1)S(1)} %fusion.19), channel_id=1, source_target_pairs={{0,1},{1,0},{2,3},{3,2},{4,5},{5,4},{6,7},{7,6},{8,9},{9,8},{10,11... | collective-permute-start | bytes 712712 | tf_op jit(solution)/shard_map/ppermute | solution.py:27
  43.2 13.6 %all-to-all-start.1 = ((bf16[16,4,1920]{2,1,0:T(4,128)(2,1)}), bf16[16,4,1920]{2,1,0:T(4,128)(2,1)S(1)}, u32[]{:S(2)}, u32[]{:S(2)}) async-start(bf16[16,4,1920]{2,1,0:T(4,128)(2,1)} %bitcast.18), calls=%async_computation.1 | async-start | bytes 491520 | tf_op jit(solution)/shard_map/all_to_all | solution.py:96

commit v2 on v1

v2 whole, which is shorter than its diff:
```python
import jax
import jax.numpy as jnp
from jax import lax
from jax.experimental import pallas as pl
from jax.experimental.pallas import tpu as pltpu
from jax.sharding import Mesh
from jax.sharding import PartitionSpec as P

EXPERT_SLOTS = 4
SUBLANES = 8
LANES = 128
SPLIT = SUBLANES // EXPERT_SLOTS
eps = 1e-06
BF = jnp.bfloat16
F32 = jnp.float32
HIGHEST = lax.Precision.HIGHEST
VMEM = pl.BlockSpec(memory_space=pltpu.VMEM)
SMEM = pl.BlockSpec(memory_space=pltpu.SMEM)
HBM = pl.BlockSpec(memory_space=pltpu.HBM)
MIB = 1 << 20


def dot(a, b, precision=None):
    return jnp.dot(a, b, precision=precision, preferred_element_type=F32)


def iota(shape, axis):
    return lax.broadcasted_iota(jnp.int32, shape, axis)


def shift(x, axis, by):
    n = lax.axis_size(axis)
    return lax.ppermute(x, axis, [(i, (i + by) % n) for i in range(n)])


def stay(*arrays):
    return [pltpu.with_memory_space_constraint(a, pltpu.HBM) for a in arrays]


def early_kernel(his, los, partial_ref, hidden_ref, ids_hbm, prob_hbm, *refs):
    own_ref, held_ref, pick_ref, comb_ref, ids_ref, prob_ref, small, large = refs
    cols = hidden_ref.shape[1]
    l = lax.axis_index("lo")
    first = [
        pltpu.make_async_copy(ids_hbm, ids_ref, small.at[0]),
        pltpu.make_async_copy(prob_hbm, prob_ref, small.at[1]),
    ]
    rest = [pltpu.make_async_copy(hidden_ref, held_ref, large.at[his])]
    for x in range(his):
        at = pl.multiple_of((x * los + l) * cols, LANES)
        rest.append(
            pltpu.make_async_copy(
                partial_ref.at[0, :, pl.ds(at, cols)], own_ref.at[x], large.at[x]
            )
        )
    for copy in first + rest:
        copy.start()
    for copy in first:
        copy.wait()
    names, tokens = ids_ref.shape
    rows, wide = pick_ref.shape[1], comb_ref.shape[2]
    experts = rows // SUBLANES
    ids, prob = ids_ref[...], prob_ref[...].astype(F32)
    expert = iota((experts, tokens), 0)
    match = jnp.zeros((experts, tokens), F32)
    weight = jnp.zeros((experts, tokens), F32)
    for k in range(names):
        same = ids[k : k + 1] == expert
        match = match + jnp.where(same, 1.0, 0.0)
        weight = weight + jnp.where(same, prob[k : k + 1], 0.0)
    earlier = jnp.where(iota((tokens, tokens), 0) < iota((tokens, tokens), 1), 1.0, 0.0)
    slot = jnp.where(match > 0.0, dot(match, earlier, HIGHEST), -1.0)

    def spread(x, count, per):
        owner = jnp.where(iota((count, experts), 0) // per == iota((count, experts), 1), 1.0, 0.0)
        return dot(owner, x, HIGHEST)

    at = iota((rows, tokens), 0)
    slots = spread(slot, rows, SUBLANES)
    for s in range(SPLIT):
        here = (slots == (at % EXPERT_SLOTS).astype(F32)) & (at // EXPERT_SLOTS % SPLIT == s)
        pick_ref[s] = jnp.where(here, 1.0, 0.0).astype(BF)
    at = iota((wide, tokens), 0)
    slots, weights = spread(slot, wide, his * SUBLANES), spread(weight, wide, his * SUBLANES)
    for s in range(SPLIT):
        here = (slots == (at % EXPERT_SLOTS).astype(F32)) & (at // EXPERT_SLOTS % SPLIT == s)
        comb_ref[s] = jnp.where(here, weights, 0.0).T.astype(BF)
    for copy in rest:
        copy.wait()


def choose_kernel(los, pick_ref, own_ref, *refs):
    others, sel_ref, res_ref = refs[: los - 1], refs[los - 1], refs[los]
    his, _, cols = own_ref.shape
    width = cols // SPLIT
    h, l = lax.axis_index("hi"), lax.axis_index("lo")
    for k in range(1, his):
        hh = lax.rem(h + k, his)
        pair = own_ref[hh].astype(F32)
        at = pl.multiple_of((hh * los + l) * cols, LANES)
        for other in others:
            pair = pair + other[:, pl.ds(at, cols)].astype(F32)
        pair = pair.astype(BF)
        res_ref[k - 1] = pair
        chosen = dot(pick_ref[0], pair[:, :width])
        for s in range(1, SPLIT):
            chosen = chosen + dot(pick_ref[s], pair[:, s * width : (s + 1) * width])
        sel_ref[k - 1] = chosen.astype(BF)


def load_kernel(los, *refs):
    gain_hbm, wg_hbm, wu_hbm, hidden_ref, pick_ref, own_ref = refs[:6]
    others = refs[6 : 5 + los]
    gain_ref, wg_ref, wu_ref, mine_ref, sel_ref, sems = refs[5 + los :]
    copies = [
        pltpu.make_async_copy(wg_hbm, wg_ref, sems.at[0]),
        pltpu.make_async_copy(wu_hbm, wu_ref, sems.at[1]),
        pltpu.make_async_copy(gain_hbm, gain_ref, sems.at[2]),
    ]
    for copy in copies:
        copy.start()
    _, cols = hidden_ref.shape
    width = cols // SPLIT
    h, l = lax.axis_index("hi"), lax.axis_index("lo")
    mine = hidden_ref[...].astype(F32) + own_ref[h].astype(F32)
    at = pl.multiple_of((h * los + l) * cols, LANES)
    for other in others:
        mine = mine + other[:, pl.ds(at, cols)].astype(F32)
    mine_ref[...] = mine
    chosen = dot(pick_ref[0].astype(F32), mine[:, :width], HIGHEST)
    for s in range(1, SPLIT):
        chosen = chosen + dot(
            pick_ref[s].astype(F32), mine[:, s * width : (s + 1) * width], HIGHEST
        )
    sel_ref[...] = chosen
    for copy in copies:
        copy.wait()


def dispatch_kernel(n, sel_ref, *refs):
    gots, out_ref = refs[:n], refs[n]
    experts, his, subs, width = out_ref.shape
    chosen = sel_ref[...]
    for got in gots:
        chosen = chosen + got[...].astype(F32)
    chosen = chosen.astype(BF).reshape(experts, subs, width)
    for x in range(his):
        out_ref[:, x] = chosen


def regroup(even, odd):
    top = iota(even.shape, 0) < EXPERT_SLOTS
    return (
        jnp.where(top, even, pltpu.roll(odd, EXPERT_SLOTS, 0)),
        jnp.where(top, pltpu.roll(even, EXPERT_SLOTS, 0), odd),
    )


def gather_rows(ref, x, experts):
    his = ref.shape[0] // experts
    low, high = [], []
    for p in range(0, experts, SPLIT):
        even, odd = ref[p * his + x].astype(F32), ref[(p + 1) * his + x].astype(F32)
        first, second = regroup(even, odd)
        low.append(first)
        high.append(second)
    return jnp.concatenate(
        [jnp.concatenate(low, axis=0), jnp.concatenate(high, axis=0)], axis=1
    )


def products(los, helds, gain_ref, wg_ref, wu_ref, gate, up, square, top):
    l, experts = lax.axis_index("lo"), lax.axis_size("dp")
    for k, held in helds:
        his = held.shape[0] // experts
        cols = SPLIT * held.shape[2]
        c = lax.rem(l - k + los, los)
        for x in range(his):
            value = gather_rows(held, x, experts)
            at = pl.multiple_of((x * los + c) * cols, LANES)
            square = square + jnp.sum(value * value, axis=1, keepdims=True)
            value = value * gain_ref[:, pl.ds(at, cols)]
            top = jnp.maximum(top, jnp.max(jnp.abs(value), axis=1, keepdims=True))
            value = value.astype(BF)
            gate = gate + dot(value, wg_ref[0, pl.ds(at, cols), :])
            up = up + dot(value, wu_ref[0, pl.ds(at, cols), :])
    return gate, up, square, top


def first_kernel(los, gain_ref, wg_ref, wu_ref, wd_hbm, held_ref, *refs):
    wd_ref, gate_ref, up_ref, square_ref, top_ref, sem = refs
    copy = pltpu.make_async_copy(wd_hbm, wd_ref, sem)
    copy.start()
    slots = gate_ref.shape[0]
    zero, none = jnp.zeros(gate_ref.shape, F32), jnp.zeros((slots, 1), F32)
    gate, up, square, top = products(
        los, [(0, held_ref)], gain_ref, wg_ref, wu_ref, zero, zero, none, none
    )
    gate_ref[...] = gate
    up_ref[...] = up
    square_ref[...] = jnp.broadcast_to(square, square_ref.shape)
    top_ref[...] = jnp.broadcast_to(top, top_ref.shape)
    copy.wait()


def down(act, wd_ref, his, los, c):
    cols = wd_ref.shape[2] // (his * los)
    for x in range(his):
        at = pl.multiple_of((x * los + c) * cols, LANES)
        yield slice(x * cols, (x + 1) * cols), dot(act, wd_ref[0, :, pl.ds(at, cols)])


def second_kernel(his, los, gain_ref, wg_ref, wu_ref, wd_ref, *refs):
    gate_ref, up_ref, square_ref, top_ref = refs[:4]
    helds = refs[4 : 3 + los]
    send_ref, act_ref, peak_ref, out_ref = refs[3 + los :]
    gate, up, square, top = products(
        los,
        list(enumerate(helds, 1)),
        gain_ref,
        wg_ref,
        wu_ref,
        gate_ref[...],
        up_ref[...],
        square_ref[:, :1],
        top_ref[:, :1],
    )
    scale = lax.rsqrt(square / wg_ref.shape[1] + eps)
    out_ref[0] = jnp.max(top * scale).astype(BF).astype(F32)
    gate, up = gate * scale, up * scale
    act = (gate / (1.0 + jnp.exp(-gate)) * up).astype(BF)
    act_ref[...] = act
    peak = jnp.max(jnp.abs(act.astype(F32)))
    peak_ref[...] = jnp.full(peak_ref.shape, peak, F32)
    l, slots = lax.axis_index("lo"), act.shape[0]
    for k in range(1, los):
        for cut, value in down(act, wd_ref, his, los, lax.rem(l + k, los)):
            send_ref[k - 1, :, cut] = value.astype(BF)
        send_ref[k - 1, :, -LANES:] = jnp.full((slots, LANES), peak, F32).astype(BF)


def third_kernel(his, los, act_ref, wd_ref, mine_ref, *refs):
    rests, keep_ref, res_ref = refs[: his - 1], refs[his - 1], refs[his]
    for cut, value in down(act_ref[...], wd_ref, his, los, lax.axis_index("lo")):
        keep_ref[:, cut] = value
    res = mine_ref[...]
    for rest in rests:
        res = res + rest[...].astype(F32)
    res_ref[...] = res


def pair_kernel(his, n, keep_ref, peak_ref, *refs):
    gots, out_ref = refs[:n], refs[n]
    blocks, subs, width = out_ref.shape
    width = width - LANES
    cols, experts = SPLIT * width, blocks // his
    peak = jnp.max(peak_ref[...])
    for got in gots:
        peak = jnp.maximum(peak, jnp.max(got[:, -LANES:].astype(F32)))
    for x in range(his):
        total = keep_ref[:, x * cols : (x + 1) * cols]
        for got in gots:
            total = total + got[:, x * cols : (x + 1) * cols].astype(F32)
        for p in range(0, experts, SPLIT):
            rows = slice(p * EXPERT_SLOTS, p * EXPERT_SLOTS + subs)
            even, odd = regroup(total[rows, :width], total[rows, width:])
            out_ref[p * his + x, :, :width] = even.astype(BF)
            out_ref[(p + 1) * his + x, :, :width] = odd.astype(BF)
    out_ref[:, :, width:] = jnp.full((blocks, subs, LANES), peak, F32).astype(BF)


def combine_kernel(res_ref, comb_ref, back_ref, out_ref, peak_ref):
    blocks, subs, width = back_ref.shape
    width = width - LANES
    experts = lax.axis_size("dp")
    his = blocks // experts
    back = back_ref[:, :, :width].reshape(blocks * subs, width)
    for s in range(SPLIT):
        cut = slice(s * width, (s + 1) * width)
        out_ref[:, cut] = (res_ref[:, cut] + dot(comb_ref[s], back)).astype(BF)
    peak = jnp.max(back_ref[pl.ds(lax.axis_index("dp") * his, his), :, width:].astype(F32))
    peak_ref[0] = peak


def call(kernel, mib, ins, outs, scratch=(), flops=0, moved=0):
    places = [SMEM if getattr(o, "memory_space", None) == pltpu.SMEM else VMEM for o in outs]
    return pl.pallas_call(
        kernel,
        out_shape=outs,
        in_specs=[HBM if at == "hbm" else VMEM for at, _ in ins],
        out_specs=places,
        scratch_shapes=scratch,
        compiler_params=pltpu.CompilerParams(vmem_limit_bytes=mib * MIB),
        cost_estimate=pl.CostEstimate(flops=flops, bytes_accessed=moved, transcendentals=0),
    )(*[stay(x)[0] if at == "hbm" else x for at, x in ins])


def near(*arrays):
    return [("vmem", a) for a in arrays]


def far(*arrays):
    return [("hbm", a) for a in arrays]


def on_device(attn_partial, hidden_in, norm_gain, expert_ids, route_prob, w_gate, w_up, w_down):
    experts, his, los = lax.axis_size("dp"), lax.axis_size("hi"), lax.axis_size("lo")
    tokens, cols = hidden_in.shape
    _, units = w_gate.shape[1:]
    width, blocks = cols // SPLIT, experts * his
    slots, rows = experts * EXPERT_SLOTS, experts * SUBLANES
    gain = norm_gain.reshape(1, -1)

    others = [shift(attn_partial[0], "lo", k) for k in range(1, los)]
    own, hidden, pick, comb = call(
        lambda *refs: early_kernel(his, los, *refs),
        4,
        far(attn_partial, hidden_in, expert_ids.T, route_prob.T),
        [
            pltpu.VMEM((his, tokens, cols), BF),
            pltpu.VMEM((tokens, cols), BF),
            pltpu.VMEM((SPLIT, rows, tokens), BF),
            pltpu.VMEM((SPLIT, tokens, blocks * SUBLANES), BF),
        ],
        [
            pltpu.VMEM(expert_ids.shape[::-1], expert_ids.dtype),
            pltpu.VMEM(route_prob.shape[::-1], route_prob.dtype),
            pltpu.SemaphoreType.DMA((2,)),
            pltpu.SemaphoreType.DMA((his + 1,)),
        ],
        moved=2 * MIB,
    )
    sels, rests = call(
        lambda *refs: choose_kernel(los, *refs),
        4,
        near(pick, own, *others),
        [
            pltpu.VMEM((his - 1, rows, width), BF),
            pltpu.VMEM((his - 1, tokens, cols), BF),
        ],
    )
    sels = [shift(sels[k - 1], "hi", k) for k in range(1, his)]
    rests = [shift(rests[k - 1], "hi", k) for k in range(1, his)]
    gain, wg, wu, mine, sel = call(
        lambda *refs: load_kernel(los, *refs),
        4,
        far(gain, w_gate, w_up) + near(hidden, pick, own, *others),
        [
            pltpu.VMEM(gain.shape, F32),
            pltpu.VMEM(w_gate.shape, BF),
            pltpu.VMEM(w_up.shape, BF),
            pltpu.VMEM((tokens, cols), F32),
            pltpu.VMEM((rows, width), F32),
        ],
        [pltpu.SemaphoreType.DMA((3,))],
        moved=8 * MIB,
    )
    (outgoing,) = call(
        lambda *refs: dispatch_kernel(his - 1, *refs),
        4,
        near(sel, *sels),
        [pltpu.VMEM((experts, his, SUBLANES, width), BF)],
    )
    incoming = lax.all_to_all(
        outgoing.reshape(blocks, SUBLANES, width), ("dp", "hi"), 0, 0, tiled=True
    )
    helds = [shift(incoming, "lo", k) for k in range(1, los)]
    wd, *sums = call(
        lambda *refs: first_kernel(los, *refs),
        12,
        near(gain, wg, wu) + far(w_down) + near(incoming),
        [
            pltpu.VMEM(w_down.shape, BF),
            pltpu.VMEM((slots, units), F32),
            pltpu.VMEM((slots, units), F32),
            pltpu.VMEM((slots, LANES), F32),
            pltpu.VMEM((slots, LANES), F32),
        ],
        [pltpu.SemaphoreType.DMA],
        moved=4 * MIB,
    )
    sends, act, peak, top = call(
        lambda *refs: second_kernel(his, los, *refs),
        12,
        near(gain, wg, wu, wd, *sums, *helds),
        [
            pltpu.VMEM((los - 1, slots, his * cols + LANES), BF),
            pltpu.VMEM((slots, units), BF),
            pltpu.VMEM((SUBLANES, LANES), F32),
            pltpu.SMEM((1,), F32),
        ],
    )
    sends = [shift(sends[k - 1], "lo", k) for k in range(1, los)]
    keep, residual = call(
        lambda *refs: third_kernel(his, los, *refs),
        8,
        near(act, wd, mine, *rests),
        [pltpu.VMEM((slots, his * cols), F32), pltpu.VMEM((tokens, cols), F32)],
        moved=2 * MIB,
    )
    (back,) = call(
        lambda *refs: pair_kernel(his, los - 1, *refs),
        4,
        near(keep, peak, *sends),
        [pltpu.VMEM((blocks, SUBLANES, width + LANES), BF)],
    )
    back = lax.all_to_all(back, ("dp", "hi"), 0, 0, tiled=True)
    layer_out, hidden_top = pl.pallas_call(
        combine_kernel,
        out_shape=[
            jax.ShapeDtypeStruct((tokens, cols), BF),
            jax.ShapeDtypeStruct((1,), F32),
        ],
        in_specs=[VMEM] * 3,
        out_specs=[VMEM, SMEM],
        compiler_params=pltpu.CompilerParams(vmem_limit_bytes=4 * MIB),
        name="combine",
    )(residual, comb, back)
    return layer_out, top, hidden_top


def solution(mesh):
    tp = mesh.shape["tp"]
    lo = 2 if tp % 2 == 0 else 1
    split = Mesh(mesh.devices.reshape(mesh.shape["dp"], tp // lo, lo), ("dp", "hi", "lo"))
    tps = ("hi", "lo")
    placed = (
        P(tps, "dp", None),
        P("dp", tps),
        P(),
        P("dp", None),
        P("dp", None),
        P("dp", None, tps),
        P("dp", None, tps),
        P("dp", tps, None),
    )

    return jax.shard_map(
        on_device,
        mesh=split,
        in_specs=placed,
        out_specs=(P("dp", tps), P("dp"), P("dp")),
        check_vma=False,
    )
```

time: 61 us -> 52.7 us (0.86)
  Pallas kernels: 0 us -> 10.2 us
  matrix products: 6.29 us -> 0 us
  other arithmetic: 5.15 us -> 0 us
  local copies, waits for them, and re-layouts: 3.79 us -> 0 us
  between operations: 4.07 us -> 1.21 us
  waiting for transfers between devices: 18.4 us -> 16.8 us
  starting transfers between devices: 7.27 us -> 8.52 us
    pallas_call x0 -> x9, Pallas kernels: none -> 10.2 us  [the longest x8 9.32 us: call(): pl.pallas_call(kernel, out_shape=outs, in_specs=[HBM if at == 'hbm' else...]
    dot_general x5 -> x0, matrix products: 6.29 us -> none  [the longest x1 2.97 us: on_device(): gate_val = jnp.dot(slot_rows, w_gate[0], preferred_element_type=F32)]
    another operation x3 -> x0, other arithmetic: 1.93 us -> none
    slice x6 -> x0, local copies, waits for them, and re-layouts: 1.59 us -> none  [the longest x1 1.18 us: on_device(): hidden_peak = jnp.maximum(hidden_peak, got[0, his * cols].astype(F32))]
    dynamic_slice x2 -> x0, local copies, waits for them, and re-layouts: 1.43 us -> none  [piece(): return lax.dynamic_slice_in_dim(x, (hh * los + ll) * cols, cols, 1)]
    reduce_max x2 -> x0, other arithmetic: 1.38 us -> none  [the longest x1 0.77 us: on_device(): input_peak = jnp.max(jnp.abs(slot_rows.astype(F32)))]
    ppermute x4 -> x5, waiting for transfers between devices: 9.16 us -> 7.8 us  [shift(): return lax.ppermute(x, axis, [(i, (i + by) % n) for i in range(n)])]
    ppermute x4 -> x5, starting transfers between devices: 3.74 us -> 4.98 us  [shift(): return lax.ppermute(x, axis, [(i, (i + by) % n) for i in range(n)])]
  transfers between devices with their start and end apart: 5 -> 6, of which waited for: 5 -> 4; matrix products, arithmetic and copies ran while one was open for 3% -> 0% of each run, Pallas kernels for 0% -> 13%
where the time goes in v2:
time: 52.7 us; the launch traced here: 52.3 us
  waiting for transfers between devices  16.8 us (32%)
  blocking collectives  15.6 us (30%)
  Pallas kernels  10.2 us (19%)
  starting transfers between devices  8.52 us (16%)
  between operations  1.21 us (2%)
    all_to_all x1, blocking collectives, on_device(): lax.all_to_all(outgoing.reshape(blocks, SUBLANES, width), ('dp', 'hi'), 0...  15.6 us
    pallas_call x8, Pallas kernels, call(): pl.pallas_call(kernel, out_shape=outs, in_specs=[HBM if at == 'hbm' else...  9.32 us
    all_to_all x1, waiting for transfers between devices, on_device(): back = lax.all_to_all(back, ('dp', 'hi'), 0, 0, tiled=True)  8.96 us
    ppermute x5, waiting for transfers between devices, shift(): return lax.ppermute(x, axis, [(i, (i + by) % n) for i in range(n)])  7.8 us
    ppermute x5, starting transfers between devices, shift(): return lax.ppermute(x, axis, [(i, (i + by) % n) for i in range(n)])  4.98 us
    all_to_all x1, starting transfers between devices, on_device(): back = lax.all_to_all(back, ('dp', 'hi'), 0, 0, tiled=True)  3.53 us
  transfers between devices with their start and end apart: 6, of which 4 were waited for; matrix products, arithmetic and copies ran while one was open for 0% of the time, Pallas kernels for 13%

profile of v2, /device:TPU:0, one launch (start us, length us, event | category | flops | bytes accessed | tf_op | source)
XLA Modules:
  0.0 52.3 jit_solution(4261144125738564191)
XLA Ops:
  0.6 0.6 %collective-permute-start = (bf16[64,7168]{1,0:T(8,128)(2,1)}, bf16[64,7168]{1,0:T(8,128)(2,1)S(1)}, u32[]{:S(2)}, u32[]{:S(2)}) collective-permute-start(bf16[64,7168]{1,0:T(8,128)(2,1)} %bitcast.12), channel_id=1, source_target_pairs={{0,1},{1,0},{2,3},{3,2},{4,5},{5,4},{6,7},{7,6},{8,9},{9,8},{10,11... | collective-permute-start | bytes 2752520 | tf_op jit(solution)/shard_map/ppermute | solution.py:33
  1.2 1.4 %shard_map.103 = (bf16[2,64,1792]{2,1,0:T(8,128)(2,1)S(1)}, bf16[64,1792]{1,0:T(8,128)(2,1)S(1)}, bf16[2,64,64]{2,1,0:T(8,128)(2,1)S(1)}, bf16[2,64,128]{2,1,0:T(8,128)(2,1)S(1)}) custom-call(bf16[1,64,7168]{2,1,0:T(8,128)(2,1)} %refs_0_.1, bf16[64,1792]{1,0:T(8,128)(2,1)} %refs_1_.2, s32[8,64]{1,0:T(8,128)} %bitcast.14, bf16[8,64]{1,0:T(8,128)(2,1)} %bitcast.15), custom_call_target="tpu_custom_call" | custom-call | bytes 2097152 | tf_op jit(solution)/shard_map/pallas_call | solution.py:287
  2.6 0.9 %collective-permute-done.refs_6_.refs_2_ = bf16[64,7168]{1,0:T(8,128)(2,1)S(1)} collective-permute-done((bf16[64,7168]{1,0:T(8,128)(2,1)}, bf16[64,7168]{1,0:T(8,128)(2,1)S(1)}, u32[]{:S(2)}, u32[]{:S(2)}) %collective-permute-start) | collective-permute-done | bytes 917536 | tf_op jit(solution)/shard_map/ppermute | solution.py:33
  3.5 0.2 shard_map.105
  3.7 2.9 %collective-permute-start.1 = (bf16[64,896]{1,0:T(8,128)(2,1)S(1)}, bf16[64,896]{1,0:T(8,128)(2,1)S(1)}, u32[]{:S(2)}, u32[]{:S(2)}) collective-permute-start(bf16[64,896]{1,0:T(8,128)(2,1)S(1)} %bitcast.11), channel_id=1, source_target_pairs={{0,2},{2,0},{1,3},{3,1},{4,6},{6,4},{5,7},{7,5},{8,10},{10,8},{9,1... | collective-permute-start | bytes 344072 | tf_op jit(solution)/shard_map/ppermute | solution.py:33
  6.6 3.2 %shard_map.104 = (f32[1,7168]{1,0:T(1,128)S(1)}, bf16[1,7168,256]{2,1,0:T(8,128)(2,1)S(1)}, bf16[1,7168,256]{2,1,0:T(8,128)(2,1)S(1)}, f32[64,1792]{1,0:T(8,128)S(1)}, f32[64,896]{1,0:T(8,128)S(1)}) custom-call(f32[1,7168]{1,0:T(1,128)} %bitcast.13, bf16[1,7168,256]{2,1,0:T(8,128)(2,1)} %refs_1_.3, bf16[1,7168,256]{2,1,0:T(8,128)(2,1)} %refs_2_.1, ...), custom_call_target="tpu_custom_call" | custom-call | bytes 8388608 | tf_op jit(solution)/shard_map/pallas_call | solution.py:287
  9.8 0.2 collective-permute-done.1.refs_1_
  10.1 15.6 %all_to_all.10.refs_4_ = bf16[16,8,896]{2,1,0:T(8,128)(2,1)S(1)} all-to-all(bf16[16,8,896]{2,1,0:T(8,128)(2,1)S(1)} %bitcast.8), channel_id=1, replica_groups=mesh['dp'=8,'hi'=2,'lo'=2] {'dp','hi'}, dimensions={0} | all-to-all | bytes 458752 | tf_op jit(solution)/shard_map/all_to_all | solution.py:364
  25.7 0.0 collective-permute-start.2
  25.7 2.1 %shard_map.107 = (bf16[1,256,7168]{2,1,0:T(8,128)(2,1)S(1)}, f32[32,256]{1,0:T(8,128)S(1)}, f32[32,256]{1,0:T(8,128)S(1)}, f32[32,128]{1,0:T(8,128)S(1)}, f32[32,128]{1,0:T(8,128)S(1)}) custom-call(f32[1,7168]{1,0:T(1,128)S(1)} %get-tuple-element.30.refs_0_, bf16[1,7168,256]{2,1,0:T(8,128)(2,1)S(1)} %get-tuple-element.31.refs_1_, ...), custom_call_target="tpu_custom_call" | custom-call | bytes 4194304 | tf_op jit(solution)/shard_map/pallas_call | solution.py:287
  27.8 0.0 collective-permute-done.2.refs_8_
  27.8 1.2 %shard_map.108 = (bf16[1,32,3712]{2,1,0:T(8,128)(2,1)S(1)}, bf16[32,256]{1,0:T(8,128)(2,1)S(1)}, f32[8,128]{1,0:T(8,128)S(1)}, f32[1]{0:T(128)S(4)}) custom-call(f32[1,7168]{1,0:T(1,128)S(1)} %get-tuple-element.30.refs_0_, bf16[1,7168,256]{2,1,0:T(8,128)(2,1)S(1)} %get-tuple-element.31.refs_1_, bf16[1,7168,256]{2,1,0:T(8,128)(2,1)S(1)} %get-tuple-element.32.refs_2_, ...), custom_call_target="tpu_custom_call" | custom-call | tf_op jit(solution)/shard_map/pallas_call | solution.py:287
  29.0 0.5 %collective-permute-start.4 = (bf16[32,3712]{1,0:T(8,128)(2,1)S(1)}, bf16[32,3712]{1,0:T(8,128)(2,1)S(1)}, u32[]{:S(2)}, u32[]{:S(2)}) collective-permute-start(bf16[32,3712]{1,0:T(8,128)(2,1)S(1)} %bitcast.9), channel_id=1, source_target_pairs={{0,1},{1,0},{2,3},{3,2},{4,5},{5,4},{6,7},{7,6},{8,9},{9,8},{10,11... | collective-permute-start | bytes 712712 | tf_op jit(solution)/shard_map/ppermute | solution.py:33
  29.5 1.0 %collective-permute-start.3 = (bf16[64,1792]{1,0:T(8,128)(2,1)S(1)}, bf16[64,1792]{1,0:T(8,128)(2,1)S(1)}, u32[]{:S(2)}, u32[]{:S(2)}) collective-permute-start(bf16[64,1792]{1,0:T(8,128)(2,1)S(1)} %bitcast.10), channel_id=1, source_target_pairs={{0,2},{2,0},{1,3},{3,1},{4,6},{6,4},{5,7},{7,5},{8,10},{10,8},{9,1... | collective-permute-start | bytes 688136 | tf_op jit(solution)/shard_map/ppermute | solution.py:33
  30.5 6.6 %collective-permute-done.3.refs_3_ = bf16[64,1792]{1,0:T(8,128)(2,1)S(1)} collective-permute-done((bf16[64,1792]{1,0:T(8,128)(2,1)S(1)}, bf16[64,1792]{1,0:T(8,128)(2,1)S(1)}, u32[]{:S(2)}, u32[]{:S(2)}) %collective-permute-start.3) | collective-permute-done | bytes 229408 | tf_op jit(solution)/shard_map/ppermute | solution.py:33
  37.1 0.4 shard_map.109
  37.6 0.0 collective-permute-done.4.refs_2_
  37.6 0.8 %shard_map.110 = bf16[16,8,1024]{2,1,0:T(8,128)(2,1)} custom-call(f32[32,3584]{1,0:T(8,128)S(1)} %get-tuple-element.45.refs_0_, f32[8,128]{1,0:T(8,128)S(1)} %get-tuple-element.46.refs_1_, bf16[32,3712]{1,0:T(8,128)(2,1)S(1)} %collective-permute-done.4.refs_2_), custom_call_target="tpu_custom_call" | custom-call | tf_op jit(solution)/shard_map/pallas_call | solution.py:287
  38.4 3.5 %all-to-all-start.1 = ((bf16[16,8,1024]{2,1,0:T(8,128)(2,1)}), bf16[16,8,1024]{2,1,0:T(8,128)(2,1)S(1)}, u32[]{:S(2)}, u32[]{:S(2)}) async-start(bf16[16,8,1024]{2,1,0:T(8,128)(2,1)} %shard_map.110), calls=%async_computation.1 | async-start | bytes 524288 | tf_op jit(solution)/shard_map/all_to_all | solution.py:407
  42.5 9.0 %all-to-all-done.1.back_ref = bf16[16,8,1024]{2,1,0:T(8,128)(2,1)S(1)} async-done(((bf16[16,8,1024]{2,1,0:T(8,128)(2,1)}), bf16[16,8,1024]{2,1,0:T(8,128)(2,1)S(1)}, u32[]{:S(2)}, u32[]{:S(2)}) %all-to-all-start.1) | async-done | bytes 262176 | tf_op jit(solution)/shard_map/all_to_all | solution.py:407
  51.4 0.9 %combine.1 = (bf16[64,1792]{1,0:T(8,128)(2,1)}, f32[1]{0:T(128)}) custom-call(f32[64,1792]{1,0:T(8,128)S(1)} %get-tuple-element.43.res_ref, bf16[2,64,128]{2,1,0:T(8,128)(2,1)S(1)} %get-tuple-element.44.comb_ref, bf16[16,8,1024]{2,1,0:T(8,128)(2,1)S(1)} %all-to-all-done.1.back_ref), custom_call_target="tpu_custom_call" | custom-call | tf_op jit(solution)/shard_map/combine/pallas_call | solution.py:408
  (1 shorter events, 0.0 us)
Async XLA Ops:
  0.6 2.9 %collective-permute-start = (bf16[64,7168]{1,0:T(8,128)(2,1)}, bf16[64,7168]{1,0:T(8,128)(2,1)S(1)}, u32[]{:S(2)}, u32[]{:S(2)}) collective-permute-start(bf16[64,7168]{1,0:T(8,128)(2,1)} %bitcast.12), channel_id=1, source_target_pairs={{0,1},{1,0},{2,3},{3,2},{4,5},{5,4},{6,7},{7,6},{8,9},{9,8},{10,11... | collective-permute-start | bytes 2752520 | tf_op jit(solution)/shard_map/ppermute | solution.py:33
  3.7 6.4 %collective-permute-start.1 = (bf16[64,896]{1,0:T(8,128)(2,1)S(1)}, bf16[64,896]{1,0:T(8,128)(2,1)S(1)}, u32[]{:S(2)}, u32[]{:S(2)}) collective-permute-start(bf16[64,896]{1,0:T(8,128)(2,1)S(1)} %bitcast.11), channel_id=1, source_target_pairs={{0,2},{2,0},{1,3},{3,1},{4,6},{6,4},{5,7},{7,5},{8,10},{10,8},{9,1... | collective-permute-start | bytes 344072 | tf_op jit(solution)/shard_map/ppermute | solution.py:33
  25.7 2.1 %collective-permute-start.2 = (bf16[16,8,896]{2,1,0:T(8,128)(2,1)S(1)}, bf16[16,8,896]{2,1,0:T(8,128)(2,1)S(1)}, u32[]{:S(2)}, u32[]{:S(2)}) collective-permute-start(bf16[16,8,896]{2,1,0:T(8,128)(2,1)S(1)} %all_to_all.10.refs_4_), channel_id=1, source_target_pairs={{0,1},{1,0},{2,3},{3,2},{4,5},{5,4},{6,7},{7,6},{8,9},{9,8},{10,11... | collective-permute-start | bytes 688136 | tf_op jit(solution)/shard_map/ppermute | solution.py:33
  29.0 8.6 %collective-permute-start.4 = (bf16[32,3712]{1,0:T(8,128)(2,1)S(1)}, bf16[32,3712]{1,0:T(8,128)(2,1)S(1)}, u32[]{:S(2)}, u32[]{:S(2)}) collective-permute-start(bf16[32,3712]{1,0:T(8,128)(2,1)S(1)} %bitcast.9), channel_id=1, source_target_pairs={{0,1},{1,0},{2,3},{3,2},{4,5},{5,4},{6,7},{7,6},{8,9},{9,8},{10,11... | collective-permute-start | bytes 712712 | tf_op jit(solution)/shard_map/ppermute | solution.py:33
  29.5 7.6 %collective-permute-start.3 = (bf16[64,1792]{1,0:T(8,128)(2,1)S(1)}, bf16[64,1792]{1,0:T(8,128)(2,1)S(1)}, u32[]{:S(2)}, u32[]{:S(2)}) collective-permute-start(bf16[64,1792]{1,0:T(8,128)(2,1)S(1)} %bitcast.10), channel_id=1, source_target_pairs={{0,2},{2,0},{1,3},{3,1},{4,6},{6,4},{5,7},{7,5},{8,10},{10,8},{9,1... | collective-permute-start | bytes 688136 | tf_op jit(solution)/shard_map/ppermute | solution.py:33
  38.4 13.0 %all-to-all-start.1 = ((bf16[16,8,1024]{2,1,0:T(8,128)(2,1)}), bf16[16,8,1024]{2,1,0:T(8,128)(2,1)S(1)}, u32[]{:S(2)}, u32[]{:S(2)}) async-start(bf16[16,8,1024]{2,1,0:T(8,128)(2,1)} %shard_map.110), calls=%async_computation.1 | async-start | bytes 524288 | tf_op jit(solution)/shard_map/all_to_all | solution.py:407

commit v3 on v2

--- a/solution.py
+++ b/solution.py
@@ -37,8 +37,8 @@
     return [pltpu.with_memory_space_constraint(a, pltpu.HBM) for a in arrays]
 
 
-def early_kernel(his, los, partial_ref, hidden_ref, ids_hbm, prob_hbm, *refs):
-    own_ref, held_ref, pick_ref, comb_ref, ids_ref, prob_ref, small, large = refs
+def early_kernel(his, los, partial_ref, hidden_ref, ids_hbm, prob_hbm, wd_hbm, *refs):
+    own_ref, held_ref, pick_ref, comb_ref, wd_ref, ids_ref, prob_ref, small, large = refs
     cols = hidden_ref.shape[1]
     l = lax.axis_index("lo")
     first = [
@@ -53,6 +53,7 @@
                 partial_ref.at[0, :, pl.ds(at, cols)], own_ref.at[x], large.at[x]
             )
         )
+    rest.append(pltpu.make_async_copy(wd_hbm, wd_ref, large.at[his + 1]))
     for copy in first + rest:
         copy.start()
     for copy in first:
@@ -187,10 +188,8 @@
     return gate, up, square, top
 
 
-def first_kernel(los, gain_ref, wg_ref, wu_ref, wd_hbm, held_ref, *refs):
-    wd_ref, gate_ref, up_ref, square_ref, top_ref, sem = refs
-    copy = pltpu.make_async_copy(wd_hbm, wd_ref, sem)
-    copy.start()
+def first_kernel(los, gain_ref, wg_ref, wu_ref, held_ref, *refs):
+    gate_ref, up_ref, square_ref, top_ref = refs
     slots = gate_ref.shape[0]
     zero, none = jnp.zeros(gate_ref.shape, F32), jnp.zeros((slots, 1), F32)
     gate, up, square, top = products(
@@ -200,7 +199,6 @@
     up_ref[...] = up
     square_ref[...] = jnp.broadcast_to(square, square_ref.shape)
     top_ref[...] = jnp.broadcast_to(top, top_ref.shape)
-    copy.wait()
 
 
 def down(act, wd_ref, his, los, c):
@@ -239,14 +237,9 @@
         send_ref[k - 1, :, -LANES:] = jnp.full((slots, LANES), peak, F32).astype(BF)
 
 
-def third_kernel(his, los, act_ref, wd_ref, mine_ref, *refs):
-    rests, keep_ref, res_ref = refs[: his - 1], refs[his - 1], refs[his]
+def third_kernel(his, los, act_ref, wd_ref, keep_ref):
     for cut, value in down(act_ref[...], wd_ref, his, los, lax.axis_index("lo")):
         keep_ref[:, cut] = value
-    res = mine_ref[...]
-    for rest in rests:
-        res = res + rest[...].astype(F32)
-    res_ref[...] = res
 
 
 def pair_kernel(his, n, keep_ref, peak_ref, *refs):
@@ -269,21 +262,26 @@
     out_ref[:, :, width:] = jnp.full((blocks, subs, LANES), peak, F32).astype(BF)
 
 
-def combine_kernel(res_ref, comb_ref, back_ref, out_ref, peak_ref):
+def peak_kernel(his, back_ref, peak_ref):
+    peak = back_ref[pl.ds(lax.axis_index("dp") * his, his), :, -LANES:]
+    peak_ref[0] = jnp.max(peak.astype(F32))
+
+
+def combine_kernel(mine_ref, comb_ref, back_ref, *refs):
+    rests, out_ref = refs[:-1], refs[-1]
     blocks, subs, width = back_ref.shape
     width = width - LANES
-    experts = lax.axis_size("dp")
-    his = blocks // experts
     back = back_ref[:, :, :width].reshape(blocks * subs, width)
     for s in range(SPLIT):
         cut = slice(s * width, (s + 1) * width)
-        out_ref[:, cut] = (res_ref[:, cut] + dot(comb_ref[s], back)).astype(BF)
-    peak = jnp.max(back_ref[pl.ds(lax.axis_index("dp") * his, his), :, width:].astype(F32))
-    peak_ref[0] = peak
+        res = mine_ref[:, cut]
+        for rest in rests:
+            res = res + rest[:, cut].astype(F32)
+        out_ref[:, cut] = (res + dot(comb_ref[s], back)).astype(BF)
 
 
 def call(kernel, mib, ins, outs, scratch=(), flops=0, moved=0):
-    places = [SMEM if getattr(o, "memory_space", None) == pltpu.SMEM else VMEM for o in outs]
+    places = [SMEM if isinstance(o, jax.ShapeDtypeStruct) else VMEM for o in outs]
     return pl.pallas_call(
         kernel,
         out_shape=outs,
@@ -312,23 +310,24 @@
     gain = norm_gain.reshape(1, -1)
 
     others = [shift(attn_partial[0], "lo", k) for k in range(1, los)]
-    own, hidden, pick, comb = call(
+    own, hidden, pick, comb, wd = call(
         lambda *refs: early_kernel(his, los, *refs),
         4,
-        far(attn_partial, hidden_in, expert_ids.T, route_prob.T),
+        far(attn_partial, hidden_in, expert_ids.T, route_prob.T, w_down),
         [
             pltpu.VMEM((his, tokens, cols), BF),
             pltpu.VMEM((tokens, cols), BF),
             pltpu.VMEM((SPLIT, rows, tokens), BF),
             pltpu.VMEM((SPLIT, tokens, blocks * SUBLANES), BF),
+            pltpu.VMEM(w_down.shape, BF),
         ],
         [
             pltpu.VMEM(expert_ids.shape[::-1], expert_ids.dtype),
             pltpu.VMEM(route_prob.shape[::-1], route_prob.dtype),
             pltpu.SemaphoreType.DMA((2,)),
-            pltpu.SemaphoreType.DMA((his + 1,)),
-        ],
-        moved=2 * MIB,
+            pltpu.SemaphoreType.DMA((his + 2,)),
+        ],
+        moved=6 * MIB,
     )
     sels, rests = call(
         lambda *refs: choose_kernel(los, *refs),
@@ -340,7 +339,6 @@
         ],
     )
     sels = [shift(sels[k - 1], "hi", k) for k in range(1, his)]
-    rests = [shift(rests[k - 1], "hi", k) for k in range(1, his)]
     gain, wg, wu, mine, sel = call(
         lambda *refs: load_kernel(los, *refs),
         4,
@@ -365,18 +363,16 @@
         outgoing.reshape(blocks, SUBLANES, width), ("dp", "hi"), 0, 0, tiled=True
     )
     helds = [shift(incoming, "lo", k) for k in range(1, los)]
-    wd, *sums = call(
+    sums = call(
         lambda *refs: first_kernel(los, *refs),
-        12,
-        near(gain, wg, wu) + far(w_down) + near(incoming),
-        [
-            pltpu.VMEM(w_down.shape, BF),
+        8,
+        near(gain, wg, wu, incoming),
+        [
             pltpu.VMEM((slots, units), F32),
             pltpu.VMEM((slots, units), F32),
             pltpu.VMEM((slots, LANES), F32),
             pltpu.VMEM((slots, LANES), F32),
         ],
-        [pltpu.SemaphoreType.DMA],
         moved=4 * MIB,
     )
     sends, act, peak, top = call(
@@ -387,15 +383,16 @@
             pltpu.VMEM((los - 1, slots, his * cols + LANES), BF),
             pltpu.VMEM((slots, units), BF),
             pltpu.VMEM((SUBLANES, LANES), F32),
-            pltpu.SMEM((1,), F32),
+            jax.ShapeDtypeStruct((1,), F32),
         ],
     )
     sends = [shift(sends[k - 1], "lo", k) for k in range(1, los)]
-    keep, residual = call(
+    rests = [shift(rests[k - 1], "hi", k) for k in range(1, his)]
+    (keep,) = call(
         lambda *refs: third_kernel(his, los, *refs),
         8,
-        near(act, wd, mine, *rests),
-        [pltpu.VMEM((slots, his * cols), F32), pltpu.VMEM((tokens, cols), F32)],
+        near(act, wd),
+        [pltpu.VMEM((slots, his * cols), F32)],
         moved=2 * MIB,
     )
     (back,) = call(
@@ -405,17 +402,20 @@
         [pltpu.VMEM((blocks, SUBLANES, width + LANES), BF)],
     )
     back = lax.all_to_all(back, ("dp", "hi"), 0, 0, tiled=True)
-    layer_out, hidden_top = pl.pallas_call(
+    (hidden_top,) = call(
+        lambda *refs: peak_kernel(his, *refs),
+        1,
+        near(back),
+        [jax.ShapeDtypeStruct((1,), F32)],
+    )
+    layer_out = pl.pallas_call(
         combine_kernel,
-        out_shape=[
-            jax.ShapeDtypeStruct((tokens, cols), BF),
-            jax.ShapeDtypeStruct((1,), F32),
-        ],
-        in_specs=[VMEM] * 3,
-        out_specs=[VMEM, SMEM],
+        out_shape=jax.ShapeDtypeStruct((tokens, cols), BF),
+        in_specs=[VMEM] * (2 + his),
+        out_specs=VMEM,
         compiler_params=pltpu.CompilerParams(vmem_limit_bytes=4 * MIB),
         name="combine",
-    )(residual, comb, back)
+    )(mine, comb, back, *rests)
     return layer_out, top, hidden_top
 
 

time: 52.7 us -> 47.2 us (0.90)
  waiting for transfers between devices: 16.8 us -> 10.7 us
  Pallas kernels: 10.2 us -> 10.8 us
    ppermute x5, waiting for transfers between devices: 7.8 us -> 2.1 us  [shift(): return lax.ppermute(x, axis, [(i, (i + by) % n) for i in range(n)])]
    pallas_call x8 -> x9, Pallas kernels: 9.32 us -> 9.9 us  [call(): pl.pallas_call(kernel, out_shape=outs, in_specs=[HBM if at == 'hbm' else...]
  transfers between devices with their start and end apart: 6 -> 6, of which waited for: 4 -> 4; matrix products, arithmetic and copies ran while one was open for 0% -> 0% of each run, Pallas kernels for 13% -> 16%
where the time goes in v3:
time: 47.2 us; the launch traced here: 46.9 us
  blocking collectives  15.8 us (33%)
  Pallas kernels  10.8 us (23%)
  waiting for transfers between devices  10.7 us (23%)
  starting transfers between devices  8.86 us (19%)
  between operations  0.7 us (1%)
    all_to_all x1, blocking collectives, on_device(): lax.all_to_all(outgoing.reshape(blocks, SUBLANES, width), ('dp', 'hi'), 0...  15.8 us
    pallas_call x9, Pallas kernels, call(): pl.pallas_call(kernel, out_shape=outs, in_specs=[HBM if at == 'hbm' else...  9.9 us
    all_to_all x1, waiting for transfers between devices, on_device(): back = lax.all_to_all(back, ('dp', 'hi'), 0, 0, tiled=True)  8.65 us
    ppermute x5, starting transfers between devices, shift(): return lax.ppermute(x, axis, [(i, (i + by) % n) for i in range(n)])  5.32 us
    all_to_all x1, starting transfers between devices, on_device(): back = lax.all_to_all(back, ('dp', 'hi'), 0, 0, tiled=True)  3.53 us
    ppermute x5, waiting for transfers between devices, shift(): return lax.ppermute(x, axis, [(i, (i + by) % n) for i in range(n)])  2.1 us
  transfers between devices with their start and end apart: 6, of which 4 were waited for; matrix products, arithmetic and copies ran while one was open for 0% of the time, Pallas kernels for 16%

profile of v3, /device:TPU:0, one launch (start us, length us, event | category | flops | bytes accessed | tf_op | source)
XLA Modules:
  0.0 46.9 jit_solution(3447292047784148271)
XLA Ops:
  0.6 0.6 %collective-permute-start = (bf16[64,7168]{1,0:T(8,128)(2,1)}, bf16[64,7168]{1,0:T(8,128)(2,1)S(1)}, u32[]{:S(2)}, u32[]{:S(2)}) collective-permute-start(bf16[64,7168]{1,0:T(8,128)(2,1)} %bitcast.12), channel_id=1, source_target_pairs={{0,1},{1,0},{2,3},{3,2},{4,5},{5,4},{6,7},{7,6},{8,9},{9,8},{10,11... | collective-permute-start | bytes 2752520 | tf_op jit(solution)/shard_map/ppermute | solution.py:33
  1.2 2.5 %shard_map.103 = (bf16[2,64,1792]{2,1,0:T(8,128)(2,1)S(1)}, bf16[64,1792]{1,0:T(8,128)(2,1)S(1)}, bf16[2,64,64]{2,1,0:T(8,128)(2,1)S(1)}, bf16[2,64,128]{2,1,0:T(8,128)(2,1)S(1)}, bf16[1,256,7168]{2,1,0:T(8,128)(2,1)S(1)}) custom-call(bf16[1,64,7168]{2,1,0:T(8,128)(2,1)} %refs_0_.1, bf16[64,1792]{1,0:T(8,128)(2,1)} %refs_1_.2, s32[8,64]{1,0:T(8,128)} %bitcast.14, ...), custom_call_target="tpu_custom_call" | custom-call | bytes 6291456 | tf_op jit(solution)/shard_map/pallas_call | solution.py:285
  3.7 0.0 collective-permute-done.refs_6_.refs_2_
  3.7 0.2 shard_map.105
  3.9 2.7 %collective-permute-start.1 = (bf16[64,896]{1,0:T(8,128)(2,1)S(1)}, bf16[64,896]{1,0:T(8,128)(2,1)S(1)}, u32[]{:S(2)}, u32[]{:S(2)}) collective-permute-start(bf16[64,896]{1,0:T(8,128)(2,1)S(1)} %bitcast.11), channel_id=1, source_target_pairs={{0,2},{2,0},{1,3},{3,1},{4,6},{6,4},{5,7},{7,5},{8,10},{10,8},{9,1... | collective-permute-start | bytes 344072 | tf_op jit(solution)/shard_map/ppermute | solution.py:33
  6.6 3.2 %shard_map.104 = (f32[1,7168]{1,0:T(1,128)S(1)}, bf16[1,7168,256]{2,1,0:T(8,128)(2,1)S(1)}, bf16[1,7168,256]{2,1,0:T(8,128)(2,1)S(1)}, f32[64,1792]{1,0:T(8,128)S(1)}, f32[64,896]{1,0:T(8,128)S(1)}) custom-call(f32[1,7168]{1,0:T(1,128)} %bitcast.13, bf16[1,7168,256]{2,1,0:T(8,128)(2,1)} %refs_1_.3, bf16[1,7168,256]{2,1,0:T(8,128)(2,1)} %refs_2_.1, ...), custom_call_target="tpu_custom_call" | custom-call | bytes 8388608 | tf_op jit(solution)/shard_map/pallas_call | solution.py:285
  9.8 0.4 collective-permute-done.1.refs_1_
  10.3 15.8 %all_to_all.10.refs_3_ = bf16[16,8,896]{2,1,0:T(8,128)(2,1)S(1)} all-to-all(bf16[16,8,896]{2,1,0:T(8,128)(2,1)S(1)} %bitcast.8), channel_id=1, replica_groups=mesh['dp'=8,'hi'=2,'lo'=2] {'dp','hi'}, dimensions={0} | all-to-all | bytes 458752 | tf_op jit(solution)/shard_map/all_to_all | solution.py:362
  26.1 0.0 collective-permute-start.2
  26.1 0.8 %shard_map.107 = (f32[32,256]{1,0:T(8,128)S(1)}, f32[32,256]{1,0:T(8,128)S(1)}, f32[32,128]{1,0:T(8,128)S(1)}, f32[32,128]{1,0:T(8,128)S(1)}) custom-call(f32[1,7168]{1,0:T(1,128)S(1)} %get-tuple-element.28.refs_0_, bf16[1,7168,256]{2,1,0:T(8,128)(2,1)S(1)} %get-tuple-element.29.refs_1_, bf16[1,7168,256]{2,1,0:T(8,128)(2,1)S(1)} %get-tuple-element.30.refs_2_, ...), custom_call_target="tpu_custom_call" | custom-call | bytes 4194304 | tf_op jit(solution)/shard_map/pallas_call | solution.py:285
  26.9 0.7 %collective-permute-done.2.refs_8_ = bf16[16,8,896]{2,1,0:T(8,128)(2,1)S(1)} collective-permute-done((bf16[16,8,896]{2,1,0:T(8,128)(2,1)S(1)}, bf16[16,8,896]{2,1,0:T(8,128)(2,1)S(1)}, u32[]{:S(2)}, u32[]{:S(2)}) %collective-permute-start.2) | collective-permute-done | bytes 229408 | tf_op jit(solution)/shard_map/ppermute | solution.py:33
  27.6 1.3 %shard_map.108 = (bf16[1,32,3712]{2,1,0:T(8,128)(2,1)S(1)}, bf16[32,256]{1,0:T(8,128)(2,1)S(1)}, f32[8,128]{1,0:T(8,128)S(1)}, f32[1]{0:T(128)}) custom-call(f32[1,7168]{1,0:T(1,128)S(1)} %get-tuple-element.28.refs_0_, bf16[1,7168,256]{2,1,0:T(8,128)(2,1)S(1)} %get-tuple-element.29.refs_1_, bf16[1,7168,256]{2,1,0:T(8,128)(2,1)S(1)} %get-tuple-element.30.refs_2_, ...), custom_call_target="tpu_custom_call" | custom-call | tf_op jit(solution)/shard_map/pallas_call | solution.py:285
  28.9 0.2 collective-permute-start.3
  29.1 0.4 shard_map.109.refs_0_
  29.6 0.9 %collective-permute-done.3.refs_2_ = bf16[32,3712]{1,0:T(8,128)(2,1)S(1)} collective-permute-done((bf16[32,3712]{1,0:T(8,128)(2,1)S(1)}, bf16[32,3712]{1,0:T(8,128)(2,1)S(1)}, u32[]{:S(2)}, u32[]{:S(2)}) %collective-permute-start.3) | collective-permute-done | bytes 237600 | tf_op jit(solution)/shard_map/ppermute | solution.py:33
  30.5 0.8 %shard_map.110 = bf16[16,8,1024]{2,1,0:T(8,128)(2,1)} custom-call(f32[32,3584]{1,0:T(8,128)S(1)} %shard_map.109.refs_0_, f32[8,128]{1,0:T(8,128)S(1)} %get-tuple-element.39.refs_1_, bf16[32,3712]{1,0:T(8,128)(2,1)S(1)} %collective-permute-done.3.refs_2_), custom_call_target="tpu_custom_call" | custom-call | tf_op jit(solution)/shard_map/pallas_call | solution.py:285
  31.3 3.5 %all-to-all-start.1 = ((bf16[16,8,1024]{2,1,0:T(8,128)(2,1)}), bf16[16,8,1024]{2,1,0:T(8,128)(2,1)S(1)}, u32[]{:S(2)}, u32[]{:S(2)}) async-start(bf16[16,8,1024]{2,1,0:T(8,128)(2,1)} %shard_map.110), calls=%async_computation.1 | async-start | bytes 524288 | tf_op jit(solution)/shard_map/all_to_all | solution.py:404
  34.9 1.9 %collective-permute-start.4 = (bf16[64,1792]{1,0:T(8,128)(2,1)S(1)}, bf16[64,1792]{1,0:T(8,128)(2,1)S(1)}, u32[]{:S(2)}, u32[]{:S(2)}) collective-permute-start(bf16[64,1792]{1,0:T(8,128)(2,1)S(1)} %bitcast.10), channel_id=1, source_target_pairs={{0,2},{2,0},{1,3},{3,1},{4,6},{6,4},{5,7},{7,5},{8,10},{10,8},{9,1... | collective-permute-start | bytes 688136 | tf_op jit(solution)/shard_map/ppermute | solution.py:33
  36.7 8.6 %all-to-all-done.1.back_ref.refs_0_ = bf16[16,8,1024]{2,1,0:T(8,128)(2,1)S(1)} async-done(((bf16[16,8,1024]{2,1,0:T(8,128)(2,1)}), bf16[16,8,1024]{2,1,0:T(8,128)(2,1)S(1)}, u32[]{:S(2)}, u32[]{:S(2)}) %all-to-all-start.1) | async-done | bytes 262176 | tf_op jit(solution)/shard_map/all_to_all | solution.py:404
  45.4 0.6 %shard_map.111 = f32[1]{0:T(128)} custom-call(bf16[16,8,1024]{2,1,0:T(8,128)(2,1)S(1)} %all-to-all-done.1.back_ref.refs_0_), custom_call_target="tpu_custom_call" | custom-call | tf_op jit(solution)/shard_map/pallas_call | solution.py:285
  46.0 0.0 collective-permute-done.4.refs_0_
  46.0 0.9 %combine.1 = bf16[64,1792]{1,0:T(8,128)(2,1)} custom-call(f32[64,1792]{1,0:T(8,128)S(1)} %get-tuple-element.26.mine_ref, bf16[2,64,128]{2,1,0:T(8,128)(2,1)S(1)} %get-tuple-element.27.comb_ref, bf16[16,8,1024]{2,1,0:T(8,128)(2,1)S(1)} %all-to-all-done.1.back_ref.refs_0_, bf16[64,1792]{1,0:T(8,128)(2,1)S(1)} %collective-permute-done.4.refs_0_), custom_call_target="tpu_custom_call" | custom-call | tf_op jit(solution)/shard_map/combine/pallas_call | solution.py:411
  (1 shorter events, 0.0 us)
Async XLA Ops:
  0.6 3.0 %collective-permute-start = (bf16[64,7168]{1,0:T(8,128)(2,1)}, bf16[64,7168]{1,0:T(8,128)(2,1)S(1)}, u32[]{:S(2)}, u32[]{:S(2)}) collective-permute-start(bf16[64,7168]{1,0:T(8,128)(2,1)} %bitcast.12), channel_id=1, source_target_pairs={{0,1},{1,0},{2,3},{3,2},{4,5},{5,4},{6,7},{7,6},{8,9},{9,8},{10,11... | collective-permute-start | bytes 2752520 | tf_op jit(solution)/shard_map/ppermute | solution.py:33
  3.9 6.4 %collective-permute-start.1 = (bf16[64,896]{1,0:T(8,128)(2,1)S(1)}, bf16[64,896]{1,0:T(8,128)(2,1)S(1)}, u32[]{:S(2)}, u32[]{:S(2)}) collective-permute-start(bf16[64,896]{1,0:T(8,128)(2,1)S(1)} %bitcast.11), channel_id=1, source_target_pairs={{0,2},{2,0},{1,3},{3,1},{4,6},{6,4},{5,7},{7,5},{8,10},{10,8},{9,1... | collective-permute-start | bytes 344072 | tf_op jit(solution)/shard_map/ppermute | solution.py:33
  26.1 1.5 %collective-permute-start.2 = (bf16[16,8,896]{2,1,0:T(8,128)(2,1)S(1)}, bf16[16,8,896]{2,1,0:T(8,128)(2,1)S(1)}, u32[]{:S(2)}, u32[]{:S(2)}) collective-permute-start(bf16[16,8,896]{2,1,0:T(8,128)(2,1)S(1)} %all_to_all.10.refs_3_), channel_id=1, source_target_pairs={{0,1},{1,0},{2,3},{3,2},{4,5},{5,4},{6,7},{7,6},{8,9},{9,8},{10,11... | collective-permute-start | bytes 688136 | tf_op jit(solution)/shard_map/ppermute | solution.py:33
  28.9 1.6 %collective-permute-start.3 = (bf16[32,3712]{1,0:T(8,128)(2,1)S(1)}, bf16[32,3712]{1,0:T(8,128)(2,1)S(1)}, u32[]{:S(2)}, u32[]{:S(2)}) collective-permute-start(bf16[32,3712]{1,0:T(8,128)(2,1)S(1)} %bitcast.9), channel_id=1, source_target_pairs={{0,1},{1,0},{2,3},{3,2},{4,5},{5,4},{6,7},{7,6},{8,9},{9,8},{10,11... | collective-permute-start | bytes 712712 | tf_op jit(solution)/shard_map/ppermute | solution.py:33
  31.3 14.0 %all-to-all-start.1 = ((bf16[16,8,1024]{2,1,0:T(8,128)(2,1)}), bf16[16,8,1024]{2,1,0:T(8,128)(2,1)S(1)}, u32[]{:S(2)}, u32[]{:S(2)}) async-start(bf16[16,8,1024]{2,1,0:T(8,128)(2,1)} %shard_map.110), calls=%async_computation.1 | async-start | bytes 524288 | tf_op jit(solution)/shard_map/all_to_all | solution.py:404
  34.9 11.1 %collective-permute-start.4 = (bf16[64,1792]{1,0:T(8,128)(2,1)S(1)}, bf16[64,1792]{1,0:T(8,128)(2,1)S(1)}, u32[]{:S(2)}, u32[]{:S(2)}) collective-permute-start(bf16[64,1792]{1,0:T(8,128)(2,1)S(1)} %bitcast.10), channel_id=1, source_target_pairs={{0,2},{2,0},{1,3},{3,1},{4,6},{6,4},{5,7},{7,5},{8,10},{10,8},{9,1... | collective-permute-start | bytes 688136 | tf_op jit(solution)/shard_map/ppermute | solution.py:33

commit v4 on v3

--- a/solution.py
+++ b/solution.py
@@ -37,8 +37,26 @@
     return [pltpu.with_memory_space_constraint(a, pltpu.HBM) for a in arrays]
 
 
-def early_kernel(his, los, partial_ref, hidden_ref, ids_hbm, prob_hbm, wd_hbm, *refs):
-    own_ref, held_ref, pick_ref, comb_ref, wd_ref, ids_ref, prob_ref, small, large = refs
+def cut_kernel(his, los, partial_ref, out_ref, sems):
+    cols = out_ref.shape[3]
+    l = lax.axis_index("lo")
+    copies = []
+    for k in range(1, los):
+        for x in range(his):
+            at = pl.multiple_of((x * los + lax.rem(l + k, los)) * cols, LANES)
+            copies.append(
+                pltpu.make_async_copy(
+                    partial_ref.at[0, :, pl.ds(at, cols)], out_ref.at[k - 1, x], sems.at[k - 1, x]
+                )
+            )
+    for copy in copies:
+        copy.start()
+    for copy in copies:
+        copy.wait()
+
+
+def early_kernel(his, los, partial_ref, hidden_ref, ids_hbm, prob_hbm, *refs):
+    own_ref, held_ref, pick_ref, comb_ref, ids_ref, prob_ref, small, large = refs
     cols = hidden_ref.shape[1]
     l = lax.axis_index("lo")
     first = [
@@ -53,7 +71,6 @@
                 partial_ref.at[0, :, pl.ds(at, cols)], own_ref.at[x], large.at[x]
             )
         )
-    rest.append(pltpu.make_async_copy(wd_hbm, wd_ref, large.at[his + 1]))
     for copy in first + rest:
         copy.start()
     for copy in first:
@@ -94,13 +111,12 @@
     others, sel_ref, res_ref = refs[: los - 1], refs[los - 1], refs[los]
     his, _, cols = own_ref.shape
     width = cols // SPLIT
-    h, l = lax.axis_index("hi"), lax.axis_index("lo")
+    h = lax.axis_index("hi")
     for k in range(1, his):
         hh = lax.rem(h + k, his)
         pair = own_ref[hh].astype(F32)
-        at = pl.multiple_of((hh * los + l) * cols, LANES)
         for other in others:
-            pair = pair + other[:, pl.ds(at, cols)].astype(F32)
+            pair = pair + other[hh].astype(F32)
         pair = pair.astype(BF)
         res_ref[k - 1] = pair
         chosen = dot(pick_ref[0], pair[:, :width])
@@ -110,23 +126,20 @@
 
 
 def load_kernel(los, *refs):
-    gain_hbm, wg_hbm, wu_hbm, hidden_ref, pick_ref, own_ref = refs[:6]
-    others = refs[6 : 5 + los]
-    gain_ref, wg_ref, wu_ref, mine_ref, sel_ref, sems = refs[5 + los :]
+    hbms, (hidden_ref, pick_ref, own_ref) = refs[:4], refs[4:7]
+    others, (mine_ref, sel_ref), sems = refs[7 : 6 + los], refs[10 + los : 12 + los], refs[-1]
     copies = [
-        pltpu.make_async_copy(wg_hbm, wg_ref, sems.at[0]),
-        pltpu.make_async_copy(wu_hbm, wu_ref, sems.at[1]),
-        pltpu.make_async_copy(gain_hbm, gain_ref, sems.at[2]),
+        pltpu.make_async_copy(hbm, vmem, sems.at[i])
+        for i, (hbm, vmem) in enumerate(zip(hbms, refs[6 + los : 10 + los]))
     ]
     for copy in copies:
         copy.start()
-    _, cols = hidden_ref.shape
+    cols = hidden_ref.shape[1]
     width = cols // SPLIT
-    h, l = lax.axis_index("hi"), lax.axis_index("lo")
+    h = lax.axis_index("hi")
     mine = hidden_ref[...].astype(F32) + own_ref[h].astype(F32)
-    at = pl.multiple_of((h * los + l) * cols, LANES)
     for other in others:
-        mine = mine + other[:, pl.ds(at, cols)].astype(F32)
+        mine = mine + other[h].astype(F32)
     mine_ref[...] = mine
     chosen = dot(pick_ref[0].astype(F32), mine[:, :width], HIGHEST)
     for s in range(1, SPLIT):
@@ -263,21 +276,27 @@
 
 
 def peak_kernel(his, back_ref, peak_ref):
-    peak = back_ref[pl.ds(lax.axis_index("dp") * his, his), :, -LANES:]
-    peak_ref[0] = jnp.max(peak.astype(F32))
-
-
-def combine_kernel(mine_ref, comb_ref, back_ref, *refs):
-    rests, out_ref = refs[:-1], refs[-1]
+    peak = back_ref[pl.ds(lax.axis_index("dp") * his, his), :, -LANES:].astype(F32)
+    peak_ref[...] = jnp.max(peak, axis=0)
+
+
+def combine_kernel(mine_ref, comb_ref, back_ref, tile_ref, *refs):
+    rests, (out_hbm, peak_ref, out_ref, sems) = refs[:-4], refs[-4:]
     blocks, subs, width = back_ref.shape
     width = width - LANES
     back = back_ref[:, :, :width].reshape(blocks * subs, width)
+    copies = []
     for s in range(SPLIT):
         cut = slice(s * width, (s + 1) * width)
         res = mine_ref[:, cut]
         for rest in rests:
             res = res + rest[:, cut].astype(F32)
         out_ref[:, cut] = (res + dot(comb_ref[s], back)).astype(BF)
+        copies.append(pltpu.make_async_copy(out_ref.at[:, cut], out_hbm.at[:, cut], sems.at[s]))
+        copies[-1].start()
+    peak_ref[0] = jnp.max(tile_ref[...])
+    for copy in copies:
+        copy.wait()
 
 
 def call(kernel, mib, ins, outs, scratch=(), flops=0, moved=0):
@@ -309,25 +328,31 @@
     slots, rows = experts * EXPERT_SLOTS, experts * SUBLANES
     gain = norm_gain.reshape(1, -1)
 
-    others = [shift(attn_partial[0], "lo", k) for k in range(1, los)]
-    own, hidden, pick, comb, wd = call(
+    (cut,) = call(
+        lambda *refs: cut_kernel(his, los, *refs),
+        1,
+        far(attn_partial),
+        [pltpu.VMEM((los - 1, his, tokens, cols), BF)],
+        [pltpu.SemaphoreType.DMA((los - 1, his))],
+    )
+    others = [shift(cut[k - 1], "lo", k) for k in range(1, los)]
+    own, hidden, pick, comb = call(
         lambda *refs: early_kernel(his, los, *refs),
         4,
-        far(attn_partial, hidden_in, expert_ids.T, route_prob.T, w_down),
+        far(attn_partial, hidden_in, expert_ids.T, route_prob.T),
         [
             pltpu.VMEM((his, tokens, cols), BF),
             pltpu.VMEM((tokens, cols), BF),
             pltpu.VMEM((SPLIT, rows, tokens), BF),
             pltpu.VMEM((SPLIT, tokens, blocks * SUBLANES), BF),
-            pltpu.VMEM(w_down.shape, BF),
         ],
         [
             pltpu.VMEM(expert_ids.shape[::-1], expert_ids.dtype),
             pltpu.VMEM(route_prob.shape[::-1], route_prob.dtype),
             pltpu.SemaphoreType.DMA((2,)),
-            pltpu.SemaphoreType.DMA((his + 2,)),
-        ],
-        moved=6 * MIB,
+            pltpu.SemaphoreType.DMA((his + 1,)),
+        ],
+        moved=MIB,
     )
     sels, rests = call(
         lambda *refs: choose_kernel(los, *refs),
@@ -339,20 +364,22 @@
         ],
     )
     sels = [shift(sels[k - 1], "hi", k) for k in range(1, his)]
-    gain, wg, wu, mine, sel = call(
+    gain, wg, wu, wd, mine, sel = call(
         lambda *refs: load_kernel(los, *refs),
         4,
-        far(gain, w_gate, w_up) + near(hidden, pick, own, *others),
+        far(gain, w_gate, w_up, w_down) + near(hidden, pick, own, *others),
         [
             pltpu.VMEM(gain.shape, F32),
             pltpu.VMEM(w_gate.shape, BF),
             pltpu.VMEM(w_up.shape, BF),
+            pltpu.VMEM(w_down.shape, BF),
             pltpu.VMEM((tokens, cols), F32),
             pltpu.VMEM((rows, width), F32),
         ],
-        [pltpu.SemaphoreType.DMA((3,))],
-        moved=8 * MIB,
-    )
+        [pltpu.SemaphoreType.DMA((4,))],
+        moved=12 * MIB,
+    )
+    rests = [shift(rests[k - 1], "hi", k) for k in range(1, his)]
     (outgoing,) = call(
         lambda *refs: dispatch_kernel(his - 1, *refs),
         4,
@@ -387,7 +414,6 @@
         ],
     )
     sends = [shift(sends[k - 1], "lo", k) for k in range(1, los)]
-    rests = [shift(rests[k - 1], "hi", k) for k in range(1, his)]
     (keep,) = call(
         lambda *refs: third_kernel(his, los, *refs),
         8,
@@ -402,20 +428,21 @@
         [pltpu.VMEM((blocks, SUBLANES, width + LANES), BF)],
     )
     back = lax.all_to_all(back, ("dp", "hi"), 0, 0, tiled=True)
-    (hidden_top,) = call(
-        lambda *refs: peak_kernel(his, *refs),
-        1,
-        near(back),
-        [jax.ShapeDtypeStruct((1,), F32)],
-    )
-    layer_out = pl.pallas_call(
+    (tile,) = call(
+        lambda *refs: peak_kernel(his, *refs), 1, near(back), [pltpu.VMEM((SUBLANES, LANES), F32)]
+    )
+    layer_out, hidden_top = pl.pallas_call(
         combine_kernel,
-        out_shape=jax.ShapeDtypeStruct((tokens, cols), BF),
-        in_specs=[VMEM] * (2 + his),
-        out_specs=VMEM,
+        out_shape=[
+            jax.ShapeDtypeStruct((tokens, cols), BF),
+            jax.ShapeDtypeStruct((1,), F32),
+        ],
+        in_specs=[VMEM] * (3 + his),
+        out_specs=[HBM, SMEM],
+        scratch_shapes=[pltpu.VMEM((tokens, cols), BF), pltpu.SemaphoreType.DMA((SPLIT,))],
         compiler_params=pltpu.CompilerParams(vmem_limit_bytes=4 * MIB),
         name="combine",
-    )(mine, comb, back, *rests)
+    )(mine, comb, back, tile, *rests)
     return layer_out, top, hidden_top
 
 

time: 47.2 us -> 47.1 us (level)
  blocking collectives: 15.8 us -> 15 us
  Pallas kernels: 10.8 us -> 11.6 us
    all_to_all x1, blocking collectives: 15.8 us -> 15 us  [on_device(): lax.all_to_all(outgoing.reshape(blocks, SUBLANES, width), ('dp', 'hi'), 0...]
    pallas_call x1, Pallas kernels: 0.91 us -> 1.4 us  [on_device(): pl.pallas_call(combine_kernel, out_shape=[jax.ShapeDtypeStruct((tokens, c...]
    pallas_call x9 -> x10, Pallas kernels: 9.9 us -> 10.2 us  [call(): pl.pallas_call(kernel, out_shape=outs, in_specs=[HBM if at == 'hbm' else...]
  transfers between devices with their start and end apart: 6 -> 6, of which waited for: 4 -> 4; matrix products, arithmetic and copies ran while one was open for 0% -> 0% of each run, Pallas kernels for 16% -> 15%
where the time goes in v4:
time: 47.1 us; the launch traced here: 46.8 us
  blocking collectives  15 us (32%)
  Pallas kernels  11.6 us (25%)
  waiting for transfers between devices  10.4 us (22%)
  starting transfers between devices  9.06 us (19%)
  between operations  0.69 us (1%)
    all_to_all x1, blocking collectives, on_device(): lax.all_to_all(outgoing.reshape(blocks, SUBLANES, width), ('dp', 'hi'), 0...  15 us
    pallas_call x10, Pallas kernels, call(): pl.pallas_call(kernel, out_shape=outs, in_specs=[HBM if at == 'hbm' else...  10.2 us
    all_to_all x1, waiting for transfers between devices, on_device(): back = lax.all_to_all(back, ('dp', 'hi'), 0, 0, tiled=True)  8.65 us
    ppermute x5, starting transfers between devices, shift(): return lax.ppermute(x, axis, [(i, (i + by) % n) for i in range(n)])  5.53 us
    all_to_all x1, starting transfers between devices, on_device(): back = lax.all_to_all(back, ('dp', 'hi'), 0, 0, tiled=True)  3.53 us
    ppermute x5, waiting for transfers between devices, shift(): return lax.ppermute(x, axis, [(i, (i + by) % n) for i in range(n)])  1.74 us
    pallas_call x1, Pallas kernels, on_device(): pl.pallas_call(combine_kernel, out_shape=[jax.ShapeDtypeStruct((tokens, c...  1.4 us
  transfers between devices with their start and end apart: 6, of which 4 were waited for; matrix products, arithmetic and copies ran while one was open for 0% of the time, Pallas kernels for 15%

profile of v4, /device:TPU:0, one launch (start us, length us, event | category | flops | bytes accessed | tf_op | source)
XLA Modules:
  0.0 46.8 jit_solution(15269304581307338436)
XLA Ops:
  0.6 1.1 %shard_map.104 = bf16[1,2,64,1792]{3,2,1,0:T(8,128)(2,1)S(1)} custom-call(bf16[1,64,7168]{2,1,0:T(8,128)(2,1)} %refs_0_.3), custom_call_target="tpu_custom_call" | custom-call | tf_op jit(solution)/shard_map/pallas_call | solution.py:304
  1.7 0.6 %collective-permute-start = (bf16[2,64,1792]{2,1,0:T(8,128)(2,1)S(1)}, bf16[2,64,1792]{2,1,0:T(8,128)(2,1)S(1)}, u32[]{:S(2)}, u32[]{:S(2)}) collective-permute-start(bf16[2,64,1792]{2,1,0:T(8,128)(2,1)S(1)} %bitcast.9), channel_id=1, source_target_pairs={{0,1},{1,0},{2,3},{3,2},{4,5},{5,4},{6,7},{7,6},{8,9},{9,8},{10,11... | collective-permute-start | bytes 1376264 | tf_op jit(solution)/shard_map/ppermute | solution.py:33
  2.3 1.4 %shard_map.103 = (bf16[2,64,1792]{2,1,0:T(8,128)(2,1)S(1)}, bf16[64,1792]{1,0:T(8,128)(2,1)S(1)}, bf16[2,64,64]{2,1,0:T(8,128)(2,1)S(1)}, bf16[2,64,128]{2,1,0:T(8,128)(2,1)S(1)}) custom-call(bf16[1,64,7168]{2,1,0:T(8,128)(2,1)} %refs_0_.3, bf16[64,1792]{1,0:T(8,128)(2,1)} %refs_1_.2, s32[8,64]{1,0:T(8,128)} %bitcast.14, bf16[8,64]{1,0:T(8,128)(2,1)} %bitcast.15), custom_call_target="tpu_custom_call" | custom-call | bytes 1048576 | tf_op jit(solution)/shard_map/pallas_call | solution.py:304
  3.6 0.1 collective-permute-done.refs_7_.refs_2_
  3.7 0.2 shard_map.106
  3.9 2.9 %collective-permute-start.1 = (bf16[64,896]{1,0:T(8,128)(2,1)S(1)}, bf16[64,896]{1,0:T(8,128)(2,1)S(1)}, u32[]{:S(2)}, u32[]{:S(2)}) collective-permute-start(bf16[64,896]{1,0:T(8,128)(2,1)S(1)} %bitcast.12), channel_id=1, source_target_pairs={{0,2},{2,0},{1,3},{3,1},{4,6},{6,4},{5,7},{7,5},{8,10},{10,8},{9,1... | collective-permute-start | bytes 344072 | tf_op jit(solution)/shard_map/ppermute | solution.py:33
  6.8 4.3 %shard_map.105 = (f32[1,7168]{1,0:T(1,128)S(1)}, bf16[1,7168,256]{2,1,0:T(8,128)(2,1)S(1)}, bf16[1,7168,256]{2,1,0:T(8,128)(2,1)S(1)}, bf16[1,256,7168]{2,1,0:T(...) custom-call(f32[1,7168]{1,0:T(1,128)} %bitcast.13, bf16[1,7168,256]{2,1,0:T(8,128)(2,1)} %refs_1_.3, ...), custom_call_target="tpu_custom_call" | custom-call | bytes 12582912 | tf_op jit(solution)/shard_map/pallas_call | solution.py:304
  11.1 0.0 collective-permute-done.1.refs_1_
  11.2 15.0 %all_to_all.10.refs_3_ = bf16[16,8,896]{2,1,0:T(8,128)(2,1)S(1)} all-to-all(bf16[16,8,896]{2,1,0:T(8,128)(2,1)S(1)} %bitcast.8), channel_id=1, replica_groups=mesh['dp'=8,'hi'=2,'lo'=2] {'dp','hi'}, dimensions={0} | all-to-all | bytes 458752 | tf_op jit(solution)/shard_map/all_to_all | solution.py:389
  26.2 0.0 collective-permute-start.2
  26.2 0.8 %shard_map.108 = (f32[32,256]{1,0:T(8,128)S(1)}, f32[32,256]{1,0:T(8,128)S(1)}, f32[32,128]{1,0:T(8,128)S(1)}, f32[32,128]{1,0:T(8,128)S(1)}) custom-call(f32[1,7168]{1,0:T(1,128)S(1)} %get-tuple-element.30.refs_0_, bf16[1,7168,256]{2,1,0:T(8,128)(2,1)S(1)} %get-tuple-element.31.refs_1_, bf16[1,7168,256]{2,1,0:T(8,128)(2,1)S(1)} %get-tuple-element.32.refs_2_, ...), custom_call_target="tpu_custom_call" | custom-call | bytes 4194304 | tf_op jit(solution)/shard_map/pallas_call | solution.py:304
  26.9 0.7 %collective-permute-done.2.refs_8_ = bf16[16,8,896]{2,1,0:T(8,128)(2,1)S(1)} collective-permute-done((bf16[16,8,896]{2,1,0:T(8,128)(2,1)S(1)}, bf16[16,8,896]{2,1,0:T(8,128)(2,1)S(1)}, u32[]{:S(2)}, u32[]{:S(2)}) %collective-permute-start.2) | collective-permute-done | bytes 229408 | tf_op jit(solution)/shard_map/ppermute | solution.py:33
  27.7 1.3 %shard_map.109 = (bf16[1,32,3712]{2,1,0:T(8,128)(2,1)S(1)}, bf16[32,256]{1,0:T(8,128)(2,1)S(1)}, f32[8,128]{1,0:T(8,128)S(1)}, f32[1]{0:T(128)}) custom-call(f32[1,7168]{1,0:T(1,128)S(1)} %get-tuple-element.30.refs_0_, bf16[1,7168,256]{2,1,0:T(8,128)(2,1)S(1)} %get-tuple-element.31.refs_1_, bf16[1,7168,256]{2,1,0:T(8,128)(2,1)S(1)} %get-tuple-element.32.refs_2_, ...), custom_call_target="tpu_custom_call" | custom-call | tf_op jit(solution)/shard_map/pallas_call | solution.py:304
  29.0 0.2 collective-permute-start.3
  29.2 0.4 shard_map.110.refs_0_
  29.6 0.9 %collective-permute-done.3.refs_2_ = bf16[32,3712]{1,0:T(8,128)(2,1)S(1)} collective-permute-done((bf16[32,3712]{1,0:T(8,128)(2,1)S(1)}, bf16[32,3712]{1,0:T(8,128)(2,1)S(1)}, u32[]{:S(2)}, u32[]{:S(2)}) %collective-permute-start.3) | collective-permute-done | bytes 237600 | tf_op jit(solution)/shard_map/ppermute | solution.py:33
  30.5 0.8 %shard_map.111 = bf16[16,8,1024]{2,1,0:T(8,128)(2,1)} custom-call(f32[32,3584]{1,0:T(8,128)S(1)} %shard_map.110.refs_0_, f32[8,128]{1,0:T(8,128)S(1)} %get-tuple-element.41.refs_1_, bf16[32,3712]{1,0:T(8,128)(2,1)S(1)} %collective-permute-done.3.refs_2_), custom_call_target="tpu_custom_call" | custom-call | tf_op jit(solution)/shard_map/pallas_call | solution.py:304
  31.4 3.5 %all-to-all-start.1 = ((bf16[16,8,1024]{2,1,0:T(8,128)(2,1)}), bf16[16,8,1024]{2,1,0:T(8,128)(2,1)S(1)}, u32[]{:S(2)}, u32[]{:S(2)}) async-start(bf16[16,8,1024]{2,1,0:T(8,128)(2,1)} %shard_map.111), calls=%async_computation.1 | async-start | bytes 524288 | tf_op jit(solution)/shard_map/all_to_all | solution.py:430
  34.9 1.9 %collective-permute-start.4 = (bf16[64,1792]{1,0:T(8,128)(2,1)S(1)}, bf16[64,1792]{1,0:T(8,128)(2,1)S(1)}, u32[]{:S(2)}, u32[]{:S(2)}) collective-permute-start(bf16[64,1792]{1,0:T(8,128)(2,1)S(1)} %bitcast.11), channel_id=1, source_target_pairs={{0,2},{2,0},{1,3},{3,1},{4,6},{6,4},{5,7},{7,5},{8,10},{10,8},{9,1... | collective-permute-start | bytes 688136 | tf_op jit(solution)/shard_map/ppermute | solution.py:33
  36.7 8.6 %all-to-all-done.1.refs_0_.back_ref = bf16[16,8,1024]{2,1,0:T(8,128)(2,1)S(1)} async-done(((bf16[16,8,1024]{2,1,0:T(8,128)(2,1)}), bf16[16,8,1024]{2,1,0:T(8,128)(2,1)S(1)}, u32[]{:S(2)}, u32[]{:S(2)}) %all-to-all-start.1) | async-done | bytes 262176 | tf_op jit(solution)/shard_map/all_to_all | solution.py:430
  45.4 0.0 collective-permute-done.4.refs_0_
  45.4 1.4 %combine.1 = (bf16[64,1792]{1,0:T(8,128)(2,1)}, f32[1]{0:T(128)}) custom-call(f32[64,1792]{1,0:T(8,128)S(1)} %get-tuple-element.28.mine_ref, bf16[2,64,128]{2,1,0:T(8,128)(2,1)S(1)} %get-tuple-element.29.comb_ref, bf16[16,8,1024]{2,1,0:T(8,128)(2,1)S(1)} %all-to-all-done.1.refs_0_.back_ref, f32[8,128]{1,0:T(8,128)S(1)} %shard_map.112.tile_ref, ...), custom_call_target="tpu_custom_call" | custom-call | tf_op jit(solution)/shard_map/combine/pallas_call | solution.py:434
  (2 shorter events, 0.0 us)
Async XLA Ops:
  1.7 2.0 %collective-permute-start = (bf16[2,64,1792]{2,1,0:T(8,128)(2,1)S(1)}, bf16[2,64,1792]{2,1,0:T(8,128)(2,1)S(1)}, u32[]{:S(2)}, u32[]{:S(2)}) collective-permute-start(bf16[2,64,1792]{2,1,0:T(8,128)(2,1)S(1)} %bitcast.9), channel_id=1, source_target_pairs={{0,1},{1,0},{2,3},{3,2},{4,5},{5,4},{6,7},{7,6},{8,9},{9,8},{10,11... | collective-permute-start | bytes 1376264 | tf_op jit(solution)/shard_map/ppermute | solution.py:33
  3.9 7.2 %collective-permute-start.1 = (bf16[64,896]{1,0:T(8,128)(2,1)S(1)}, bf16[64,896]{1,0:T(8,128)(2,1)S(1)}, u32[]{:S(2)}, u32[]{:S(2)}) collective-permute-start(bf16[64,896]{1,0:T(8,128)(2,1)S(1)} %bitcast.12), channel_id=1, source_target_pairs={{0,2},{2,0},{1,3},{3,1},{4,6},{6,4},{5,7},{7,5},{8,10},{10,8},{9,1... | collective-permute-start | bytes 344072 | tf_op jit(solution)/shard_map/ppermute | solution.py:33
  26.2 1.5 %collective-permute-start.2 = (bf16[16,8,896]{2,1,0:T(8,128)(2,1)S(1)}, bf16[16,8,896]{2,1,0:T(8,128)(2,1)S(1)}, u32[]{:S(2)}, u32[]{:S(2)}) collective-permute-start(bf16[16,8,896]{2,1,0:T(8,128)(2,1)S(1)} %all_to_all.10.refs_3_), channel_id=1, source_target_pairs={{0,1},{1,0},{2,3},{3,2},{4,5},{5,4},{6,7},{7,6},{8,9},{9,8},{10,11... | collective-permute-start | bytes 688136 | tf_op jit(solution)/shard_map/ppermute | solution.py:33
  29.0 1.6 %collective-permute-start.3 = (bf16[32,3712]{1,0:T(8,128)(2,1)S(1)}, bf16[32,3712]{1,0:T(8,128)(2,1)S(1)}, u32[]{:S(2)}, u32[]{:S(2)}) collective-permute-start(bf16[32,3712]{1,0:T(8,128)(2,1)S(1)} %bitcast.10), channel_id=1, source_target_pairs={{0,1},{1,0},{2,3},{3,2},{4,5},{5,4},{6,7},{7,6},{8,9},{9,8},{10,11... | collective-permute-start | bytes 712712 | tf_op jit(solution)/shard_map/ppermute | solution.py:33
  31.4 14.0 %all-to-all-start.1 = ((bf16[16,8,1024]{2,1,0:T(8,128)(2,1)}), bf16[16,8,1024]{2,1,0:T(8,128)(2,1)S(1)}, u32[]{:S(2)}, u32[]{:S(2)}) async-start(bf16[16,8,1024]{2,1,0:T(8,128)(2,1)} %shard_map.111), calls=%async_computation.1 | async-start | bytes 524288 | tf_op jit(solution)/shard_map/all_to_all | solution.py:430
  34.9 10.5 %collective-permute-start.4 = (bf16[64,1792]{1,0:T(8,128)(2,1)S(1)}, bf16[64,1792]{1,0:T(8,128)(2,1)S(1)}, u32[]{:S(2)}, u32[]{:S(2)}) collective-permute-start(bf16[64,1792]{1,0:T(8,128)(2,1)S(1)} %bitcast.11), channel_id=1, source_target_pairs={{0,2},{2,0},{1,3},{3,1},{4,6},{6,4},{5,7},{7,5},{8,10},{10,8},{9,1... | collective-permute-start | bytes 688136 | tf_op jit(solution)/shard_map/ppermute | solution.py:33

commit v5 on v4

--- a/solution.py
+++ b/solution.py
@@ -35,24 +35,6 @@
 
 def stay(*arrays):
     return [pltpu.with_memory_space_constraint(a, pltpu.HBM) for a in arrays]
-
-
-def cut_kernel(his, los, partial_ref, out_ref, sems):
-    cols = out_ref.shape[3]
-    l = lax.axis_index("lo")
-    copies = []
-    for k in range(1, los):
-        for x in range(his):
-            at = pl.multiple_of((x * los + lax.rem(l + k, los)) * cols, LANES)
-            copies.append(
-                pltpu.make_async_copy(
-                    partial_ref.at[0, :, pl.ds(at, cols)], out_ref.at[k - 1, x], sems.at[k - 1, x]
-                )
-            )
-    for copy in copies:
-        copy.start()
-    for copy in copies:
-        copy.wait()
 
 
 def early_kernel(his, los, partial_ref, hidden_ref, ids_hbm, prob_hbm, *refs):
@@ -111,12 +93,13 @@
     others, sel_ref, res_ref = refs[: los - 1], refs[los - 1], refs[los]
     his, _, cols = own_ref.shape
     width = cols // SPLIT
-    h = lax.axis_index("hi")
+    h, l = lax.axis_index("hi"), lax.axis_index("lo")
     for k in range(1, his):
         hh = lax.rem(h + k, his)
         pair = own_ref[hh].astype(F32)
+        at = pl.multiple_of((hh * los + l) * cols, LANES)
         for other in others:
-            pair = pair + other[hh].astype(F32)
+            pair = pair + other[:, pl.ds(at, cols)].astype(F32)
         pair = pair.astype(BF)
         res_ref[k - 1] = pair
         chosen = dot(pick_ref[0], pair[:, :width])
@@ -136,10 +119,11 @@
         copy.start()
     cols = hidden_ref.shape[1]
     width = cols // SPLIT
-    h = lax.axis_index("hi")
+    h, l = lax.axis_index("hi"), lax.axis_index("lo")
     mine = hidden_ref[...].astype(F32) + own_ref[h].astype(F32)
+    at = pl.multiple_of((h * los + l) * cols, LANES)
     for other in others:
-        mine = mine + other[h].astype(F32)
+        mine = mine + other[:, pl.ds(at, cols)].astype(F32)
     mine_ref[...] = mine
     chosen = dot(pick_ref[0].astype(F32), mine[:, :width], HIGHEST)
     for s in range(1, SPLIT):
@@ -281,22 +265,17 @@
 
 
 def combine_kernel(mine_ref, comb_ref, back_ref, tile_ref, *refs):
-    rests, (out_hbm, peak_ref, out_ref, sems) = refs[:-4], refs[-4:]
+    rests, (out_ref, peak_ref) = refs[:-2], refs[-2:]
     blocks, subs, width = back_ref.shape
     width = width - LANES
     back = back_ref[:, :, :width].reshape(blocks * subs, width)
-    copies = []
     for s in range(SPLIT):
         cut = slice(s * width, (s + 1) * width)
         res = mine_ref[:, cut]
         for rest in rests:
             res = res + rest[:, cut].astype(F32)
         out_ref[:, cut] = (res + dot(comb_ref[s], back)).astype(BF)
-        copies.append(pltpu.make_async_copy(out_ref.at[:, cut], out_hbm.at[:, cut], sems.at[s]))
-        copies[-1].start()
     peak_ref[0] = jnp.max(tile_ref[...])
-    for copy in copies:
-        copy.wait()
 
 
 def call(kernel, mib, ins, outs, scratch=(), flops=0, moved=0):
@@ -328,14 +307,7 @@
     slots, rows = experts * EXPERT_SLOTS, experts * SUBLANES
     gain = norm_gain.reshape(1, -1)
 
-    (cut,) = call(
-        lambda *refs: cut_kernel(his, los, *refs),
-        1,
-        far(attn_partial),
-        [pltpu.VMEM((los - 1, his, tokens, cols), BF)],
-        [pltpu.SemaphoreType.DMA((los - 1, his))],
-    )
-    others = [shift(cut[k - 1], "lo", k) for k in range(1, los)]
+    others = [shift(attn_partial[0], "lo", k) for k in range(1, los)]
     own, hidden, pick, comb = call(
         lambda *refs: early_kernel(his, los, *refs),
         4,
@@ -379,7 +351,6 @@
         [pltpu.SemaphoreType.DMA((4,))],
         moved=12 * MIB,
     )
-    rests = [shift(rests[k - 1], "hi", k) for k in range(1, his)]
     (outgoing,) = call(
         lambda *refs: dispatch_kernel(his - 1, *refs),
         4,
@@ -414,6 +385,7 @@
         ],
     )
     sends = [shift(sends[k - 1], "lo", k) for k in range(1, los)]
+    rests = [shift(rests[k - 1], "hi", k) for k in range(1, his)]
     (keep,) = call(
         lambda *refs: third_kernel(his, los, *refs),
         8,
@@ -429,7 +401,10 @@
     )
     back = lax.all_to_all(back, ("dp", "hi"), 0, 0, tiled=True)
     (tile,) = call(
-        lambda *refs: peak_kernel(his, *refs), 1, near(back), [pltpu.VMEM((SUBLANES, LANES), F32)]
+        lambda *refs: peak_kernel(his, *refs),
+        1,
+        near(back),
+        [pltpu.VMEM((SUBLANES, LANES), F32)],
     )
     layer_out, hidden_top = pl.pallas_call(
         combine_kernel,
@@ -438,8 +413,7 @@
             jax.ShapeDtypeStruct((1,), F32),
         ],
         in_specs=[VMEM] * (3 + his),
-        out_specs=[HBM, SMEM],
-        scratch_shapes=[pltpu.VMEM((tokens, cols), BF), pltpu.SemaphoreType.DMA((SPLIT,))],
+        out_specs=[VMEM, SMEM],
         compiler_params=pltpu.CompilerParams(vmem_limit_bytes=4 * MIB),
         name="combine",
     )(mine, comb, back, tile, *rests)

time: 47.1 us -> 46.4 us (0.985)
  Pallas kernels: 11.6 us -> 10.1 us
  waiting for transfers between devices: 10.4 us -> 11.3 us
    pallas_call x10 -> x9, Pallas kernels: 10.2 us -> 9.18 us  [call(): pl.pallas_call(kernel, out_shape=outs, in_specs=[HBM if at == 'hbm' else...]
    ppermute x5, waiting for transfers between devices: 1.74 us -> 2.61 us  [shift(): return lax.ppermute(x, axis, [(i, (i + by) % n) for i in range(n)])]
    pallas_call x1, Pallas kernels: 1.4 us -> 0.91 us  [on_device(): pl.pallas_call(combine_kernel, out_shape=[jax.ShapeDtypeStruct((tokens, c...]
where the time goes in v5:
time: 46.4 us; the launch traced here: 46.1 us
  blocking collectives  15 us (32%)
  waiting for transfers between devices  11.3 us (24%)
  Pallas kernels  10.1 us (22%)
  starting transfers between devices  9.05 us (20%)
  between operations  0.69 us (1%)
    all_to_all x1, blocking collectives, on_device(): lax.all_to_all(outgoing.reshape(blocks, SUBLANES, width), ('dp', 'hi'), 0...  15 us
    pallas_call x9, Pallas kernels, call(): pl.pallas_call(kernel, out_shape=outs, in_specs=[HBM if at == 'hbm' else...  9.18 us
    all_to_all x1, waiting for transfers between devices, on_device(): back = lax.all_to_all(back, ('dp', 'hi'), 0, 0, tiled=True)  8.65 us
    ppermute x5, starting transfers between devices, shift(): return lax.ppermute(x, axis, [(i, (i + by) % n) for i in range(n)])  5.52 us
    all_to_all x1, starting transfers between devices, on_device(): back = lax.all_to_all(back, ('dp', 'hi'), 0, 0, tiled=True)  3.53 us
    ppermute x5, waiting for transfers between devices, shift(): return lax.ppermute(x, axis, [(i, (i + by) % n) for i in range(n)])  2.61 us
  transfers between devices with their start and end apart: 6, of which 4 were waited for; matrix products, arithmetic and copies ran while one was open for 0% of the time, Pallas kernels for 15%

profile of v5, /device:TPU:0, one launch (start us, length us, event | category | flops | bytes accessed | tf_op | source)
XLA Modules:
  0.0 46.1 jit_solution(17837984734189192722)
XLA Ops:
  0.6 0.6 %collective-permute-start = (bf16[64,7168]{1,0:T(8,128)(2,1)}, bf16[64,7168]{1,0:T(8,128)(2,1)S(1)}, u32[]{:S(2)}, u32[]{:S(2)}) collective-permute-start(bf16[64,7168]{1,0:T(8,128)(2,1)} %bitcast.12), channel_id=1, source_target_pairs={{0,1},{1,0},{2,3},{3,2},{4,5},{5,4},{6,7},{7,6},{8,9},{9,8},{10,11... | collective-permute-start | bytes 2752520 | tf_op jit(solution)/shard_map/ppermute | solution.py:33
  1.2 1.4 %shard_map.103 = (bf16[2,64,1792]{2,1,0:T(8,128)(2,1)S(1)}, bf16[64,1792]{1,0:T(8,128)(2,1)S(1)}, bf16[2,64,64]{2,1,0:T(8,128)(2,1)S(1)}, bf16[2,64,128]{2,1,0:T(8,128)(2,1)S(1)}) custom-call(bf16[1,64,7168]{2,1,0:T(8,128)(2,1)} %refs_0_.1, bf16[64,1792]{1,0:T(8,128)(2,1)} %refs_1_.2, s32[8,64]{1,0:T(8,128)} %bitcast.14, bf16[8,64]{1,0:T(8,128)(2,1)} %bitcast.15), custom_call_target="tpu_custom_call" | custom-call | bytes 1048576 | tf_op jit(solution)/shard_map/pallas_call | solution.py:283
  2.6 0.9 %collective-permute-done.refs_7_.refs_2_ = bf16[64,7168]{1,0:T(8,128)(2,1)S(1)} collective-permute-done((bf16[64,7168]{1,0:T(8,128)(2,1)}, bf16[64,7168]{1,0:T(8,128)(2,1)S(1)}, u32[]{:S(2)}, u32[]{:S(2)}) %collective-permute-start) | collective-permute-done | bytes 917536 | tf_op jit(solution)/shard_map/ppermute | solution.py:33
  3.5 0.2 shard_map.105
  3.7 2.9 %collective-permute-start.1 = (bf16[64,896]{1,0:T(8,128)(2,1)S(1)}, bf16[64,896]{1,0:T(8,128)(2,1)S(1)}, u32[]{:S(2)}, u32[]{:S(2)}) collective-permute-start(bf16[64,896]{1,0:T(8,128)(2,1)S(1)} %bitcast.11), channel_id=1, source_target_pairs={{0,2},{2,0},{1,3},{3,1},{4,6},{6,4},{5,7},{7,5},{8,10},{10,8},{9,1... | collective-permute-start | bytes 344072 | tf_op jit(solution)/shard_map/ppermute | solution.py:33
  6.6 4.3 %shard_map.104 = (f32[1,7168]{1,0:T(1,128)S(1)}, bf16[1,7168,256]{2,1,0:T(8,128)(2,1)S(1)}, bf16[1,7168,256]{2,1,0:T(8,128)(2,1)S(1)}, bf16[1,256,7168]{2,1,0:T(...) custom-call(f32[1,7168]{1,0:T(1,128)} %bitcast.13, bf16[1,7168,256]{2,1,0:T(8,128)(2,1)} %refs_1_.3, ...), custom_call_target="tpu_custom_call" | custom-call | bytes 12582912 | tf_op jit(solution)/shard_map/pallas_call | solution.py:283
  10.9 0.0 collective-permute-done.1.refs_1_
  10.9 15.0 %all_to_all.10.refs_3_ = bf16[16,8,896]{2,1,0:T(8,128)(2,1)S(1)} all-to-all(bf16[16,8,896]{2,1,0:T(8,128)(2,1)S(1)} %bitcast.8), channel_id=1, replica_groups=mesh['dp'=8,'hi'=2,'lo'=2] {'dp','hi'}, dimensions={0} | all-to-all | bytes 458752 | tf_op jit(solution)/shard_map/all_to_all | solution.py:360
  26.0 0.0 collective-permute-start.2
  26.0 0.8 %shard_map.107 = (f32[32,256]{1,0:T(8,128)S(1)}, f32[32,256]{1,0:T(8,128)S(1)}, f32[32,128]{1,0:T(8,128)S(1)}, f32[32,128]{1,0:T(8,128)S(1)}) custom-call(f32[1,7168]{1,0:T(1,128)S(1)} %get-tuple-element.30.refs_0_, bf16[1,7168,256]{2,1,0:T(8,128)(2,1)S(1)} %get-tuple-element.31.refs_1_, bf16[1,7168,256]{2,1,0:T(8,128)(2,1)S(1)} %get-tuple-element.32.refs_2_, ...), custom_call_target="tpu_custom_call" | custom-call | bytes 4194304 | tf_op jit(solution)/shard_map/pallas_call | solution.py:283
  26.7 0.7 %collective-permute-done.2.refs_8_ = bf16[16,8,896]{2,1,0:T(8,128)(2,1)S(1)} collective-permute-done((bf16[16,8,896]{2,1,0:T(8,128)(2,1)S(1)}, bf16[16,8,896]{2,1,0:T(8,128)(2,1)S(1)}, u32[]{:S(2)}, u32[]{:S(2)}) %collective-permute-start.2) | collective-permute-done | bytes 229408 | tf_op jit(solution)/shard_map/ppermute | solution.py:33
  27.5 1.3 %shard_map.108 = (bf16[1,32,3712]{2,1,0:T(8,128)(2,1)S(1)}, bf16[32,256]{1,0:T(8,128)(2,1)S(1)}, f32[8,128]{1,0:T(8,128)S(1)}, f32[1]{0:T(128)}) custom-call(f32[1,7168]{1,0:T(1,128)S(1)} %get-tuple-element.30.refs_0_, bf16[1,7168,256]{2,1,0:T(8,128)(2,1)S(1)} %get-tuple-element.31.refs_1_, bf16[1,7168,256]{2,1,0:T(8,128)(2,1)S(1)} %get-tuple-element.32.refs_2_, ...), custom_call_target="tpu_custom_call" | custom-call | tf_op jit(solution)/shard_map/pallas_call | solution.py:283
  28.7 0.2 collective-permute-start.3
  28.9 0.4 shard_map.109.refs_0_
  29.4 0.9 %collective-permute-done.3.refs_2_ = bf16[32,3712]{1,0:T(8,128)(2,1)S(1)} collective-permute-done((bf16[32,3712]{1,0:T(8,128)(2,1)S(1)}, bf16[32,3712]{1,0:T(8,128)(2,1)S(1)}, u32[]{:S(2)}, u32[]{:S(2)}) %collective-permute-start.3) | collective-permute-done | bytes 237600 | tf_op jit(solution)/shard_map/ppermute | solution.py:33
  30.3 0.8 %shard_map.110 = bf16[16,8,1024]{2,1,0:T(8,128)(2,1)} custom-call(f32[32,3584]{1,0:T(8,128)S(1)} %shard_map.109.refs_0_, f32[8,128]{1,0:T(8,128)S(1)} %get-tuple-element.41.refs_1_, bf16[32,3712]{1,0:T(8,128)(2,1)S(1)} %collective-permute-done.3.refs_2_), custom_call_target="tpu_custom_call" | custom-call | tf_op jit(solution)/shard_map/pallas_call | solution.py:283
  31.2 3.5 %all-to-all-start.1 = ((bf16[16,8,1024]{2,1,0:T(8,128)(2,1)}), bf16[16,8,1024]{2,1,0:T(8,128)(2,1)S(1)}, u32[]{:S(2)}, u32[]{:S(2)}) async-start(bf16[16,8,1024]{2,1,0:T(8,128)(2,1)} %shard_map.110), calls=%async_computation.1 | async-start | bytes 524288 | tf_op jit(solution)/shard_map/all_to_all | solution.py:402
  34.7 1.8 %collective-permute-start.4 = (bf16[64,1792]{1,0:T(8,128)(2,1)S(1)}, bf16[64,1792]{1,0:T(8,128)(2,1)S(1)}, u32[]{:S(2)}, u32[]{:S(2)}) collective-permute-start(bf16[64,1792]{1,0:T(8,128)(2,1)S(1)} %bitcast.10), channel_id=1, source_target_pairs={{0,2},{2,0},{1,3},{3,1},{4,6},{6,4},{5,7},{7,5},{8,10},{10,8},{9,1... | collective-permute-start | bytes 688136 | tf_op jit(solution)/shard_map/ppermute | solution.py:33
  36.5 8.6 %all-to-all-done.1.refs_0_.back_ref = bf16[16,8,1024]{2,1,0:T(8,128)(2,1)S(1)} async-done(((bf16[16,8,1024]{2,1,0:T(8,128)(2,1)}), bf16[16,8,1024]{2,1,0:T(8,128)(2,1)S(1)}, u32[]{:S(2)}, u32[]{:S(2)}) %all-to-all-start.1) | async-done | bytes 262176 | tf_op jit(solution)/shard_map/all_to_all | solution.py:402
  45.2 0.0 collective-permute-done.4.refs_0_
  45.2 0.9 %combine.1 = (bf16[64,1792]{1,0:T(8,128)(2,1)}, f32[1]{0:T(128)}) custom-call(f32[64,1792]{1,0:T(8,128)S(1)} %get-tuple-element.28.mine_ref, bf16[2,64,128]{2,1,0:T(8,128)(2,1)S(1)} %get-tuple-element.29.comb_ref, bf16[16,8,1024]{2,1,0:T(8,128)(2,1)S(1)} %all-to-all-done.1.refs_0_.back_ref, f32[8,128]{1,0:T(8,128)S(1)} %shard_map.111.tile_ref, ...), custom_call_target="tpu_custom_call" | custom-call | tf_op jit(solution)/shard_map/combine/pallas_call | solution.py:409
  (2 shorter events, 0.0 us)
Async XLA Ops:
  0.6 2.9 %collective-permute-start = (bf16[64,7168]{1,0:T(8,128)(2,1)}, bf16[64,7168]{1,0:T(8,128)(2,1)S(1)}, u32[]{:S(2)}, u32[]{:S(2)}) collective-permute-start(bf16[64,7168]{1,0:T(8,128)(2,1)} %bitcast.12), channel_id=1, source_target_pairs={{0,1},{1,0},{2,3},{3,2},{4,5},{5,4},{6,7},{7,6},{8,9},{9,8},{10,11... | collective-permute-start | bytes 2752520 | tf_op jit(solution)/shard_map/ppermute | solution.py:33
  3.7 7.2 %collective-permute-start.1 = (bf16[64,896]{1,0:T(8,128)(2,1)S(1)}, bf16[64,896]{1,0:T(8,128)(2,1)S(1)}, u32[]{:S(2)}, u32[]{:S(2)}) collective-permute-start(bf16[64,896]{1,0:T(8,128)(2,1)S(1)} %bitcast.11), channel_id=1, source_target_pairs={{0,2},{2,0},{1,3},{3,1},{4,6},{6,4},{5,7},{7,5},{8,10},{10,8},{9,1... | collective-permute-start | bytes 344072 | tf_op jit(solution)/shard_map/ppermute | solution.py:33
  26.0 1.5 %collective-permute-start.2 = (bf16[16,8,896]{2,1,0:T(8,128)(2,1)S(1)}, bf16[16,8,896]{2,1,0:T(8,128)(2,1)S(1)}, u32[]{:S(2)}, u32[]{:S(2)}) collective-permute-start(bf16[16,8,896]{2,1,0:T(8,128)(2,1)S(1)} %all_to_all.10.refs_3_), channel_id=1, source_target_pairs={{0,1},{1,0},{2,3},{3,2},{4,5},{5,4},{6,7},{7,6},{8,9},{9,8},{10,11... | collective-permute-start | bytes 688136 | tf_op jit(solution)/shard_map/ppermute | solution.py:33
  28.7 1.6 %collective-permute-start.3 = (bf16[32,3712]{1,0:T(8,128)(2,1)S(1)}, bf16[32,3712]{1,0:T(8,128)(2,1)S(1)}, u32[]{:S(2)}, u32[]{:S(2)}) collective-permute-start(bf16[32,3712]{1,0:T(8,128)(2,1)S(1)} %bitcast.9), channel_id=1, source_target_pairs={{0,1},{1,0},{2,3},{3,2},{4,5},{5,4},{6,7},{7,6},{8,9},{9,8},{10,11... | collective-permute-start | bytes 712712 | tf_op jit(solution)/shard_map/ppermute | solution.py:33
  31.2 14.0 %all-to-all-start.1 = ((bf16[16,8,1024]{2,1,0:T(8,128)(2,1)}), bf16[16,8,1024]{2,1,0:T(8,128)(2,1)S(1)}, u32[]{:S(2)}, u32[]{:S(2)}) async-start(bf16[16,8,1024]{2,1,0:T(8,128)(2,1)} %shard_map.110), calls=%async_computation.1 | async-start | bytes 524288 | tf_op jit(solution)/shard_map/all_to_all | solution.py:402
  34.7 10.5 %collective-permute-start.4 = (bf16[64,1792]{1,0:T(8,128)(2,1)S(1)}, bf16[64,1792]{1,0:T(8,128)(2,1)S(1)}, u32[]{:S(2)}, u32[]{:S(2)}) collective-permute-start(bf16[64,1792]{1,0:T(8,128)(2,1)S(1)} %bitcast.10), channel_id=1, source_target_pairs={{0,2},{2,0},{1,3},{3,1},{4,6},{6,4},{5,7},{7,5},{8,10},{10,8},{9,1... | collective-permute-start | bytes 688136 | tf_op jit(solution)/shard_map/ppermute | solution.py:33

commit v6 on v5

--- a/solution.py
+++ b/solution.py
@@ -205,10 +205,10 @@
         yield slice(x * cols, (x + 1) * cols), dot(act, wd_ref[0, :, pl.ds(at, cols)])
 
 
-def second_kernel(his, los, gain_ref, wg_ref, wu_ref, wd_ref, *refs):
+def second_kernel(los, gain_ref, wg_ref, wu_ref, *refs):
     gate_ref, up_ref, square_ref, top_ref = refs[:4]
     helds = refs[4 : 3 + los]
-    send_ref, act_ref, peak_ref, out_ref = refs[3 + los :]
+    act_ref, peak_ref, out_ref = refs[3 + los :]
     gate, up, square, top = products(
         los,
         list(enumerate(helds, 1)),
@@ -221,17 +221,19 @@
         top_ref[:, :1],
     )
     scale = lax.rsqrt(square / wg_ref.shape[1] + eps)
-    out_ref[0] = jnp.max(top * scale).astype(BF).astype(F32)
+    out_ref[...] = jnp.full(out_ref.shape, jnp.max(top * scale), F32)
     gate, up = gate * scale, up * scale
     act = (gate / (1.0 + jnp.exp(-gate)) * up).astype(BF)
     act_ref[...] = act
     peak = jnp.max(jnp.abs(act.astype(F32)))
     peak_ref[...] = jnp.full(peak_ref.shape, peak, F32)
-    l, slots = lax.axis_index("lo"), act.shape[0]
+
+
+def down_kernel(his, los, act_ref, wd_ref, send_ref):
     for k in range(1, los):
-        for cut, value in down(act, wd_ref, his, los, lax.rem(l + k, los)):
+        c = lax.rem(lax.axis_index("lo") + k, los)
+        for cut, value in down(act_ref[...], wd_ref, his, los, c):
             send_ref[k - 1, :, cut] = value.astype(BF)
-        send_ref[k - 1, :, -LANES:] = jnp.full((slots, LANES), peak, F32).astype(BF)
 
 
 def third_kernel(his, los, act_ref, wd_ref, keep_ref):
@@ -239,14 +241,22 @@
         keep_ref[:, cut] = value
 
 
-def pair_kernel(his, n, keep_ref, peak_ref, *refs):
+def tag_kernel(los, rests_ref, peak_ref, *refs):
+    tiles, (out_ref, tile_ref) = refs[: los - 1], refs[los - 1 :]
+    peak = peak_ref[...]
+    for tile in tiles:
+        peak = jnp.maximum(peak, tile[...])
+    tile_ref[...] = peak
+    cols = rests_ref.shape[2]
+    for k in range(rests_ref.shape[0]):
+        out_ref[k, :, :cols] = rests_ref[k]
+        out_ref[k, :, cols:] = jnp.broadcast_to(peak[:1], (out_ref.shape[1], LANES)).astype(BF)
+
+
+def pair_kernel(his, n, keep_ref, *refs):
     gots, out_ref = refs[:n], refs[n]
     blocks, subs, width = out_ref.shape
-    width = width - LANES
     cols, experts = SPLIT * width, blocks // his
-    peak = jnp.max(peak_ref[...])
-    for got in gots:
-        peak = jnp.maximum(peak, jnp.max(got[:, -LANES:].astype(F32)))
     for x in range(his):
         total = keep_ref[:, x * cols : (x + 1) * cols]
         for got in gots:
@@ -256,26 +266,27 @@
             even, odd = regroup(total[rows, :width], total[rows, width:])
             out_ref[p * his + x, :, :width] = even.astype(BF)
             out_ref[(p + 1) * his + x, :, :width] = odd.astype(BF)
-    out_ref[:, :, width:] = jnp.full((blocks, subs, LANES), peak, F32).astype(BF)
-
-
-def peak_kernel(his, back_ref, peak_ref):
-    peak = back_ref[pl.ds(lax.axis_index("dp") * his, his), :, -LANES:].astype(F32)
-    peak_ref[...] = jnp.max(peak, axis=0)
-
-
-def combine_kernel(mine_ref, comb_ref, back_ref, tile_ref, *refs):
-    rests, (out_ref, peak_ref) = refs[:-2], refs[-2:]
+
+
+def hold_kernel(back_ref, tile_ref, out_ref):
+    out_ref[...] = tile_ref[...]
+
+
+def combine_kernel(his, mine_ref, comb_ref, back_ref, top_ref, tile_ref, *refs):
+    rests, (out_ref, input_ref, hidden_ref) = refs[: his - 1], refs[-3:]
+    input_ref[0] = jnp.max(top_ref[...].astype(BF).astype(F32))
     blocks, subs, width = back_ref.shape
-    width = width - LANES
-    back = back_ref[:, :, :width].reshape(blocks * subs, width)
+    back = back_ref[...].reshape(blocks * subs, width)
     for s in range(SPLIT):
         cut = slice(s * width, (s + 1) * width)
         res = mine_ref[:, cut]
         for rest in rests:
             res = res + rest[:, cut].astype(F32)
         out_ref[:, cut] = (res + dot(comb_ref[s], back)).astype(BF)
-    peak_ref[0] = jnp.max(tile_ref[...])
+    peak = tile_ref[...]
+    for rest in rests:
+        peak = jnp.maximum(peak, rest[:SUBLANES, -LANES:].astype(F32))
+    hidden_ref[0] = jnp.max(peak)
 
 
 def call(kernel, mib, ins, outs, scratch=(), flops=0, moved=0):
@@ -373,19 +384,25 @@
         ],
         moved=4 * MIB,
     )
-    sends, act, peak, top = call(
-        lambda *refs: second_kernel(his, los, *refs),
-        12,
-        near(gain, wg, wu, wd, *sums, *helds),
-        [
-            pltpu.VMEM((los - 1, slots, his * cols + LANES), BF),
+    act, peak, top = call(
+        lambda *refs: second_kernel(los, *refs),
+        8,
+        near(gain, wg, wu, *sums, *helds),
+        [
             pltpu.VMEM((slots, units), BF),
             pltpu.VMEM((SUBLANES, LANES), F32),
-            jax.ShapeDtypeStruct((1,), F32),
-        ],
+            pltpu.VMEM((SUBLANES, LANES), F32),
+        ],
+    )
+    tiles = [shift(peak, "lo", k) for k in range(1, los)]
+    (sends,) = call(
+        lambda *refs: down_kernel(his, los, *refs),
+        8,
+        near(act, wd),
+        [pltpu.VMEM((los - 1, slots, his * cols), BF)],
+        moved=2 * MIB,
     )
     sends = [shift(sends[k - 1], "lo", k) for k in range(1, los)]
-    rests = [shift(rests[k - 1], "hi", k) for k in range(1, his)]
     (keep,) = call(
         lambda *refs: third_kernel(his, los, *refs),
         8,
@@ -393,31 +410,37 @@
         [pltpu.VMEM((slots, his * cols), F32)],
         moved=2 * MIB,
     )
+    rests, tile = call(
+        lambda *refs: tag_kernel(los, *refs),
+        4,
+        near(rests, peak, *tiles),
+        [
+            pltpu.VMEM((his - 1, tokens, cols + LANES), BF),
+            pltpu.VMEM((SUBLANES, LANES), F32),
+        ],
+    )
+    rests = [shift(rests[k - 1], "hi", k) for k in range(1, his)]
     (back,) = call(
         lambda *refs: pair_kernel(his, los - 1, *refs),
         4,
-        near(keep, peak, *sends),
-        [pltpu.VMEM((blocks, SUBLANES, width + LANES), BF)],
+        near(keep, *sends),
+        [pltpu.VMEM((blocks, SUBLANES, width), BF)],
     )
     back = lax.all_to_all(back, ("dp", "hi"), 0, 0, tiled=True)
-    (tile,) = call(
-        lambda *refs: peak_kernel(his, *refs),
-        1,
-        near(back),
-        [pltpu.VMEM((SUBLANES, LANES), F32)],
-    )
-    layer_out, hidden_top = pl.pallas_call(
-        combine_kernel,
+    (tile,) = call(hold_kernel, 1, near(back, tile), [pltpu.VMEM((SUBLANES, LANES), F32)])
+    layer_out, input_top, hidden_top = pl.pallas_call(
+        lambda *refs: combine_kernel(his, *refs),
         out_shape=[
             jax.ShapeDtypeStruct((tokens, cols), BF),
             jax.ShapeDtypeStruct((1,), F32),
-        ],
-        in_specs=[VMEM] * (3 + his),
-        out_specs=[VMEM, SMEM],
+            jax.ShapeDtypeStruct((1,), F32),
+        ],
+        in_specs=[VMEM] * (4 + his),
+        out_specs=[VMEM, SMEM, SMEM],
         compiler_params=pltpu.CompilerParams(vmem_limit_bytes=4 * MIB),
         name="combine",
-    )(mine, comb, back, tile, *rests)
-    return layer_out, top, hidden_top
+    )(mine, comb, back, top, tile, *rests)
+    return layer_out, input_top, hidden_top
 
 
 def solution(mesh):

time: 46.4 us -> 46.9 us (1.011)
    ppermute x5 -> x6, waiting for transfers between devices: 2.61 us -> 4.91 us  [shift(): return lax.ppermute(x, axis, [(i, (i + by) % n) for i in range(n)])]
    all_to_all x1, waiting for transfers between devices: 8.65 us -> 6.68 us  [on_device(): back = lax.all_to_all(back, ('dp', 'hi'), 0, 0, tiled=True)]
    ppermute x5 -> x6, starting transfers between devices: 5.52 us -> 5.7 us  [shift(): return lax.ppermute(x, axis, [(i, (i + by) % n) for i in range(n)])]
    pallas_call x9 -> x11, Pallas kernels: 9.18 us -> 9.14 us  [call(): pl.pallas_call(kernel, out_shape=outs, in_specs=[HBM if at == 'hbm' else...]
  transfers between devices with their start and end apart: 6 -> 7, of which waited for: 4 -> 6; matrix products, arithmetic and copies ran while one was open for 0% -> 0% of each run, Pallas kernels for 15% -> 15%
where the time goes in v6:
time: 46.9 us; the launch traced here: 46.6 us
  blocking collectives  15 us (32%)
  waiting for transfers between devices  11.6 us (25%)
  Pallas kernels  10.1 us (22%)
  starting transfers between devices  9.23 us (20%)
  between operations  0.7 us (1%)
    all_to_all x1, blocking collectives, on_device(): lax.all_to_all(outgoing.reshape(blocks, SUBLANES, width), ('dp', 'hi'), 0...  15 us
    pallas_call x11, Pallas kernels, call(): pl.pallas_call(kernel, out_shape=outs, in_specs=[HBM if at == 'hbm' else...  9.14 us
    all_to_all x1, waiting for transfers between devices, on_device(): back = lax.all_to_all(back, ('dp', 'hi'), 0, 0, tiled=True)  6.68 us
    ppermute x6, starting transfers between devices, shift(): return lax.ppermute(x, axis, [(i, (i + by) % n) for i in range(n)])  5.7 us
    ppermute x6, waiting for transfers between devices, shift(): return lax.ppermute(x, axis, [(i, (i + by) % n) for i in range(n)])  4.91 us
    all_to_all x1, starting transfers between devices, on_device(): back = lax.all_to_all(back, ('dp', 'hi'), 0, 0, tiled=True)  3.53 us
  transfers between devices with their start and end apart: 7, of which 6 were waited for; matrix products, arithmetic and copies ran while one was open for 0% of the time, Pallas kernels for 15%

profile of v6, /device:TPU:0, one launch (start us, length us, event | category | flops | bytes accessed | tf_op | source)
XLA Modules:
  0.0 46.6 jit_solution(5579238447428562118)
XLA Ops:
  0.6 0.6 %collective-permute-start = (bf16[64,7168]{1,0:T(8,128)(2,1)}, bf16[64,7168]{1,0:T(8,128)(2,1)S(1)}, u32[]{:S(2)}, u32[]{:S(2)}) collective-permute-start(bf16[64,7168]{1,0:T(8,128)(2,1)} %bitcast.12), channel_id=1, source_target_pairs={{0,1},{1,0},{2,3},{3,2},{4,5},{5,4},{6,7},{7,6},{8,9},{9,8},{10,11... | collective-permute-start | bytes 2752520 | tf_op jit(solution)/shard_map/ppermute | solution.py:33
  1.2 1.4 %shard_map.103 = (bf16[2,64,1792]{2,1,0:T(8,128)(2,1)S(1)}, bf16[64,1792]{1,0:T(8,128)(2,1)S(1)}, bf16[2,64,64]{2,1,0:T(8,128)(2,1)S(1)}, bf16[2,64,128]{2,1,0:T(8,128)(2,1)S(1)}) custom-call(bf16[1,64,7168]{2,1,0:T(8,128)(2,1)} %refs_0_.1, bf16[64,1792]{1,0:T(8,128)(2,1)} %refs_1_.2, s32[8,64]{1,0:T(8,128)} %bitcast.14, bf16[8,64]{1,0:T(8,128)(2,1)} %bitcast.15), custom_call_target="tpu_custom_call" | custom-call | bytes 1048576 | tf_op jit(solution)/shard_map/pallas_call | solution.py:294
  2.6 0.9 %collective-permute-done.refs_7_.refs_2_ = bf16[64,7168]{1,0:T(8,128)(2,1)S(1)} collective-permute-done((bf16[64,7168]{1,0:T(8,128)(2,1)}, bf16[64,7168]{1,0:T(8,128)(2,1)S(1)}, u32[]{:S(2)}, u32[]{:S(2)}) %collective-permute-start) | collective-permute-done | bytes 917536 | tf_op jit(solution)/shard_map/ppermute | solution.py:33
  3.5 0.2 shard_map.105
  3.7 2.9 %collective-permute-start.1 = (bf16[64,896]{1,0:T(8,128)(2,1)S(1)}, bf16[64,896]{1,0:T(8,128)(2,1)S(1)}, u32[]{:S(2)}, u32[]{:S(2)}) collective-permute-start(bf16[64,896]{1,0:T(8,128)(2,1)S(1)} %bitcast.11), channel_id=1, source_target_pairs={{0,2},{2,0},{1,3},{3,1},{4,6},{6,4},{5,7},{7,5},{8,10},{10,8},{9,1... | collective-permute-start | bytes 344072 | tf_op jit(solution)/shard_map/ppermute | solution.py:33
  6.6 4.3 %shard_map.104 = (f32[1,7168]{1,0:T(1,128)S(1)}, bf16[1,7168,256]{2,1,0:T(8,128)(2,1)S(1)}, bf16[1,7168,256]{2,1,0:T(8,128)(2,1)S(1)}, bf16[1,256,7168]{2,1,0:T(...) custom-call(f32[1,7168]{1,0:T(1,128)} %bitcast.13, bf16[1,7168,256]{2,1,0:T(8,128)(2,1)} %refs_1_.3, ...), custom_call_target="tpu_custom_call" | custom-call | bytes 12582912 | tf_op jit(solution)/shard_map/pallas_call | solution.py:294
  10.9 0.0 collective-permute-done.1.refs_1_
  10.9 15.0 %all_to_all.10.refs_3_ = bf16[16,8,896]{2,1,0:T(8,128)(2,1)S(1)} all-to-all(bf16[16,8,896]{2,1,0:T(8,128)(2,1)S(1)} %bitcast.8), channel_id=1, replica_groups=mesh['dp'=8,'hi'=2,'lo'=2] {'dp','hi'}, dimensions={0} | all-to-all | bytes 458752 | tf_op jit(solution)/shard_map/all_to_all | solution.py:371
  26.0 0.0 collective-permute-start.2
  26.0 0.8 %shard_map.107 = (f32[32,256]{1,0:T(8,128)S(1)}, f32[32,256]{1,0:T(8,128)S(1)}, f32[32,128]{1,0:T(8,128)S(1)}, f32[32,128]{1,0:T(8,128)S(1)}) custom-call(f32[1,7168]{1,0:T(1,128)S(1)} %get-tuple-element.29.refs_0_, bf16[1,7168,256]{2,1,0:T(8,128)(2,1)S(1)} %get-tuple-element.30.refs_1_, bf16[1,7168,256]{2,1,0:T(8,128)(2,1)S(1)} %get-tuple-element.31.refs_2_, ...), custom_call_target="tpu_custom_call" | custom-call | bytes 4194304 | tf_op jit(solution)/shard_map/pallas_call | solution.py:294
  26.7 0.7 %collective-permute-done.2.refs_7_ = bf16[16,8,896]{2,1,0:T(8,128)(2,1)S(1)} collective-permute-done((bf16[16,8,896]{2,1,0:T(8,128)(2,1)S(1)}, bf16[16,8,896]{2,1,0:T(8,128)(2,1)S(1)}, u32[]{:S(2)}, u32[]{:S(2)}) %collective-permute-start.2) | collective-permute-done | bytes 229408 | tf_op jit(solution)/shard_map/ppermute | solution.py:33
  27.5 0.9 %shard_map.108 = (bf16[32,256]{1,0:T(8,128)(2,1)S(1)}, f32[8,128]{1,0:T(8,128)S(1)}, f32[8,128]{1,0:T(8,128)S(1)}) custom-call(f32[1,7168]{1,0:T(1,128)S(1)} %get-tuple-element.29.refs_0_, bf16[1,7168,256]{2,1,0:T(8,128)(2,1)S(1)} %get-tuple-element.30.refs_1_, bf16[1,7168,256]{2,1,0:T(8,128)(2,1)S(1)} %get-tuple-element.31.refs_2_, ...), custom_call_target="tpu_custom_call" | custom-call | tf_op jit(solution)/shard_map/pallas_call | solution.py:294
  28.4 0.4 shard_map.110
  28.8 0.2 collective-permute-start.3
  29.0 0.4 shard_map.109.refs_0_
  29.4 0.9 %collective-permute-done.3.refs_1_ = bf16[32,3584]{1,0:T(8,128)(2,1)S(1)} collective-permute-done((bf16[32,3584]{1,0:T(8,128)(2,1)S(1)}, bf16[32,3584]{1,0:T(8,128)(2,1)S(1)}, u32[]{:S(2)}, u32[]{:S(2)}) %collective-permute-start.3) | collective-permute-done | bytes 229408 | tf_op jit(solution)/shard_map/ppermute | solution.py:33
  30.3 0.8 %shard_map.111 = bf16[16,8,896]{2,1,0:T(8,128)(2,1)} custom-call(f32[32,3584]{1,0:T(8,128)S(1)} %shard_map.109.refs_0_, bf16[32,3584]{1,0:T(8,128)(2,1)S(1)} %collective-permute-done.3.refs_1_), custom_call_target="tpu_custom_call" | custom-call | tf_op jit(solution)/shard_map/pallas_call | solution.py:294
  31.1 3.5 %all-to-all-start.1 = ((bf16[16,8,896]{2,1,0:T(8,128)(2,1)}), bf16[16,8,896]{2,1,0:T(8,128)(2,1)S(1)}, u32[]{:S(2)}, u32[]{:S(2)}) async-start(bf16[16,8,896]{2,1,0:T(8,128)(2,1)} %shard_map.111), calls=%async_computation.1 | async-start | bytes 458752 | tf_op jit(solution)/shard_map/all_to_all | solution.py:429
  34.6 0.2 collective-permute-start.4
  34.8 1.0 %collective-permute-done.4.refs_2_ = f32[8,128]{1,0:T(8,128)S(1)} collective-permute-done((f32[8,128]{1,0:T(8,128)S(1)}, f32[8,128]{1,0:T(8,128)S(1)}, u32[]{:S(2)}, u32[]{:S(2)}) %collective-permute-start.4) | collective-permute-done | bytes 4128 | tf_op jit(solution)/shard_map/ppermute | solution.py:33
  35.9 1.8 %collective-permute-start.5 = (bf16[64,1920]{1,0:T(8,128)(2,1)S(1)}, bf16[64,1920]{1,0:T(8,128)(2,1)S(1)}, u32[]{:S(2)}, u32[]{:S(2)}) collective-permute-start(bf16[64,1920]{1,0:T(8,128)(2,1)S(1)} %bitcast.10), channel_id=1, source_target_pairs={{0,2},{2,0},{1,3},{3,1},{4,6},{6,4},{5,7},{7,5},{8,10},{10,8},{9,1... | collective-permute-start | bytes 737288 | tf_op jit(solution)/shard_map/ppermute | solution.py:33
  37.7 6.7 %all-to-all-done.1.back_ref.refs_2_ = bf16[16,8,896]{2,1,0:T(8,128)(2,1)S(1)} async-done(((bf16[16,8,896]{2,1,0:T(8,128)(2,1)}), bf16[16,8,896]{2,1,0:T(8,128)(2,1)S(1)}, u32[]{:S(2)}, u32[]{:S(2)}) %all-to-all-start.1) | async-done | bytes 229408 | tf_op jit(solution)/shard_map/all_to_all | solution.py:429
  44.4 1.3 %collective-permute-done.5.refs_5_ = bf16[64,1920]{1,0:T(8,128)(2,1)S(1)} collective-permute-done((bf16[64,1920]{1,0:T(8,128)(2,1)S(1)}, bf16[64,1920]{1,0:T(8,128)(2,1)S(1)}, u32[]{:S(2)}, u32[]{:S(2)}) %collective-permute-start.5) | collective-permute-done | bytes 245792 | tf_op jit(solution)/shard_map/ppermute | solution.py:33
  45.7 0.9 %combine.1 = (bf16[64,1792]{1,0:T(8,128)(2,1)}, f32[1]{0:T(128)}, f32[1]{0:T(128)}) custom-call(f32[64,1792]{1,0:T(8,128)S(1)} %get-tuple-element.27.refs_0_, bf16[2,64,128]{2,1,0:T(8,128)(2,1)S(1)} %get-tuple-element.28.refs_1_, bf16[16,8,896]{2,1,0:T(8,128)(2,1)S(1)} %all-to-all-done.1.back_ref.refs_2_, f32[8,128]{1,0:T(8,128)S(1)} %get-tuple-element.40.refs_3_, ...), custom_call_target="tpu_custom_call" | custom-call | tf_op jit(solution)/shard_map/combine/pallas_call | solution.py:431
  (3 shorter events, 0.0 us)
Async XLA Ops:
  0.6 2.9 %collective-permute-start = (bf16[64,7168]{1,0:T(8,128)(2,1)}, bf16[64,7168]{1,0:T(8,128)(2,1)S(1)}, u32[]{:S(2)}, u32[]{:S(2)}) collective-permute-start(bf16[64,7168]{1,0:T(8,128)(2,1)} %bitcast.12), channel_id=1, source_target_pairs={{0,1},{1,0},{2,3},{3,2},{4,5},{5,4},{6,7},{7,6},{8,9},{9,8},{10,11... | collective-permute-start | bytes 2752520 | tf_op jit(solution)/shard_map/ppermute | solution.py:33
  3.7 7.2 %collective-permute-start.1 = (bf16[64,896]{1,0:T(8,128)(2,1)S(1)}, bf16[64,896]{1,0:T(8,128)(2,1)S(1)}, u32[]{:S(2)}, u32[]{:S(2)}) collective-permute-start(bf16[64,896]{1,0:T(8,128)(2,1)S(1)} %bitcast.11), channel_id=1, source_target_pairs={{0,2},{2,0},{1,3},{3,1},{4,6},{6,4},{5,7},{7,5},{8,10},{10,8},{9,1... | collective-permute-start | bytes 344072 | tf_op jit(solution)/shard_map/ppermute | solution.py:33
  26.0 1.5 %collective-permute-start.2 = (bf16[16,8,896]{2,1,0:T(8,128)(2,1)S(1)}, bf16[16,8,896]{2,1,0:T(8,128)(2,1)S(1)}, u32[]{:S(2)}, u32[]{:S(2)}) collective-permute-start(bf16[16,8,896]{2,1,0:T(8,128)(2,1)S(1)} %all_to_all.10.refs_3_), channel_id=1, source_target_pairs={{0,1},{1,0},{2,3},{3,2},{4,5},{5,4},{6,7},{7,6},{8,9},{9,8},{10,11... | collective-permute-start | bytes 688136 | tf_op jit(solution)/shard_map/ppermute | solution.py:33
  28.8 1.5 %collective-permute-start.3 = (bf16[32,3584]{1,0:T(8,128)(2,1)S(1)}, bf16[32,3584]{1,0:T(8,128)(2,1)S(1)}, u32[]{:S(2)}, u32[]{:S(2)}) collective-permute-start(bf16[32,3584]{1,0:T(8,128)(2,1)S(1)} %bitcast.9), channel_id=1, source_target_pairs={{0,1},{1,0},{2,3},{3,2},{4,5},{5,4},{6,7},{7,6},{8,9},{9,8},{10,11... | collective-permute-start | bytes 688136 | tf_op jit(solution)/shard_map/ppermute | solution.py:33
  31.1 13.3 %all-to-all-start.1 = ((bf16[16,8,896]{2,1,0:T(8,128)(2,1)}), bf16[16,8,896]{2,1,0:T(8,128)(2,1)S(1)}, u32[]{:S(2)}, u32[]{:S(2)}) async-start(bf16[16,8,896]{2,1,0:T(8,128)(2,1)} %shard_map.111), calls=%async_computation.1 | async-start | bytes 458752 | tf_op jit(solution)/shard_map/all_to_all | solution.py:429
  34.6 1.2 %collective-permute-start.4 = (f32[8,128]{1,0:T(8,128)S(1)}, f32[8,128]{1,0:T(8,128)S(1)}, u32[]{:S(2)}, u32[]{:S(2)}) collective-permute-start(f32[8,128]{1,0:T(8,128)S(1)} %get-tuple-element.42.refs_1_), channel_id=1, source_target_pairs={{0,1},{1,0},{2,3},{3,2},{4,5},{5,4},{6,7},{7,6},{8,9},{9,8},{10,11... | collective-permute-start | bytes 12296 | tf_op jit(solution)/shard_map/ppermute | solution.py:33
  35.9 9.8 %collective-permute-start.5 = (bf16[64,1920]{1,0:T(8,128)(2,1)S(1)}, bf16[64,1920]{1,0:T(8,128)(2,1)S(1)}, u32[]{:S(2)}, u32[]{:S(2)}) collective-permute-start(bf16[64,1920]{1,0:T(8,128)(2,1)S(1)} %bitcast.10), channel_id=1, source_target_pairs={{0,2},{2,0},{1,3},{3,1},{4,6},{6,4},{5,7},{7,5},{8,10},{10,8},{9,1... | collective-permute-start | bytes 737288 | tf_op jit(solution)/shard_map/ppermute | solution.py:33

commit v7 on v5

--- a/solution.py
+++ b/solution.py
@@ -58,7 +58,7 @@
     for copy in first:
         copy.wait()
     names, tokens = ids_ref.shape
-    rows, wide = pick_ref.shape[1], comb_ref.shape[2]
+    rows, wide = pick_ref.shape[1], comb_ref.shape[1]
     experts = rows // SUBLANES
     ids, prob = ids_ref[...], prob_ref[...].astype(F32)
     expert = iota((experts, tokens), 0)
@@ -81,10 +81,10 @@
         here = (slots == (at % EXPERT_SLOTS).astype(F32)) & (at // EXPERT_SLOTS % SPLIT == s)
         pick_ref[s] = jnp.where(here, 1.0, 0.0).astype(BF)
     at = iota((wide, tokens), 0)
-    slots, weights = spread(slot, wide, his * SUBLANES), spread(weight, wide, his * SUBLANES)
-    for s in range(SPLIT):
-        here = (slots == (at % EXPERT_SLOTS).astype(F32)) & (at // EXPERT_SLOTS % SPLIT == s)
-        comb_ref[s] = jnp.where(here, weights, 0.0).T.astype(BF)
+    per = his * EXPERT_SLOTS
+    slots, weights = spread(slot, wide, per), spread(weight, wide, per)
+    here = slots == (at % EXPERT_SLOTS).astype(F32)
+    comb_ref[...] = jnp.where(here, weights, 0.0).T.astype(BF)
     for copy in rest:
         copy.wait()
 
@@ -180,8 +180,10 @@
             value = value * gain_ref[:, pl.ds(at, cols)]
             top = jnp.maximum(top, jnp.max(jnp.abs(value), axis=1, keepdims=True))
             value = value.astype(BF)
-            gate = gate + dot(value, wg_ref[0, pl.ds(at, cols), :])
-            up = up + dot(value, wu_ref[0, pl.ds(at, cols), :])
+            for n in range(0, cols, 896):
+                part, here = value[:, n : n + 896], pl.ds(at + n, 896)
+                gate = gate + dot(part, wg_ref[0, here, :])
+                up = up + dot(part, wu_ref[0, here, :])
     return gate, up, square, top
 
 
@@ -221,17 +223,17 @@
         top_ref[:, :1],
     )
     scale = lax.rsqrt(square / wg_ref.shape[1] + eps)
-    out_ref[0] = jnp.max(top * scale).astype(BF).astype(F32)
+    out_ref[...] = jnp.full(out_ref.shape, jnp.max(top * scale), F32)
     gate, up = gate * scale, up * scale
     act = (gate / (1.0 + jnp.exp(-gate)) * up).astype(BF)
     act_ref[...] = act
     peak = jnp.max(jnp.abs(act.astype(F32)))
     peak_ref[...] = jnp.full(peak_ref.shape, peak, F32)
-    l, slots = lax.axis_index("lo"), act.shape[0]
     for k in range(1, los):
-        for cut, value in down(act, wd_ref, his, los, lax.rem(l + k, los)):
+        c = lax.rem(lax.axis_index("lo") + k, los)
+        for cut, value in down(act, wd_ref, his, los, c):
             send_ref[k - 1, :, cut] = value.astype(BF)
-        send_ref[k - 1, :, -LANES:] = jnp.full((slots, LANES), peak, F32).astype(BF)
+        send_ref[k - 1, :, -LANES:] = jnp.full((act.shape[0], LANES), peak, F32).astype(BF)
 
 
 def third_kernel(his, los, act_ref, wd_ref, keep_ref):
@@ -241,41 +243,36 @@
 
 def pair_kernel(his, n, keep_ref, peak_ref, *refs):
     gots, out_ref = refs[:n], refs[n]
-    blocks, subs, width = out_ref.shape
-    width = width - LANES
-    cols, experts = SPLIT * width, blocks // his
-    peak = jnp.max(peak_ref[...])
+    experts, cols = out_ref.shape[0] // his, out_ref.shape[2] - LANES
+    peak = peak_ref[:EXPERT_SLOTS]
     for got in gots:
-        peak = jnp.maximum(peak, jnp.max(got[:, -LANES:].astype(F32)))
+        peak = jnp.maximum(peak, got[:EXPERT_SLOTS, -LANES:].astype(F32))
     for x in range(his):
         total = keep_ref[:, x * cols : (x + 1) * cols]
         for got in gots:
             total = total + got[:, x * cols : (x + 1) * cols].astype(F32)
-        for p in range(0, experts, SPLIT):
-            rows = slice(p * EXPERT_SLOTS, p * EXPERT_SLOTS + subs)
-            even, odd = regroup(total[rows, :width], total[rows, width:])
-            out_ref[p * his + x, :, :width] = even.astype(BF)
-            out_ref[(p + 1) * his + x, :, :width] = odd.astype(BF)
-    out_ref[:, :, width:] = jnp.full((blocks, subs, LANES), peak, F32).astype(BF)
-
-
-def peak_kernel(his, back_ref, peak_ref):
+        for e in range(experts):
+            rows = total[e * EXPERT_SLOTS : (e + 1) * EXPERT_SLOTS]
+            out_ref[e * his + x, :, :cols] = rows.astype(BF)
+            out_ref[e * his + x, :, cols:] = peak.astype(BF)
+
+
+def hold_kernel(his, back_ref, out_ref):
     peak = back_ref[pl.ds(lax.axis_index("dp") * his, his), :, -LANES:].astype(F32)
-    peak_ref[...] = jnp.max(peak, axis=0)
-
-
-def combine_kernel(mine_ref, comb_ref, back_ref, tile_ref, *refs):
-    rests, (out_ref, peak_ref) = refs[:-2], refs[-2:]
-    blocks, subs, width = back_ref.shape
-    width = width - LANES
-    back = back_ref[:, :, :width].reshape(blocks * subs, width)
-    for s in range(SPLIT):
-        cut = slice(s * width, (s + 1) * width)
-        res = mine_ref[:, cut]
-        for rest in rests:
-            res = res + rest[:, cut].astype(F32)
-        out_ref[:, cut] = (res + dot(comb_ref[s], back)).astype(BF)
-    peak_ref[0] = jnp.max(tile_ref[...])
+    out_ref[...] = jnp.max(peak, axis=0)
+
+
+def combine_kernel(his, mine_ref, comb_ref, back_ref, top_ref, tile_ref, *refs):
+    rests, (out_ref, input_ref, hidden_ref) = refs[: his - 1], refs[-3:]
+    input_ref[0] = jnp.max(top_ref[...].astype(BF).astype(F32))
+    hidden_ref[0] = jnp.max(tile_ref[...])
+    blocks, slots, cols = back_ref.shape
+    cols = cols - LANES
+    back = back_ref[:, :, :cols].reshape(blocks * slots, cols)
+    res = mine_ref[...]
+    for rest in rests:
+        res = res + rest[...].astype(F32)
+    out_ref[...] = (res + dot(comb_ref[...], back)).astype(BF)
 
 
 def call(kernel, mib, ins, outs, scratch=(), flops=0, moved=0):
@@ -316,7 +313,7 @@
             pltpu.VMEM((his, tokens, cols), BF),
             pltpu.VMEM((tokens, cols), BF),
             pltpu.VMEM((SPLIT, rows, tokens), BF),
-            pltpu.VMEM((SPLIT, tokens, blocks * SUBLANES), BF),
+            pltpu.VMEM((tokens, blocks * EXPERT_SLOTS), BF),
         ],
         [
             pltpu.VMEM(expert_ids.shape[::-1], expert_ids.dtype),
@@ -361,6 +358,7 @@
         outgoing.reshape(blocks, SUBLANES, width), ("dp", "hi"), 0, 0, tiled=True
     )
     helds = [shift(incoming, "lo", k) for k in range(1, los)]
+    rests = [shift(rests[k - 1], "hi", k) for k in range(1, his)]
     sums = call(
         lambda *refs: first_kernel(los, *refs),
         8,
@@ -375,17 +373,16 @@
     )
     sends, act, peak, top = call(
         lambda *refs: second_kernel(his, los, *refs),
-        12,
+        8,
         near(gain, wg, wu, wd, *sums, *helds),
         [
             pltpu.VMEM((los - 1, slots, his * cols + LANES), BF),
             pltpu.VMEM((slots, units), BF),
             pltpu.VMEM((SUBLANES, LANES), F32),
-            jax.ShapeDtypeStruct((1,), F32),
+            pltpu.VMEM((SUBLANES, LANES), F32),
         ],
     )
     sends = [shift(sends[k - 1], "lo", k) for k in range(1, los)]
-    rests = [shift(rests[k - 1], "hi", k) for k in range(1, his)]
     (keep,) = call(
         lambda *refs: third_kernel(his, los, *refs),
         8,
@@ -397,27 +394,28 @@
         lambda *refs: pair_kernel(his, los - 1, *refs),
         4,
         near(keep, peak, *sends),
-        [pltpu.VMEM((blocks, SUBLANES, width + LANES), BF)],
+        [pltpu.VMEM((blocks, EXPERT_SLOTS, cols + LANES), BF)],
     )
     back = lax.all_to_all(back, ("dp", "hi"), 0, 0, tiled=True)
     (tile,) = call(
-        lambda *refs: peak_kernel(his, *refs),
+        lambda *refs: hold_kernel(his, *refs),
         1,
         near(back),
-        [pltpu.VMEM((SUBLANES, LANES), F32)],
-    )
-    layer_out, hidden_top = pl.pallas_call(
-        combine_kernel,
+        [pltpu.VMEM((EXPERT_SLOTS, LANES), F32)],
+    )
+    layer_out, input_top, hidden_top = pl.pallas_call(
+        lambda *refs: combine_kernel(his, *refs),
         out_shape=[
             jax.ShapeDtypeStruct((tokens, cols), BF),
             jax.ShapeDtypeStruct((1,), F32),
-        ],
-        in_specs=[VMEM] * (3 + his),
-        out_specs=[VMEM, SMEM],
+            jax.ShapeDtypeStruct((1,), F32),
+        ],
+        in_specs=[VMEM] * (4 + his),
+        out_specs=[VMEM, SMEM, SMEM],
         compiler_params=pltpu.CompilerParams(vmem_limit_bytes=4 * MIB),
         name="combine",
-    )(mine, comb, back, tile, *rests)
-    return layer_out, top, hidden_top
+    )(mine, comb, back, top, tile, *rests)
+    return layer_out, input_top, hidden_top
 
 
 def solution(mesh):

time: 46.4 us -> 45.9 us (0.989)
  transfers between devices with their start and end apart: 6 -> 6, of which waited for: 4 -> 5; matrix products, arithmetic and copies ran while one was open for 0% -> 0% of each run, Pallas kernels for 15% -> 15%
where the time goes in v7:
time: 45.9 us; the launch traced here: 45.6 us
  blocking collectives  15 us (33%)
  waiting for transfers between devices  11.1 us (24%)
  Pallas kernels  9.85 us (21%)
  starting transfers between devices  9.02 us (20%)
  between operations  0.68 us (1%)
    all_to_all x1, blocking collectives, on_device(): lax.all_to_all(outgoing.reshape(blocks, SUBLANES, width), ('dp', 'hi'), 0...  15 us
    pallas_call x9, Pallas kernels, call(): pl.pallas_call(kernel, out_shape=outs, in_specs=[HBM if at == 'hbm' else...  8.94 us
    all_to_all x1, waiting for transfers between devices, on_device(): back = lax.all_to_all(back, ('dp', 'hi'), 0, 0, tiled=True)  8.24 us
    ppermute x5, starting transfers between devices, shift(): return lax.ppermute(x, axis, [(i, (i + by) % n) for i in range(n)])  5.49 us
    all_to_all x1, starting transfers between devices, on_device(): back = lax.all_to_all(back, ('dp', 'hi'), 0, 0, tiled=True)  3.53 us
    ppermute x5, waiting for transfers between devices, shift(): return lax.ppermute(x, axis, [(i, (i + by) % n) for i in range(n)])  2.84 us
  transfers between devices with their start and end apart: 6, of which 5 were waited for; matrix products, arithmetic and copies ran while one was open for 0% of the time, Pallas kernels for 15%

profile of v7, /device:TPU:0, one launch (start us, length us, event | category | flops | bytes accessed | tf_op | source)
XLA Modules:
  0.0 45.6 jit_solution(9611844753389283885)
XLA Ops:
  0.6 0.6 %collective-permute-start = (bf16[64,7168]{1,0:T(8,128)(2,1)}, bf16[64,7168]{1,0:T(8,128)(2,1)S(1)}, u32[]{:S(2)}, u32[]{:S(2)}) collective-permute-start(bf16[64,7168]{1,0:T(8,128)(2,1)} %bitcast.12), channel_id=1, source_target_pairs={{0,1},{1,0},{2,3},{3,2},{4,5},{5,4},{6,7},{7,6},{8,9},{9,8},{10,11... | collective-permute-start | bytes 2752520 | tf_op jit(solution)/shard_map/ppermute | solution.py:33
  1.2 1.3 %shard_map.103 = (bf16[2,64,1792]{2,1,0:T(8,128)(2,1)S(1)}, bf16[64,1792]{1,0:T(8,128)(2,1)S(1)}, bf16[2,64,64]{2,1,0:T(8,128)(2,1)S(1)}, bf16[64,64]{1,0:T(8,128)(2,1)S(1)}) custom-call(bf16[1,64,7168]{2,1,0:T(8,128)(2,1)} %refs_0_.1, bf16[64,1792]{1,0:T(8,128)(2,1)} %refs_1_.2, s32[8,64]{1,0:T(8,128)} %bitcast.14, bf16[8,64]{1,0:T(8,128)(2,1)} %bitcast.15), custom_call_target="tpu_custom_call" | custom-call | bytes 1048576 | tf_op jit(solution)/shard_map/pallas_call | solution.py:280
  2.5 1.0 %collective-permute-done.refs_7_.refs_2_ = bf16[64,7168]{1,0:T(8,128)(2,1)S(1)} collective-permute-done((bf16[64,7168]{1,0:T(8,128)(2,1)}, bf16[64,7168]{1,0:T(8,128)(2,1)S(1)}, u32[]{:S(2)}, u32[]{:S(2)}) %collective-permute-start) | collective-permute-done | bytes 917536 | tf_op jit(solution)/shard_map/ppermute | solution.py:33
  3.5 0.2 shard_map.105
  3.7 2.9 %collective-permute-start.1 = (bf16[64,896]{1,0:T(8,128)(2,1)S(1)}, bf16[64,896]{1,0:T(8,128)(2,1)S(1)}, u32[]{:S(2)}, u32[]{:S(2)}) collective-permute-start(bf16[64,896]{1,0:T(8,128)(2,1)S(1)} %bitcast.11), channel_id=1, source_target_pairs={{0,2},{2,0},{1,3},{3,1},{4,6},{6,4},{5,7},{7,5},{8,10},{10,8},{9,1... | collective-permute-start | bytes 344072 | tf_op jit(solution)/shard_map/ppermute | solution.py:33
  6.6 4.3 %shard_map.104 = (f32[1,7168]{1,0:T(1,128)S(1)}, bf16[1,7168,256]{2,1,0:T(8,128)(2,1)S(1)}, bf16[1,7168,256]{2,1,0:T(8,128)(2,1)S(1)}, bf16[1,256,7168]{2,1,0:T(...) custom-call(f32[1,7168]{1,0:T(1,128)} %bitcast.13, bf16[1,7168,256]{2,1,0:T(8,128)(2,1)} %refs_1_.3, ...), custom_call_target="tpu_custom_call" | custom-call | bytes 12582912 | tf_op jit(solution)/shard_map/pallas_call | solution.py:280
  10.9 0.0 collective-permute-done.1.refs_1_
  10.9 15.0 %all_to_all.10.refs_3_ = bf16[16,8,896]{2,1,0:T(8,128)(2,1)S(1)} all-to-all(bf16[16,8,896]{2,1,0:T(8,128)(2,1)S(1)} %bitcast.8), channel_id=1, replica_groups=mesh['dp'=8,'hi'=2,'lo'=2] {'dp','hi'}, dimensions={0} | all-to-all | bytes 458752 | tf_op jit(solution)/shard_map/all_to_all | solution.py:357
  26.0 0.0 collective-permute-start.2
  26.0 0.8 %shard_map.107 = (f32[32,256]{1,0:T(8,128)S(1)}, f32[32,256]{1,0:T(8,128)S(1)}, f32[32,128]{1,0:T(8,128)S(1)}, f32[32,128]{1,0:T(8,128)S(1)}) custom-call(f32[1,7168]{1,0:T(1,128)S(1)} %get-tuple-element.28.refs_0_, bf16[1,7168,256]{2,1,0:T(8,128)(2,1)S(1)} %get-tuple-element.29.refs_1_, bf16[1,7168,256]{2,1,0:T(8,128)(2,1)S(1)} %get-tuple-element.30.refs_2_, ...), custom_call_target="tpu_custom_call" | custom-call | bytes 4194304 | tf_op jit(solution)/shard_map/pallas_call | solution.py:280
  26.7 0.7 %collective-permute-done.2.refs_8_ = bf16[16,8,896]{2,1,0:T(8,128)(2,1)S(1)} collective-permute-done((bf16[16,8,896]{2,1,0:T(8,128)(2,1)S(1)}, bf16[16,8,896]{2,1,0:T(8,128)(2,1)S(1)}, u32[]{:S(2)}, u32[]{:S(2)}) %collective-permute-start.2) | collective-permute-done | bytes 229408 | tf_op jit(solution)/shard_map/ppermute | solution.py:33
  27.5 1.2 %shard_map.108 = (bf16[1,32,3712]{2,1,0:T(8,128)(2,1)S(1)}, bf16[32,256]{1,0:T(8,128)(2,1)S(1)}, f32[8,128]{1,0:T(8,128)S(1)}, f32[8,128]{1,0:T(8,128)S(1)}) custom-call(f32[1,7168]{1,0:T(1,128)S(1)} %get-tuple-element.28.refs_0_, bf16[1,7168,256]{2,1,0:T(8,128)(2,1)S(1)} %get-tuple-element.29.refs_1_, bf16[1,7168,256]{2,1,0:T(8,128)(2,1)S(1)} %get-tuple-element.30.refs_2_, ...), custom_call_target="tpu_custom_call" | custom-call | tf_op jit(solution)/shard_map/pallas_call | solution.py:280
  28.6 0.2 collective-permute-start.3
  28.8 0.4 shard_map.109.refs_0_
  29.2 0.9 %collective-permute-done.3.refs_2_ = bf16[32,3712]{1,0:T(8,128)(2,1)S(1)} collective-permute-done((bf16[32,3712]{1,0:T(8,128)(2,1)S(1)}, bf16[32,3712]{1,0:T(8,128)(2,1)S(1)}, u32[]{:S(2)}, u32[]{:S(2)}) %collective-permute-start.3) | collective-permute-done | bytes 237600 | tf_op jit(solution)/shard_map/ppermute | solution.py:33
  30.2 0.8 %shard_map.110 = bf16[16,4,1920]{2,1,0:T(4,128)(2,1)} custom-call(f32[32,3584]{1,0:T(8,128)S(1)} %shard_map.109.refs_0_, f32[8,128]{1,0:T(8,128)S(1)} %get-tuple-element.39.refs_1_, bf16[32,3712]{1,0:T(8,128)(2,1)S(1)} %collective-permute-done.3.refs_2_), custom_call_target="tpu_custom_call" | custom-call | tf_op jit(solution)/shard_map/pallas_call | solution.py:280
  30.9 3.5 %all-to-all-start.1 = ((bf16[16,4,1920]{2,1,0:T(4,128)(2,1)}), bf16[16,4,1920]{2,1,0:T(4,128)(2,1)S(1)}, u32[]{:S(2)}, u32[]{:S(2)}) async-start(bf16[16,4,1920]{2,1,0:T(4,128)(2,1)} %shard_map.110), calls=%async_computation.1 | async-start | bytes 491520 | tf_op jit(solution)/shard_map/all_to_all | solution.py:399
  34.5 1.8 %collective-permute-start.4 = (bf16[64,1792]{1,0:T(8,128)(2,1)S(1)}, bf16[64,1792]{1,0:T(8,128)(2,1)S(1)}, u32[]{:S(2)}, u32[]{:S(2)}) collective-permute-start(bf16[64,1792]{1,0:T(8,128)(2,1)S(1)} %bitcast.10), channel_id=1, source_target_pairs={{0,2},{2,0},{1,3},{3,1},{4,6},{6,4},{5,7},{7,5},{8,10},{10,8},{9,1... | collective-permute-start | bytes 688136 | tf_op jit(solution)/shard_map/ppermute | solution.py:33
  36.3 8.2 %all-to-all-done.1.refs_0_.refs_2_ = bf16[16,4,1920]{2,1,0:T(4,128)(2,1)S(1)} async-done(((bf16[16,4,1920]{2,1,0:T(4,128)(2,1)}), bf16[16,4,1920]{2,1,0:T(4,128)(2,1)S(1)}, u32[]{:S(2)}, u32[]{:S(2)}) %all-to-all-start.1) | async-done | bytes 245792 | tf_op jit(solution)/shard_map/all_to_all | solution.py:399
  44.6 0.2 collective-permute-done.4.refs_5_
  44.7 0.9 %combine.1 = (bf16[64,1792]{1,0:T(8,128)(2,1)}, f32[1]{0:T(128)}, f32[1]{0:T(128)}) custom-call(f32[64,1792]{1,0:T(8,128)S(1)} %get-tuple-element.26.refs_0_, bf16[64,64]{1,0:T(8,128)(2,1)S(1)} %get-tuple-element.27.refs_1_, bf16[16,4,1920]{2,1,0:T(4,128)(2,1)S(1)} %all-to-all-done.1.refs_0_.refs_2_, f32[8,128]{1,0:T(8,128)S(1)} %get-tuple-element.41.refs_3_, ...), custom_call_target="tpu_custom_call" | custom-call | tf_op jit(solution)/shard_map/combine/pallas_call | solution.py:406
  (2 shorter events, 0.0 us)
Async XLA Ops:
  0.6 2.9 %collective-permute-start = (bf16[64,7168]{1,0:T(8,128)(2,1)}, bf16[64,7168]{1,0:T(8,128)(2,1)S(1)}, u32[]{:S(2)}, u32[]{:S(2)}) collective-permute-start(bf16[64,7168]{1,0:T(8,128)(2,1)} %bitcast.12), channel_id=1, source_target_pairs={{0,1},{1,0},{2,3},{3,2},{4,5},{5,4},{6,7},{7,6},{8,9},{9,8},{10,11... | collective-permute-start | bytes 2752520 | tf_op jit(solution)/shard_map/ppermute | solution.py:33
  3.7 7.2 %collective-permute-start.1 = (bf16[64,896]{1,0:T(8,128)(2,1)S(1)}, bf16[64,896]{1,0:T(8,128)(2,1)S(1)}, u32[]{:S(2)}, u32[]{:S(2)}) collective-permute-start(bf16[64,896]{1,0:T(8,128)(2,1)S(1)} %bitcast.11), channel_id=1, source_target_pairs={{0,2},{2,0},{1,3},{3,1},{4,6},{6,4},{5,7},{7,5},{8,10},{10,8},{9,1... | collective-permute-start | bytes 344072 | tf_op jit(solution)/shard_map/ppermute | solution.py:33
  26.0 1.5 %collective-permute-start.2 = (bf16[16,8,896]{2,1,0:T(8,128)(2,1)S(1)}, bf16[16,8,896]{2,1,0:T(8,128)(2,1)S(1)}, u32[]{:S(2)}, u32[]{:S(2)}) collective-permute-start(bf16[16,8,896]{2,1,0:T(8,128)(2,1)S(1)} %all_to_all.10.refs_3_), channel_id=1, source_target_pairs={{0,1},{1,0},{2,3},{3,2},{4,5},{5,4},{6,7},{7,6},{8,9},{9,8},{10,11... | collective-permute-start | bytes 688136 | tf_op jit(solution)/shard_map/ppermute | solution.py:33
  28.6 1.5 %collective-permute-start.3 = (bf16[32,3712]{1,0:T(8,128)(2,1)S(1)}, bf16[32,3712]{1,0:T(8,128)(2,1)S(1)}, u32[]{:S(2)}, u32[]{:S(2)}) collective-permute-start(bf16[32,3712]{1,0:T(8,128)(2,1)S(1)} %bitcast.9), channel_id=1, source_target_pairs={{0,1},{1,0},{2,3},{3,2},{4,5},{5,4},{6,7},{7,6},{8,9},{9,8},{10,11... | collective-permute-start | bytes 712712 | tf_op jit(solution)/shard_map/ppermute | solution.py:33
  30.9 13.6 %all-to-all-start.1 = ((bf16[16,4,1920]{2,1,0:T(4,128)(2,1)}), bf16[16,4,1920]{2,1,0:T(4,128)(2,1)S(1)}, u32[]{:S(2)}, u32[]{:S(2)}) async-start(bf16[16,4,1920]{2,1,0:T(4,128)(2,1)} %shard_map.110), calls=%async_computation.1 | async-start | bytes 491520 | tf_op jit(solution)/shard_map/all_to_all | solution.py:399
  34.5 10.3 %collective-permute-start.4 = (bf16[64,1792]{1,0:T(8,128)(2,1)S(1)}, bf16[64,1792]{1,0:T(8,128)(2,1)S(1)}, u32[]{:S(2)}, u32[]{:S(2)}) collective-permute-start(bf16[64,1792]{1,0:T(8,128)(2,1)S(1)} %bitcast.10), channel_id=1, source_target_pairs={{0,2},{2,0},{1,3},{3,1},{4,6},{6,4},{5,7},{7,5},{8,10},{10,8},{9,1... | collective-permute-start | bytes 688136 | tf_op jit(solution)/shard_map/ppermute | solution.py:33

commit v8 on v7

--- a/solution.py
+++ b/solution.py
@@ -171,7 +171,8 @@
     l, experts = lax.axis_index("lo"), lax.axis_size("dp")
     for k, held in helds:
         his = held.shape[0] // experts
-        cols = SPLIT * held.shape[2]
+        width = held.shape[2]
+        cols = SPLIT * width
         c = lax.rem(l - k + los, los)
         for x in range(his):
             value = gather_rows(held, x, experts)
@@ -180,8 +181,8 @@
             value = value * gain_ref[:, pl.ds(at, cols)]
             top = jnp.maximum(top, jnp.max(jnp.abs(value), axis=1, keepdims=True))
             value = value.astype(BF)
-            for n in range(0, cols, 896):
-                part, here = value[:, n : n + 896], pl.ds(at + n, 896)
+            for n in range(0, cols, width):
+                part, here = value[:, n : n + width], pl.ds(at + n, width)
                 gate = gate + dot(part, wg_ref[0, here, :])
                 up = up + dot(part, wu_ref[0, here, :])
     return gate, up, square, top

time: 45.9 us -> 45.9 us (level)
  no operation moved by 1% of the time
where the time goes in v8:
time: 45.9 us; the launch traced here: 45.6 us
  blocking collectives  15 us (33%)
  waiting for transfers between devices  11.1 us (24%)
  Pallas kernels  9.85 us (21%)
  starting transfers between devices  9.02 us (20%)
  between operations  0.68 us (1%)
    all_to_all x1, blocking collectives, on_device(): lax.all_to_all(outgoing.reshape(blocks, SUBLANES, width), ('dp', 'hi'), 0...  15 us
    pallas_call x9, Pallas kernels, call(): pl.pallas_call(kernel, out_shape=outs, in_specs=[HBM if at == 'hbm' else...  8.94 us
    all_to_all x1, waiting for transfers between devices, on_device(): back = lax.all_to_all(back, ('dp', 'hi'), 0, 0, tiled=True)  8.24 us
    ppermute x5, starting transfers between devices, shift(): return lax.ppermute(x, axis, [(i, (i + by) % n) for i in range(n)])  5.49 us
    all_to_all x1, starting transfers between devices, on_device(): back = lax.all_to_all(back, ('dp', 'hi'), 0, 0, tiled=True)  3.53 us
    ppermute x5, waiting for transfers between devices, shift(): return lax.ppermute(x, axis, [(i, (i + by) % n) for i in range(n)])  2.84 us
  transfers between devices with their start and end apart: 6, of which 5 were waited for; matrix products, arithmetic and copies ran while one was open for 0% of the time, Pallas kernels for 15%

profile of v8, /device:TPU:0, one launch (start us, length us, event | category | flops | bytes accessed | tf_op | source)
XLA Modules:
  0.0 45.6 jit_solution(9611844753389283885)
XLA Ops:
  0.6 0.6 %collective-permute-start = (bf16[64,7168]{1,0:T(8,128)(2,1)}, bf16[64,7168]{1,0:T(8,128)(2,1)S(1)}, u32[]{:S(2)}, u32[]{:S(2)}) collective-permute-start(bf16[64,7168]{1,0:T(8,128)(2,1)} %bitcast.12), channel_id=1, source_target_pairs={{0,1},{1,0},{2,3},{3,2},{4,5},{5,4},{6,7},{7,6},{8,9},{9,8},{10,11... | collective-permute-start | bytes 2752520 | tf_op jit(solution)/shard_map/ppermute | solution.py:33
  1.2 1.3 %shard_map.103 = (bf16[2,64,1792]{2,1,0:T(8,128)(2,1)S(1)}, bf16[64,1792]{1,0:T(8,128)(2,1)S(1)}, bf16[2,64,64]{2,1,0:T(8,128)(2,1)S(1)}, bf16[64,64]{1,0:T(8,128)(2,1)S(1)}) custom-call(bf16[1,64,7168]{2,1,0:T(8,128)(2,1)} %refs_0_.1, bf16[64,1792]{1,0:T(8,128)(2,1)} %refs_1_.2, s32[8,64]{1,0:T(8,128)} %bitcast.14, bf16[8,64]{1,0:T(8,128)(2,1)} %bitcast.15), custom_call_target="tpu_custom_call" | custom-call | bytes 1048576 | tf_op jit(solution)/shard_map/pallas_call | solution.py:281
  2.5 1.0 %collective-permute-done.refs_7_.refs_2_ = bf16[64,7168]{1,0:T(8,128)(2,1)S(1)} collective-permute-done((bf16[64,7168]{1,0:T(8,128)(2,1)}, bf16[64,7168]{1,0:T(8,128)(2,1)S(1)}, u32[]{:S(2)}, u32[]{:S(2)}) %collective-permute-start) | collective-permute-done | bytes 917536 | tf_op jit(solution)/shard_map/ppermute | solution.py:33
  3.5 0.2 shard_map.105
  3.7 2.9 %collective-permute-start.1 = (bf16[64,896]{1,0:T(8,128)(2,1)S(1)}, bf16[64,896]{1,0:T(8,128)(2,1)S(1)}, u32[]{:S(2)}, u32[]{:S(2)}) collective-permute-start(bf16[64,896]{1,0:T(8,128)(2,1)S(1)} %bitcast.11), channel_id=1, source_target_pairs={{0,2},{2,0},{1,3},{3,1},{4,6},{6,4},{5,7},{7,5},{8,10},{10,8},{9,1... | collective-permute-start | bytes 344072 | tf_op jit(solution)/shard_map/ppermute | solution.py:33
  6.6 4.3 %shard_map.104 = (f32[1,7168]{1,0:T(1,128)S(1)}, bf16[1,7168,256]{2,1,0:T(8,128)(2,1)S(1)}, bf16[1,7168,256]{2,1,0:T(8,128)(2,1)S(1)}, bf16[1,256,7168]{2,1,0:T(...) custom-call(f32[1,7168]{1,0:T(1,128)} %bitcast.13, bf16[1,7168,256]{2,1,0:T(8,128)(2,1)} %refs_1_.3, ...), custom_call_target="tpu_custom_call" | custom-call | bytes 12582912 | tf_op jit(solution)/shard_map/pallas_call | solution.py:281
  10.9 0.0 collective-permute-done.1.refs_1_
  10.9 15.0 %all_to_all.10.refs_3_ = bf16[16,8,896]{2,1,0:T(8,128)(2,1)S(1)} all-to-all(bf16[16,8,896]{2,1,0:T(8,128)(2,1)S(1)} %bitcast.8), channel_id=1, replica_groups=mesh['dp'=8,'hi'=2,'lo'=2] {'dp','hi'}, dimensions={0} | all-to-all | bytes 458752 | tf_op jit(solution)/shard_map/all_to_all | solution.py:358
  26.0 0.0 collective-permute-start.2
  26.0 0.8 %shard_map.107 = (f32[32,256]{1,0:T(8,128)S(1)}, f32[32,256]{1,0:T(8,128)S(1)}, f32[32,128]{1,0:T(8,128)S(1)}, f32[32,128]{1,0:T(8,128)S(1)}) custom-call(f32[1,7168]{1,0:T(1,128)S(1)} %get-tuple-element.28.refs_0_, bf16[1,7168,256]{2,1,0:T(8,128)(2,1)S(1)} %get-tuple-element.29.refs_1_, bf16[1,7168,256]{2,1,0:T(8,128)(2,1)S(1)} %get-tuple-element.30.refs_2_, ...), custom_call_target="tpu_custom_call" | custom-call | bytes 4194304 | tf_op jit(solution)/shard_map/pallas_call | solution.py:281
  26.7 0.7 %collective-permute-done.2.refs_8_ = bf16[16,8,896]{2,1,0:T(8,128)(2,1)S(1)} collective-permute-done((bf16[16,8,896]{2,1,0:T(8,128)(2,1)S(1)}, bf16[16,8,896]{2,1,0:T(8,128)(2,1)S(1)}, u32[]{:S(2)}, u32[]{:S(2)}) %collective-permute-start.2) | collective-permute-done | bytes 229408 | tf_op jit(solution)/shard_map/ppermute | solution.py:33
  27.5 1.2 %shard_map.108 = (bf16[1,32,3712]{2,1,0:T(8,128)(2,1)S(1)}, bf16[32,256]{1,0:T(8,128)(2,1)S(1)}, f32[8,128]{1,0:T(8,128)S(1)}, f32[8,128]{1,0:T(8,128)S(1)}) custom-call(f32[1,7168]{1,0:T(1,128)S(1)} %get-tuple-element.28.refs_0_, bf16[1,7168,256]{2,1,0:T(8,128)(2,1)S(1)} %get-tuple-element.29.refs_1_, bf16[1,7168,256]{2,1,0:T(8,128)(2,1)S(1)} %get-tuple-element.30.refs_2_, ...), custom_call_target="tpu_custom_call" | custom-call | tf_op jit(solution)/shard_map/pallas_call | solution.py:281
  28.6 0.2 collective-permute-start.3
  28.8 0.4 shard_map.109.refs_0_
  29.2 0.9 %collective-permute-done.3.refs_2_ = bf16[32,3712]{1,0:T(8,128)(2,1)S(1)} collective-permute-done((bf16[32,3712]{1,0:T(8,128)(2,1)S(1)}, bf16[32,3712]{1,0:T(8,128)(2,1)S(1)}, u32[]{:S(2)}, u32[]{:S(2)}) %collective-permute-start.3) | collective-permute-done | bytes 237600 | tf_op jit(solution)/shard_map/ppermute | solution.py:33
  30.2 0.8 %shard_map.110 = bf16[16,4,1920]{2,1,0:T(4,128)(2,1)} custom-call(f32[32,3584]{1,0:T(8,128)S(1)} %shard_map.109.refs_0_, f32[8,128]{1,0:T(8,128)S(1)} %get-tuple-element.39.refs_1_, bf16[32,3712]{1,0:T(8,128)(2,1)S(1)} %collective-permute-done.3.refs_2_), custom_call_target="tpu_custom_call" | custom-call | tf_op jit(solution)/shard_map/pallas_call | solution.py:281
  30.9 3.5 %all-to-all-start.1 = ((bf16[16,4,1920]{2,1,0:T(4,128)(2,1)}), bf16[16,4,1920]{2,1,0:T(4,128)(2,1)S(1)}, u32[]{:S(2)}, u32[]{:S(2)}) async-start(bf16[16,4,1920]{2,1,0:T(4,128)(2,1)} %shard_map.110), calls=%async_computation.1 | async-start | bytes 491520 | tf_op jit(solution)/shard_map/all_to_all | solution.py:400
  34.5 1.8 %collective-permute-start.4 = (bf16[64,1792]{1,0:T(8,128)(2,1)S(1)}, bf16[64,1792]{1,0:T(8,128)(2,1)S(1)}, u32[]{:S(2)}, u32[]{:S(2)}) collective-permute-start(bf16[64,1792]{1,0:T(8,128)(2,1)S(1)} %bitcast.10), channel_id=1, source_target_pairs={{0,2},{2,0},{1,3},{3,1},{4,6},{6,4},{5,7},{7,5},{8,10},{10,8},{9,1... | collective-permute-start | bytes 688136 | tf_op jit(solution)/shard_map/ppermute | solution.py:33
  36.3 8.2 %all-to-all-done.1.refs_0_.refs_2_ = bf16[16,4,1920]{2,1,0:T(4,128)(2,1)S(1)} async-done(((bf16[16,4,1920]{2,1,0:T(4,128)(2,1)}), bf16[16,4,1920]{2,1,0:T(4,128)(2,1)S(1)}, u32[]{:S(2)}, u32[]{:S(2)}) %all-to-all-start.1) | async-done | bytes 245792 | tf_op jit(solution)/shard_map/all_to_all | solution.py:400
  44.6 0.2 collective-permute-done.4.refs_5_
  44.7 0.9 %combine.1 = (bf16[64,1792]{1,0:T(8,128)(2,1)}, f32[1]{0:T(128)}, f32[1]{0:T(128)}) custom-call(f32[64,1792]{1,0:T(8,128)S(1)} %get-tuple-element.26.refs_0_, bf16[64,64]{1,0:T(8,128)(2,1)S(1)} %get-tuple-element.27.refs_1_, bf16[16,4,1920]{2,1,0:T(4,128)(2,1)S(1)} %all-to-all-done.1.refs_0_.refs_2_, f32[8,128]{1,0:T(8,128)S(1)} %get-tuple-element.41.refs_3_, ...), custom_call_target="tpu_custom_call" | custom-call | tf_op jit(solution)/shard_map/combine/pallas_call | solution.py:407
  (2 shorter events, 0.0 us)
Async XLA Ops:
  0.6 2.9 %collective-permute-start = (bf16[64,7168]{1,0:T(8,128)(2,1)}, bf16[64,7168]{1,0:T(8,128)(2,1)S(1)}, u32[]{:S(2)}, u32[]{:S(2)}) collective-permute-start(bf16[64,7168]{1,0:T(8,128)(2,1)} %bitcast.12), channel_id=1, source_target_pairs={{0,1},{1,0},{2,3},{3,2},{4,5},{5,4},{6,7},{7,6},{8,9},{9,8},{10,11... | collective-permute-start | bytes 2752520 | tf_op jit(solution)/shard_map/ppermute | solution.py:33
  3.7 7.2 %collective-permute-start.1 = (bf16[64,896]{1,0:T(8,128)(2,1)S(1)}, bf16[64,896]{1,0:T(8,128)(2,1)S(1)}, u32[]{:S(2)}, u32[]{:S(2)}) collective-permute-start(bf16[64,896]{1,0:T(8,128)(2,1)S(1)} %bitcast.11), channel_id=1, source_target_pairs={{0,2},{2,0},{1,3},{3,1},{4,6},{6,4},{5,7},{7,5},{8,10},{10,8},{9,1... | collective-permute-start | bytes 344072 | tf_op jit(solution)/shard_map/ppermute | solution.py:33
  26.0 1.5 %collective-permute-start.2 = (bf16[16,8,896]{2,1,0:T(8,128)(2,1)S(1)}, bf16[16,8,896]{2,1,0:T(8,128)(2,1)S(1)}, u32[]{:S(2)}, u32[]{:S(2)}) collective-permute-start(bf16[16,8,896]{2,1,0:T(8,128)(2,1)S(1)} %all_to_all.10.refs_3_), channel_id=1, source_target_pairs={{0,1},{1,0},{2,3},{3,2},{4,5},{5,4},{6,7},{7,6},{8,9},{9,8},{10,11... | collective-permute-start | bytes 688136 | tf_op jit(solution)/shard_map/ppermute | solution.py:33
  28.6 1.5 %collective-permute-start.3 = (bf16[32,3712]{1,0:T(8,128)(2,1)S(1)}, bf16[32,3712]{1,0:T(8,128)(2,1)S(1)}, u32[]{:S(2)}, u32[]{:S(2)}) collective-permute-start(bf16[32,3712]{1,0:T(8,128)(2,1)S(1)} %bitcast.9), channel_id=1, source_target_pairs={{0,1},{1,0},{2,3},{3,2},{4,5},{5,4},{6,7},{7,6},{8,9},{9,8},{10,11... | collective-permute-start | bytes 712712 | tf_op jit(solution)/shard_map/ppermute | solution.py:33
  30.9 13.6 %all-to-all-start.1 = ((bf16[16,4,1920]{2,1,0:T(4,128)(2,1)}), bf16[16,4,1920]{2,1,0:T(4,128)(2,1)S(1)}, u32[]{:S(2)}, u32[]{:S(2)}) async-start(bf16[16,4,1920]{2,1,0:T(4,128)(2,1)} %shard_map.110), calls=%async_computation.1 | async-start | bytes 491520 | tf_op jit(solution)/shard_map/all_to_all | solution.py:400
  34.5 10.3 %collective-permute-start.4 = (bf16[64,1792]{1,0:T(8,128)(2,1)S(1)}, bf16[64,1792]{1,0:T(8,128)(2,1)S(1)}, u32[]{:S(2)}, u32[]{:S(2)}) collective-permute-start(bf16[64,1792]{1,0:T(8,128)(2,1)S(1)} %bitcast.10), channel_id=1, source_target_pairs={{0,2},{2,0},{1,3},{3,1},{4,6},{6,4},{5,7},{7,5},{8,10},{10,8},{9,1... | collective-permute-start | bytes 688136 | tf_op jit(solution)/shard_map/ppermute | solution.py:33

commit v9 on v8

--- a/solution.py
+++ b/solution.py
@@ -37,8 +37,8 @@
     return [pltpu.with_memory_space_constraint(a, pltpu.HBM) for a in arrays]
 
 
-def early_kernel(his, los, partial_ref, hidden_ref, ids_hbm, prob_hbm, *refs):
-    own_ref, held_ref, pick_ref, comb_ref, ids_ref, prob_ref, small, large = refs
+def early_kernel(his, los, partial_ref, hidden_ref, ids_hbm, prob_hbm, up_hbm, *refs):
+    own_ref, held_ref, pick_ref, comb_ref, up_ref, ids_ref, prob_ref, small, large = refs
     cols = hidden_ref.shape[1]
     l = lax.axis_index("lo")
     first = [
@@ -53,6 +53,8 @@
                 partial_ref.at[0, :, pl.ds(at, cols)], own_ref.at[x], large.at[x]
             )
         )
+    part = up_hbm.at[:, pl.ds(0, up_ref.shape[1]), :]
+    rest.append(pltpu.make_async_copy(part, up_ref, large.at[his + 1]))
     for copy in first + rest:
         copy.start()
     for copy in first:
@@ -112,7 +114,11 @@
     hbms, (hidden_ref, pick_ref, own_ref) = refs[:4], refs[4:7]
     others, (mine_ref, sel_ref), sems = refs[7 : 6 + los], refs[10 + los : 12 + los], refs[-1]
     copies = [
-        pltpu.make_async_copy(hbm, vmem, sems.at[i])
+        pltpu.make_async_copy(
+            hbm if i != 2 else hbm.at[:, pl.ds(hbm.shape[1] - vmem.shape[1], vmem.shape[1]), :],
+            vmem,
+            sems.at[i],
+        )
         for i, (hbm, vmem) in enumerate(zip(hbms, refs[6 + los : 10 + los]))
     ]
     for copy in copies:
@@ -167,7 +173,7 @@
     )
 
 
-def products(los, helds, gain_ref, wg_ref, wu_ref, gate, up, square, top):
+def products(los, helds, gain_ref, wg_ref, wu_refs, gate, up, square, top):
     l, experts = lax.axis_index("lo"), lax.axis_size("dp")
     for k, held in helds:
         his = held.shape[0] // experts
@@ -184,16 +190,17 @@
             for n in range(0, cols, width):
                 part, here = value[:, n : n + width], pl.ds(at + n, width)
                 gate = gate + dot(part, wg_ref[0, here, :])
-                up = up + dot(part, wu_ref[0, here, :])
+                wu_ref, base = (wu_refs[0], 0) if x == 0 else (wu_refs[1], los * cols)
+                up = up + dot(part, wu_ref[0, pl.ds(at + n - base, width), :])
     return gate, up, square, top
 
 
-def first_kernel(los, gain_ref, wg_ref, wu_ref, held_ref, *refs):
+def first_kernel(los, gain_ref, wg_ref, wu_first, wu_rest, held_ref, *refs):
     gate_ref, up_ref, square_ref, top_ref = refs
     slots = gate_ref.shape[0]
     zero, none = jnp.zeros(gate_ref.shape, F32), jnp.zeros((slots, 1), F32)
     gate, up, square, top = products(
-        los, [(0, held_ref)], gain_ref, wg_ref, wu_ref, zero, zero, none, none
+        los, [(0, held_ref)], gain_ref, wg_ref, (wu_first, wu_rest), zero, zero, none, none
     )
     gate_ref[...] = gate
     up_ref[...] = up
@@ -208,7 +215,7 @@
         yield slice(x * cols, (x + 1) * cols), dot(act, wd_ref[0, :, pl.ds(at, cols)])
 
 
-def second_kernel(his, los, gain_ref, wg_ref, wu_ref, wd_ref, *refs):
+def second_kernel(his, los, gain_ref, wg_ref, wu_first, wu_rest, wd_ref, *refs):
     gate_ref, up_ref, square_ref, top_ref = refs[:4]
     helds = refs[4 : 3 + los]
     send_ref, act_ref, peak_ref, out_ref = refs[3 + los :]
@@ -217,7 +224,7 @@
         list(enumerate(helds, 1)),
         gain_ref,
         wg_ref,
-        wu_ref,
+        (wu_first, wu_rest),
         gate_ref[...],
         up_ref[...],
         square_ref[:, :1],
@@ -300,27 +307,28 @@
 def on_device(attn_partial, hidden_in, norm_gain, expert_ids, route_prob, w_gate, w_up, w_down):
     experts, his, los = lax.axis_size("dp"), lax.axis_size("hi"), lax.axis_size("lo")
     tokens, cols = hidden_in.shape
-    _, units = w_gate.shape[1:]
+    features, units = w_gate.shape[1:]
     width, blocks = cols // SPLIT, experts * his
     slots, rows = experts * EXPERT_SLOTS, experts * SUBLANES
     gain = norm_gain.reshape(1, -1)
 
     others = [shift(attn_partial[0], "lo", k) for k in range(1, los)]
-    own, hidden, pick, comb = call(
+    own, hidden, pick, comb, wu_first = call(
         lambda *refs: early_kernel(his, los, *refs),
         4,
-        far(attn_partial, hidden_in, expert_ids.T, route_prob.T),
+        far(attn_partial, hidden_in, expert_ids.T, route_prob.T, w_up),
         [
             pltpu.VMEM((his, tokens, cols), BF),
             pltpu.VMEM((tokens, cols), BF),
             pltpu.VMEM((SPLIT, rows, tokens), BF),
             pltpu.VMEM((tokens, blocks * EXPERT_SLOTS), BF),
+            pltpu.VMEM((1, features // his, units), BF),
         ],
         [
             pltpu.VMEM(expert_ids.shape[::-1], expert_ids.dtype),
             pltpu.VMEM(route_prob.shape[::-1], route_prob.dtype),
             pltpu.SemaphoreType.DMA((2,)),
-            pltpu.SemaphoreType.DMA((his + 1,)),
+            pltpu.SemaphoreType.DMA((his + 2,)),
         ],
         moved=MIB,
     )
@@ -334,14 +342,14 @@
         ],
     )
     sels = [shift(sels[k - 1], "hi", k) for k in range(1, his)]
-    gain, wg, wu, wd, mine, sel = call(
+    gain, wg, wu_rest, wd, mine, sel = call(
         lambda *refs: load_kernel(los, *refs),
         4,
         far(gain, w_gate, w_up, w_down) + near(hidden, pick, own, *others),
         [
             pltpu.VMEM(gain.shape, F32),
             pltpu.VMEM(w_gate.shape, BF),
-            pltpu.VMEM(w_up.shape, BF),
+            pltpu.VMEM((1, features - features // his, units), BF),
             pltpu.VMEM(w_down.shape, BF),
             pltpu.VMEM((tokens, cols), F32),
             pltpu.VMEM((rows, width), F32),
@@ -363,7 +371,7 @@
     sums = call(
         lambda *refs: first_kernel(los, *refs),
         8,
-        near(gain, wg, wu, incoming),
+        near(gain, wg, wu_first, wu_rest, incoming),
         [
             pltpu.VMEM((slots, units), F32),
             pltpu.VMEM((slots, units), F32),
@@ -375,7 +383,7 @@
     sends, act, peak, top = call(
         lambda *refs: second_kernel(his, los, *refs),
         8,
-        near(gain, wg, wu, wd, *sums, *helds),
+        near(gain, wg, wu_first, wu_rest, wd, *sums, *helds),
         [
             pltpu.VMEM((los - 1, slots, his * cols + LANES), BF),
             pltpu.VMEM((slots, units), BF),

time: 45.9 us -> 45.7 us (level)
  waiting for transfers between devices: 11.1 us -> 10.5 us
    ppermute x5, waiting for transfers between devices: 2.84 us -> 2.22 us  [shift(): return lax.ppermute(x, axis, [(i, (i + by) % n) for i in range(n)])]
where the time goes in v9:
time: 45.7 us; the launch traced here: 45.4 us
  blocking collectives  15.3 us (33%)
  waiting for transfers between devices  10.5 us (23%)
  Pallas kernels  9.98 us (22%)
  starting transfers between devices  9.01 us (20%)
  between operations  0.68 us (1%)
    all_to_all x1, blocking collectives, on_device(): lax.all_to_all(outgoing.reshape(blocks, SUBLANES, width), ('dp', 'hi'), 0...  15.3 us
    pallas_call x9, Pallas kernels, call(): pl.pallas_call(kernel, out_shape=outs, in_specs=[HBM if at == 'hbm' else...  9.07 us
    all_to_all x1, waiting for transfers between devices, on_device(): back = lax.all_to_all(back, ('dp', 'hi'), 0, 0, tiled=True)  8.24 us
    ppermute x5, starting transfers between devices, shift(): return lax.ppermute(x, axis, [(i, (i + by) % n) for i in range(n)])  5.49 us
    all_to_all x1, starting transfers between devices, on_device(): back = lax.all_to_all(back, ('dp', 'hi'), 0, 0, tiled=True)  3.53 us
    ppermute x5, waiting for transfers between devices, shift(): return lax.ppermute(x, axis, [(i, (i + by) % n) for i in range(n)])  2.22 us
  transfers between devices with their start and end apart: 6, of which 5 were waited for; matrix products, arithmetic and copies ran while one was open for 0% of the time, Pallas kernels for 15%

profile of v9, /device:TPU:0, one launch (start us, length us, event | category | flops | bytes accessed | tf_op | source)
XLA Modules:
  0.0 45.4 jit_solution(9769204641301724328)
XLA Ops:
  0.6 0.6 %collective-permute-start = (bf16[64,7168]{1,0:T(8,128)(2,1)}, bf16[64,7168]{1,0:T(8,128)(2,1)S(1)}, u32[]{:S(2)}, u32[]{:S(2)}) collective-permute-start(bf16[64,7168]{1,0:T(8,128)(2,1)} %bitcast.12), channel_id=1, source_target_pairs={{0,1},{1,0},{2,3},{3,2},{4,5},{5,4},{6,7},{7,6},{8,9},{9,8},{10,11... | collective-permute-start | bytes 2752520 | tf_op jit(solution)/shard_map/ppermute | solution.py:33
  1.2 1.9 %shard_map.103 = (bf16[2,64,1792]{2,1,0:T(8,128)(2,1)S(1)}, bf16[64,1792]{1,0:T(8,128)(2,1)S(1)}, bf16[2,64,64]{2,1,0:T(8,128)(2,1)S(1)}, bf16[64,64]{1,0:T(8,128)(2,1)S(1)}, bf16[1,3584,256]{2,1,0:T(8,128)(2,1)S(1)}) custom-call(bf16[1,64,7168]{2,1,0:T(8,128)(2,1)} %refs_0_.1, bf16[64,1792]{1,0:T(8,128)(2,1)} %refs_1_.2, s32[8,64]{1,0:T(8,128)} %bitcast.14, ...), custom_call_target="tpu_custom_call" | custom-call | bytes 1048576 | tf_op jit(solution)/shard_map/pallas_call | solution.py:288
  3.1 0.4 collective-permute-done.refs_7_.refs_2_
  3.5 0.2 shard_map.105
  3.7 2.9 %collective-permute-start.1 = (bf16[64,896]{1,0:T(8,128)(2,1)S(1)}, bf16[64,896]{1,0:T(8,128)(2,1)S(1)}, u32[]{:S(2)}, u32[]{:S(2)}) collective-permute-start(bf16[64,896]{1,0:T(8,128)(2,1)S(1)} %bitcast.11), channel_id=1, source_target_pairs={{0,2},{2,0},{1,3},{3,1},{4,6},{6,4},{5,7},{7,5},{8,10},{10,8},{9,1... | collective-permute-start | bytes 344072 | tf_op jit(solution)/shard_map/ppermute | solution.py:33
  6.6 3.8 %shard_map.104 = (f32[1,7168]{1,0:T(1,128)S(1)}, bf16[1,7168,256]{2,1,0:T(8,128)(2,1)S(1)}, bf16[1,3584,256]{2,1,0:T(8,128)(2,1)S(1)}, bf16[1,256,7168]{2,1,0:T(...) custom-call(f32[1,7168]{1,0:T(1,128)} %bitcast.13, bf16[1,7168,256]{2,1,0:T(8,128)(2,1)} %refs_1_.3, ...), custom_call_target="tpu_custom_call" | custom-call | bytes 12582912 | tf_op jit(solution)/shard_map/pallas_call | solution.py:288
  10.4 0.0 collective-permute-done.1.refs_1_
  10.4 15.3 %all_to_all.10.refs_4_ = bf16[16,8,896]{2,1,0:T(8,128)(2,1)S(1)} all-to-all(bf16[16,8,896]{2,1,0:T(8,128)(2,1)S(1)} %bitcast.8), channel_id=1, replica_groups=mesh['dp'=8,'hi'=2,'lo'=2] {'dp','hi'}, dimensions={0} | all-to-all | bytes 458752 | tf_op jit(solution)/shard_map/all_to_all | solution.py:366
  25.7 0.0 collective-permute-start.2
  25.7 0.8 %shard_map.107 = (f32[32,256]{1,0:T(8,128)S(1)}, f32[32,256]{1,0:T(8,128)S(1)}, f32[32,128]{1,0:T(8,128)S(1)}, f32[32,128]{1,0:T(8,128)S(1)}) custom-call(f32[1,7168]{1,0:T(1,128)S(1)} %get-tuple-element.29.refs_0_, bf16[1,7168,256]{2,1,0:T(8,128)(2,1)S(1)} %get-tuple-element.30.refs_1_, bf16[1,3584,256]{2,1,0:T(8,128)(2,1)S(1)} %get-tuple-element.31.refs_2_, ...), custom_call_target="tpu_custom_call" | custom-call | bytes 4194304 | tf_op jit(solution)/shard_map/pallas_call | solution.py:288
  26.5 0.7 %collective-permute-done.2.refs_9_ = bf16[16,8,896]{2,1,0:T(8,128)(2,1)S(1)} collective-permute-done((bf16[16,8,896]{2,1,0:T(8,128)(2,1)S(1)}, bf16[16,8,896]{2,1,0:T(8,128)(2,1)S(1)}, u32[]{:S(2)}, u32[]{:S(2)}) %collective-permute-start.2) | collective-permute-done | bytes 229408 | tf_op jit(solution)/shard_map/ppermute | solution.py:33
  27.2 1.2 %shard_map.108 = (bf16[1,32,3712]{2,1,0:T(8,128)(2,1)S(1)}, bf16[32,256]{1,0:T(8,128)(2,1)S(1)}, f32[8,128]{1,0:T(8,128)S(1)}, f32[8,128]{1,0:T(8,128)S(1)}) custom-call(f32[1,7168]{1,0:T(1,128)S(1)} %get-tuple-element.29.refs_0_, bf16[1,7168,256]{2,1,0:T(8,128)(2,1)S(1)} %get-tuple-element.30.refs_1_, bf16[1,3584,256]{2,1,0:T(8,128)(2,1)S(1)} %get-tuple-element.31.refs_2_, ...), custom_call_target="tpu_custom_call" | custom-call | tf_op jit(solution)/shard_map/pallas_call | solution.py:288
  28.4 0.2 collective-permute-start.3
  28.6 0.4 shard_map.109.refs_0_
  29.0 0.9 %collective-permute-done.3.refs_2_ = bf16[32,3712]{1,0:T(8,128)(2,1)S(1)} collective-permute-done((bf16[32,3712]{1,0:T(8,128)(2,1)S(1)}, bf16[32,3712]{1,0:T(8,128)(2,1)S(1)}, u32[]{:S(2)}, u32[]{:S(2)}) %collective-permute-start.3) | collective-permute-done | bytes 237600 | tf_op jit(solution)/shard_map/ppermute | solution.py:33
  29.9 0.8 %shard_map.110 = bf16[16,4,1920]{2,1,0:T(4,128)(2,1)} custom-call(f32[32,3584]{1,0:T(8,128)S(1)} %shard_map.109.refs_0_, f32[8,128]{1,0:T(8,128)S(1)} %get-tuple-element.41.refs_1_, bf16[32,3712]{1,0:T(8,128)(2,1)S(1)} %collective-permute-done.3.refs_2_), custom_call_target="tpu_custom_call" | custom-call | tf_op jit(solution)/shard_map/pallas_call | solution.py:288
  30.7 3.5 %all-to-all-start.1 = ((bf16[16,4,1920]{2,1,0:T(4,128)(2,1)}), bf16[16,4,1920]{2,1,0:T(4,128)(2,1)S(1)}, u32[]{:S(2)}, u32[]{:S(2)}) async-start(bf16[16,4,1920]{2,1,0:T(4,128)(2,1)} %shard_map.110), calls=%async_computation.1 | async-start | bytes 491520 | tf_op jit(solution)/shard_map/all_to_all | solution.py:408
  34.2 1.8 %collective-permute-start.4 = (bf16[64,1792]{1,0:T(8,128)(2,1)S(1)}, bf16[64,1792]{1,0:T(8,128)(2,1)S(1)}, u32[]{:S(2)}, u32[]{:S(2)}) collective-permute-start(bf16[64,1792]{1,0:T(8,128)(2,1)S(1)} %bitcast.10), channel_id=1, source_target_pairs={{0,2},{2,0},{1,3},{3,1},{4,6},{6,4},{5,7},{7,5},{8,10},{10,8},{9,1... | collective-permute-start | bytes 688136 | tf_op jit(solution)/shard_map/ppermute | solution.py:33
  36.1 8.2 %all-to-all-done.1.refs_0_.refs_2_ = bf16[16,4,1920]{2,1,0:T(4,128)(2,1)S(1)} async-done(((bf16[16,4,1920]{2,1,0:T(4,128)(2,1)}), bf16[16,4,1920]{2,1,0:T(4,128)(2,1)S(1)}, u32[]{:S(2)}, u32[]{:S(2)}) %all-to-all-start.1) | async-done | bytes 245792 | tf_op jit(solution)/shard_map/all_to_all | solution.py:408
  44.3 0.2 collective-permute-done.4.refs_5_
  44.5 0.9 %combine.1 = (bf16[64,1792]{1,0:T(8,128)(2,1)}, f32[1]{0:T(128)}, f32[1]{0:T(128)}) custom-call(f32[64,1792]{1,0:T(8,128)S(1)} %get-tuple-element.27.refs_0_, bf16[64,64]{1,0:T(8,128)(2,1)S(1)} %get-tuple-element.28.refs_1_, bf16[16,4,1920]{2,1,0:T(4,128)(2,1)S(1)} %all-to-all-done.1.refs_0_.refs_2_, f32[8,128]{1,0:T(8,128)S(1)} %get-tuple-element.43.refs_3_, ...), custom_call_target="tpu_custom_call" | custom-call | tf_op jit(solution)/shard_map/combine/pallas_call | solution.py:415
  (2 shorter events, 0.0 us)
Async XLA Ops:
  0.6 2.9 %collective-permute-start = (bf16[64,7168]{1,0:T(8,128)(2,1)}, bf16[64,7168]{1,0:T(8,128)(2,1)S(1)}, u32[]{:S(2)}, u32[]{:S(2)}) collective-permute-start(bf16[64,7168]{1,0:T(8,128)(2,1)} %bitcast.12), channel_id=1, source_target_pairs={{0,1},{1,0},{2,3},{3,2},{4,5},{5,4},{6,7},{7,6},{8,9},{9,8},{10,11... | collective-permute-start | bytes 2752520 | tf_op jit(solution)/shard_map/ppermute | solution.py:33
  3.7 6.7 %collective-permute-start.1 = (bf16[64,896]{1,0:T(8,128)(2,1)S(1)}, bf16[64,896]{1,0:T(8,128)(2,1)S(1)}, u32[]{:S(2)}, u32[]{:S(2)}) collective-permute-start(bf16[64,896]{1,0:T(8,128)(2,1)S(1)} %bitcast.11), channel_id=1, source_target_pairs={{0,2},{2,0},{1,3},{3,1},{4,6},{6,4},{5,7},{7,5},{8,10},{10,8},{9,1... | collective-permute-start | bytes 344072 | tf_op jit(solution)/shard_map/ppermute | solution.py:33
  25.7 1.5 %collective-permute-start.2 = (bf16[16,8,896]{2,1,0:T(8,128)(2,1)S(1)}, bf16[16,8,896]{2,1,0:T(8,128)(2,1)S(1)}, u32[]{:S(2)}, u32[]{:S(2)}) collective-permute-start(bf16[16,8,896]{2,1,0:T(8,128)(2,1)S(1)} %all_to_all.10.refs_4_), channel_id=1, source_target_pairs={{0,1},{1,0},{2,3},{3,2},{4,5},{5,4},{6,7},{7,6},{8,9},{9,8},{10,11... | collective-permute-start | bytes 688136 | tf_op jit(solution)/shard_map/ppermute | solution.py:33
  28.4 1.5 %collective-permute-start.3 = (bf16[32,3712]{1,0:T(8,128)(2,1)S(1)}, bf16[32,3712]{1,0:T(8,128)(2,1)S(1)}, u32[]{:S(2)}, u32[]{:S(2)}) collective-permute-start(bf16[32,3712]{1,0:T(8,128)(2,1)S(1)} %bitcast.9), channel_id=1, source_target_pairs={{0,1},{1,0},{2,3},{3,2},{4,5},{5,4},{6,7},{7,6},{8,9},{9,8},{10,11... | collective-permute-start | bytes 712712 | tf_op jit(solution)/shard_map/ppermute | solution.py:33
  30.7 13.6 %all-to-all-start.1 = ((bf16[16,4,1920]{2,1,0:T(4,128)(2,1)}), bf16[16,4,1920]{2,1,0:T(4,128)(2,1)S(1)}, u32[]{:S(2)}, u32[]{:S(2)}) async-start(bf16[16,4,1920]{2,1,0:T(4,128)(2,1)} %shard_map.110), calls=%async_computation.1 | async-start | bytes 491520 | tf_op jit(solution)/shard_map/all_to_all | solution.py:408
  34.2 10.3 %collective-permute-start.4 = (bf16[64,1792]{1,0:T(8,128)(2,1)S(1)}, bf16[64,1792]{1,0:T(8,128)(2,1)S(1)}, u32[]{:S(2)}, u32[]{:S(2)}) collective-permute-start(bf16[64,1792]{1,0:T(8,128)(2,1)S(1)} %bitcast.10), channel_id=1, source_target_pairs={{0,2},{2,0},{1,3},{3,1},{4,6},{6,4},{5,7},{7,5},{8,10},{10,8},{9,1... | collective-permute-start | bytes 688136 | tf_op jit(solution)/shard_map/ppermute | solution.py:33

commit v10 on v9

--- a/solution.py
+++ b/solution.py
@@ -92,7 +92,7 @@
 
 
 def choose_kernel(los, pick_ref, own_ref, *refs):
-    others, sel_ref, res_ref = refs[: los - 1], refs[los - 1], refs[los]
+    others, sel_ref = refs[: los - 1], refs[los - 1]
     his, _, cols = own_ref.shape
     width = cols // SPLIT
     h, l = lax.axis_index("hi"), lax.axis_index("lo")
@@ -103,7 +103,6 @@
         for other in others:
             pair = pair + other[:, pl.ds(at, cols)].astype(F32)
         pair = pair.astype(BF)
-        res_ref[k - 1] = pair
         chosen = dot(pick_ref[0], pair[:, :width])
         for s in range(1, SPLIT):
             chosen = chosen + dot(pick_ref[s], pair[:, s * width : (s + 1) * width])
@@ -112,7 +111,7 @@
 
 def load_kernel(los, *refs):
     hbms, (hidden_ref, pick_ref, own_ref) = refs[:4], refs[4:7]
-    others, (mine_ref, sel_ref), sems = refs[7 : 6 + los], refs[10 + los : 12 + los], refs[-1]
+    others, (mine_ref, sel_ref, res_ref), sems = refs[7 : 6 + los], refs[10 + los : -1], refs[-1]
     copies = [
         pltpu.make_async_copy(
             hbm if i != 2 else hbm.at[:, pl.ds(hbm.shape[1] - vmem.shape[1], vmem.shape[1]), :],
@@ -131,6 +130,14 @@
     for other in others:
         mine = mine + other[:, pl.ds(at, cols)].astype(F32)
     mine_ref[...] = mine
+    his = own_ref.shape[0]
+    for k in range(1, his):
+        hh = lax.rem(h + k, his)
+        pair = own_ref[hh].astype(F32)
+        at = pl.multiple_of((hh * los + l) * cols, LANES)
+        for other in others:
+            pair = pair + other[:, pl.ds(at, cols)].astype(F32)
+        res_ref[k - 1] = pair.astype(BF)
     chosen = dot(pick_ref[0].astype(F32), mine[:, :width], HIGHEST)
     for s in range(1, SPLIT):
         chosen = chosen + dot(
@@ -332,17 +339,16 @@
         ],
         moved=MIB,
     )
-    sels, rests = call(
+    (sels,) = call(
         lambda *refs: choose_kernel(los, *refs),
         4,
         near(pick, own, *others),
         [
             pltpu.VMEM((his - 1, rows, width), BF),
-            pltpu.VMEM((his - 1, tokens, cols), BF),
         ],
     )
     sels = [shift(sels[k - 1], "hi", k) for k in range(1, his)]
-    gain, wg, wu_rest, wd, mine, sel = call(
+    gain, wg, wu_rest, wd, mine, sel, rests = call(
         lambda *refs: load_kernel(los, *refs),
         4,
         far(gain, w_gate, w_up, w_down) + near(hidden, pick, own, *others),
@@ -353,6 +359,7 @@
             pltpu.VMEM(w_down.shape, BF),
             pltpu.VMEM((tokens, cols), F32),
             pltpu.VMEM((rows, width), F32),
+            pltpu.VMEM((his - 1, tokens, cols), BF),
         ],
         [pltpu.SemaphoreType.DMA((4,))],
         moved=12 * MIB,

time: 45.7 us -> 45.7 us (level)
  transfers between devices with their start and end apart: 6 -> 6, of which waited for: 5 -> 5; matrix products, arithmetic and copies ran while one was open for 0% -> 0% of each run, Pallas kernels for 15% -> 16%
where the time goes in v10:
time: 45.7 us; the launch traced here: 45.4 us
  blocking collectives  15 us (33%)
  waiting for transfers between devices  10.4 us (23%)
  Pallas kernels  10.2 us (22%)
  starting transfers between devices  9.02 us (20%)
  between operations  0.68 us (1%)
    all_to_all x1, blocking collectives, on_device(): lax.all_to_all(outgoing.reshape(blocks, SUBLANES, width), ('dp', 'hi'), 0...  15 us
    pallas_call x9, Pallas kernels, call(): pl.pallas_call(kernel, out_shape=outs, in_specs=[HBM if at == 'hbm' else...  9.33 us
    all_to_all x1, waiting for transfers between devices, on_device(): back = lax.all_to_all(back, ('dp', 'hi'), 0, 0, tiled=True)  8.24 us
    ppermute x5, starting transfers between devices, shift(): return lax.ppermute(x, axis, [(i, (i + by) % n) for i in range(n)])  5.49 us
    all_to_all x1, starting transfers between devices, on_device(): back = lax.all_to_all(back, ('dp', 'hi'), 0, 0, tiled=True)  3.53 us
    ppermute x5, waiting for transfers between devices, shift(): return lax.ppermute(x, axis, [(i, (i + by) % n) for i in range(n)])  2.21 us
  transfers between devices with their start and end apart: 6, of which 5 were waited for; matrix products, arithmetic and copies ran while one was open for 0% of the time, Pallas kernels for 16%

profile of v10, /device:TPU:0, one launch (start us, length us, event | category | flops | bytes accessed | tf_op | source)
XLA Modules:
  0.0 45.4 jit_solution(1818258924256348104)
XLA Ops:
  0.6 0.6 %collective-permute-start = (bf16[64,7168]{1,0:T(8,128)(2,1)}, bf16[64,7168]{1,0:T(8,128)(2,1)S(1)}, u32[]{:S(2)}, u32[]{:S(2)}) collective-permute-start(bf16[64,7168]{1,0:T(8,128)(2,1)} %bitcast.12), channel_id=1, source_target_pairs={{0,1},{1,0},{2,3},{3,2},{4,5},{5,4},{6,7},{7,6},{8,9},{9,8},{10,11... | collective-permute-start | bytes 2752520 | tf_op jit(solution)/shard_map/ppermute | solution.py:33
  1.2 1.9 %shard_map.103 = (bf16[2,64,1792]{2,1,0:T(8,128)(2,1)S(1)}, bf16[64,1792]{1,0:T(8,128)(2,1)S(1)}, bf16[2,64,64]{2,1,0:T(8,128)(2,1)S(1)}, bf16[64,64]{1,0:T(8,128)(2,1)S(1)}, bf16[1,3584,256]{2,1,0:T(8,128)(2,1)S(1)}) custom-call(bf16[1,64,7168]{2,1,0:T(8,128)(2,1)} %refs_0_.1, bf16[64,1792]{1,0:T(8,128)(2,1)} %refs_1_.2, s32[8,64]{1,0:T(8,128)} %bitcast.14, ...), custom_call_target="tpu_custom_call" | custom-call | bytes 1048576 | tf_op jit(solution)/shard_map/pallas_call | solution.py:295
  3.1 0.4 collective-permute-done.refs_7_.refs_2_
  3.5 0.2 shard_map.105
  3.7 2.9 %collective-permute-start.1 = (bf16[64,896]{1,0:T(8,128)(2,1)S(1)}, bf16[64,896]{1,0:T(8,128)(2,1)S(1)}, u32[]{:S(2)}, u32[]{:S(2)}) collective-permute-start(bf16[64,896]{1,0:T(8,128)(2,1)S(1)} %bitcast.9), channel_id=1, source_target_pairs={{0,2},{2,0},{1,3},{3,1},{4,6},{6,4},{5,7},{7,5},{8,10},{10,8},{9,1... | collective-permute-start | bytes 344072 | tf_op jit(solution)/shard_map/ppermute | solution.py:33
  6.6 4.0 %shard_map.104 = (f32[1,7168]{1,0:T(1,128)S(1)}, bf16[1,7168,256]{2,1,0:T(8,128)(2,1)S(1)}, bf16[1,3584,256]{2,1,0:T(8,128)(2,1)S(1)}, bf16[1,256,7168]{2,1,0:T(...) custom-call(f32[1,7168]{1,0:T(1,128)} %bitcast.13, ...), custom_call_target="tpu_custom_call" | custom-call | bytes 12582912 | tf_op jit(solution)/shard_map/pallas_call | solution.py:295
  10.7 0.0 collective-permute-done.1.refs_1_
  10.7 15.0 %all_to_all.10.refs_4_ = bf16[16,8,896]{2,1,0:T(8,128)(2,1)S(1)} all-to-all(bf16[16,8,896]{2,1,0:T(8,128)(2,1)S(1)} %bitcast.8), channel_id=1, replica_groups=mesh['dp'=8,'hi'=2,'lo'=2] {'dp','hi'}, dimensions={0} | all-to-all | bytes 458752 | tf_op jit(solution)/shard_map/all_to_all | solution.py:373
  25.7 0.0 collective-permute-start.2
  25.7 0.8 %shard_map.107 = (f32[32,256]{1,0:T(8,128)S(1)}, f32[32,256]{1,0:T(8,128)S(1)}, f32[32,128]{1,0:T(8,128)S(1)}, f32[32,128]{1,0:T(8,128)S(1)}) custom-call(f32[1,7168]{1,0:T(1,128)S(1)} %get-tuple-element.28.refs_0_, bf16[1,7168,256]{2,1,0:T(8,128)(2,1)S(1)} %get-tuple-element.29.refs_1_, bf16[1,3584,256]{2,1,0:T(8,128)(2,1)S(1)} %get-tuple-element.30.refs_2_, ...), custom_call_target="tpu_custom_call" | custom-call | bytes 4194304 | tf_op jit(solution)/shard_map/pallas_call | solution.py:295
  26.5 0.7 %collective-permute-done.2.refs_9_ = bf16[16,8,896]{2,1,0:T(8,128)(2,1)S(1)} collective-permute-done((bf16[16,8,896]{2,1,0:T(8,128)(2,1)S(1)}, bf16[16,8,896]{2,1,0:T(8,128)(2,1)S(1)}, u32[]{:S(2)}, u32[]{:S(2)}) %collective-permute-start.2) | collective-permute-done | bytes 229408 | tf_op jit(solution)/shard_map/ppermute | solution.py:33
  27.2 1.2 %shard_map.108 = (bf16[1,32,3712]{2,1,0:T(8,128)(2,1)S(1)}, bf16[32,256]{1,0:T(8,128)(2,1)S(1)}, f32[8,128]{1,0:T(8,128)S(1)}, f32[8,128]{1,0:T(8,128)S(1)}) custom-call(f32[1,7168]{1,0:T(1,128)S(1)} %get-tuple-element.28.refs_0_, bf16[1,7168,256]{2,1,0:T(8,128)(2,1)S(1)} %get-tuple-element.29.refs_1_, bf16[1,3584,256]{2,1,0:T(8,128)(2,1)S(1)} %get-tuple-element.30.refs_2_, ...), custom_call_target="tpu_custom_call" | custom-call | tf_op jit(solution)/shard_map/pallas_call | solution.py:295
  28.4 0.2 collective-permute-start.3
  28.6 0.4 shard_map.109.refs_0_
  29.0 0.9 %collective-permute-done.3.refs_2_ = bf16[32,3712]{1,0:T(8,128)(2,1)S(1)} collective-permute-done((bf16[32,3712]{1,0:T(8,128)(2,1)S(1)}, bf16[32,3712]{1,0:T(8,128)(2,1)S(1)}, u32[]{:S(2)}, u32[]{:S(2)}) %collective-permute-start.3) | collective-permute-done | bytes 237600 | tf_op jit(solution)/shard_map/ppermute | solution.py:33
  29.9 0.8 %shard_map.110 = bf16[16,4,1920]{2,1,0:T(4,128)(2,1)} custom-call(f32[32,3584]{1,0:T(8,128)S(1)} %shard_map.109.refs_0_, f32[8,128]{1,0:T(8,128)S(1)} %get-tuple-element.39.refs_1_, bf16[32,3712]{1,0:T(8,128)(2,1)S(1)} %collective-permute-done.3.refs_2_), custom_call_target="tpu_custom_call" | custom-call | tf_op jit(solution)/shard_map/pallas_call | solution.py:295
  30.7 3.5 %all-to-all-start.1 = ((bf16[16,4,1920]{2,1,0:T(4,128)(2,1)}), bf16[16,4,1920]{2,1,0:T(4,128)(2,1)S(1)}, u32[]{:S(2)}, u32[]{:S(2)}) async-start(bf16[16,4,1920]{2,1,0:T(4,128)(2,1)} %shard_map.110), calls=%async_computation.1 | async-start | bytes 491520 | tf_op jit(solution)/shard_map/all_to_all | solution.py:415
  34.2 1.8 %collective-permute-start.4 = (bf16[64,1792]{1,0:T(8,128)(2,1)S(1)}, bf16[64,1792]{1,0:T(8,128)(2,1)S(1)}, u32[]{:S(2)}, u32[]{:S(2)}) collective-permute-start(bf16[64,1792]{1,0:T(8,128)(2,1)S(1)} %bitcast.11), channel_id=1, source_target_pairs={{0,2},{2,0},{1,3},{3,1},{4,6},{6,4},{5,7},{7,5},{8,10},{10,8},{9,1... | collective-permute-start | bytes 688136 | tf_op jit(solution)/shard_map/ppermute | solution.py:33
  36.1 8.2 %all-to-all-done.1.refs_0_.refs_2_ = bf16[16,4,1920]{2,1,0:T(4,128)(2,1)S(1)} async-done(((bf16[16,4,1920]{2,1,0:T(4,128)(2,1)}), bf16[16,4,1920]{2,1,0:T(4,128)(2,1)S(1)}, u32[]{:S(2)}, u32[]{:S(2)}) %all-to-all-start.1) | async-done | bytes 245792 | tf_op jit(solution)/shard_map/all_to_all | solution.py:415
  44.3 0.2 collective-permute-done.4.refs_5_
  44.5 0.9 %combine.1 = (bf16[64,1792]{1,0:T(8,128)(2,1)}, f32[1]{0:T(128)}, f32[1]{0:T(128)}) custom-call(f32[64,1792]{1,0:T(8,128)S(1)} %get-tuple-element.26.refs_0_, bf16[64,64]{1,0:T(8,128)(2,1)S(1)} %get-tuple-element.27.refs_1_, bf16[16,4,1920]{2,1,0:T(4,128)(2,1)S(1)} %all-to-all-done.1.refs_0_.refs_2_, f32[8,128]{1,0:T(8,128)S(1)} %get-tuple-element.41.refs_3_, ...), custom_call_target="tpu_custom_call" | custom-call | tf_op jit(solution)/shard_map/combine/pallas_call | solution.py:422
  (2 shorter events, 0.0 us)
Async XLA Ops:
  0.6 2.9 %collective-permute-start = (bf16[64,7168]{1,0:T(8,128)(2,1)}, bf16[64,7168]{1,0:T(8,128)(2,1)S(1)}, u32[]{:S(2)}, u32[]{:S(2)}) collective-permute-start(bf16[64,7168]{1,0:T(8,128)(2,1)} %bitcast.12), channel_id=1, source_target_pairs={{0,1},{1,0},{2,3},{3,2},{4,5},{5,4},{6,7},{7,6},{8,9},{9,8},{10,11... | collective-permute-start | bytes 2752520 | tf_op jit(solution)/shard_map/ppermute | solution.py:33
  3.7 7.0 %collective-permute-start.1 = (bf16[64,896]{1,0:T(8,128)(2,1)S(1)}, bf16[64,896]{1,0:T(8,128)(2,1)S(1)}, u32[]{:S(2)}, u32[]{:S(2)}) collective-permute-start(bf16[64,896]{1,0:T(8,128)(2,1)S(1)} %bitcast.9), channel_id=1, source_target_pairs={{0,2},{2,0},{1,3},{3,1},{4,6},{6,4},{5,7},{7,5},{8,10},{10,8},{9,1... | collective-permute-start | bytes 344072 | tf_op jit(solution)/shard_map/ppermute | solution.py:33
  25.7 1.5 %collective-permute-start.2 = (bf16[16,8,896]{2,1,0:T(8,128)(2,1)S(1)}, bf16[16,8,896]{2,1,0:T(8,128)(2,1)S(1)}, u32[]{:S(2)}, u32[]{:S(2)}) collective-permute-start(bf16[16,8,896]{2,1,0:T(8,128)(2,1)S(1)} %all_to_all.10.refs_4_), channel_id=1, source_target_pairs={{0,1},{1,0},{2,3},{3,2},{4,5},{5,4},{6,7},{7,6},{8,9},{9,8},{10,11... | collective-permute-start | bytes 688136 | tf_op jit(solution)/shard_map/ppermute | solution.py:33
  28.4 1.5 %collective-permute-start.3 = (bf16[32,3712]{1,0:T(8,128)(2,1)S(1)}, bf16[32,3712]{1,0:T(8,128)(2,1)S(1)}, u32[]{:S(2)}, u32[]{:S(2)}) collective-permute-start(bf16[32,3712]{1,0:T(8,128)(2,1)S(1)} %bitcast.10), channel_id=1, source_target_pairs={{0,1},{1,0},{2,3},{3,2},{4,5},{5,4},{6,7},{7,6},{8,9},{9,8},{10,11... | collective-permute-start | bytes 712712 | tf_op jit(solution)/shard_map/ppermute | solution.py:33
  30.7 13.6 %all-to-all-start.1 = ((bf16[16,4,1920]{2,1,0:T(4,128)(2,1)}), bf16[16,4,1920]{2,1,0:T(4,128)(2,1)S(1)}, u32[]{:S(2)}, u32[]{:S(2)}) async-start(bf16[16,4,1920]{2,1,0:T(4,128)(2,1)} %shard_map.110), calls=%async_computation.1 | async-start | bytes 491520 | tf_op jit(solution)/shard_map/all_to_all | solution.py:415
  34.2 10.3 %collective-permute-start.4 = (bf16[64,1792]{1,0:T(8,128)(2,1)S(1)}, bf16[64,1792]{1,0:T(8,128)(2,1)S(1)}, u32[]{:S(2)}, u32[]{:S(2)}) collective-permute-start(bf16[64,1792]{1,0:T(8,128)(2,1)S(1)} %bitcast.11), channel_id=1, source_target_pairs={{0,2},{2,0},{1,3},{3,1},{4,6},{6,4},{5,7},{7,5},{8,10},{10,8},{9,1... | collective-permute-start | bytes 688136 | tf_op jit(solution)/shard_map/ppermute | solution.py:33
